TPU v7x, 256 devices: a whole 4x4x8 slice. The times are simulated.
256 devices in a mesh: row: 16 (over z_lo, x, core), col: 16 (over z_hi, y).
Axes of the slice: x: 4, y: 4, z: 8 (z_hi: 4, z_lo: 2; z = z_hi * 2 + z_lo), core: 2. Of those that a mesh axis runs over, the one named last changes fastest.
Arguments:
- embeddings: bfloat16 [32768, 768], P(('row', 'col')), may hold values from -400 to 400
- tile_list: int32 [16, 16, 32, 2], P('row', 'col'), may hold values from -1 to 15, as said below
- seeds: int32 [32768], P(('row', 'col')), may hold values from 0 to 127
Outputs:
- scores: float32 [32768, 64], P(('row', 'col'))
Inputs may be any that keep to these rules, and one draw needn't show every extreme that they name: tile_list[r, c] lists the tiles of the device at row index r and column index c: a live slot (a, b) stands for the tile of document block r * 16 + a against block b * 16 + c, with a < 16, b < 16 and r * 16 + a <= b * 16 + c. Live slots come first and are distinct, empty slots hold -1 in both entries, the tile (c, r) of a block against itself is always listed, and some device fills all 32 slots. `seeds`: values of 64 or more mark a document without a seed label.
All inputs are finite; a program needn't handle non-finite values.
Results may differ from a plain program's by a relative error of at most 0.00056.
Values may be sent and summed in bfloat16 or wider, within the bound.
No kernel may reach another device: no remote copies, remote signals or barrier semaphores. Data moves between devices by JAX's collectives and lax.ppermute only.
A program may use at most 64 MiB of HBM per device.

v0:
```python
import jax
import jax.numpy as jnp
from jax import lax
from jax.sharding import PartitionSpec as P

CLASSES = 64
ITERS = 3


BLEND = 0.8
EPSILON = 1e-06


def slot_table(picks, slot_alive, extent):
    hits = picks[None, :] == jnp.arange(extent, dtype=jnp.int32)[:, None]
    return (hits & slot_alive[None, :]).astype(jnp.float32)


def settle(to_rows, to_cols, col_index):
    col_share = lax.psum_scatter(to_cols, "row", scatter_dimension=0, tiled=True)
    own_block = lax.dynamic_slice_in_dim(to_rows, col_index, 1, 0) + col_share
    placed = lax.dynamic_update_slice_in_dim(to_rows, own_block, col_index, 0)
    return lax.psum(placed, "col")


def local(embeddings, tile_list, seeds):
    row_index = lax.axis_index("row")
    col_index = lax.axis_index("col")
    row_devices = lax.axis_size("row")
    col_devices = lax.axis_size("col")
    row_count, feat_width = embeddings.shape
    sharpness = feat_width**0.5
    highest = lax.Precision.HIGHEST
    features = embeddings.astype(jnp.float32)
    normed = (
        features * lax.rsqrt(jnp.sum(features * features, axis=1, keepdims=True) + EPSILON)
    ).astype(jnp.bfloat16)
    normed_rows = lax.all_gather(normed, "col", axis=0, tiled=True).reshape(
        col_devices, row_count, feat_width
    )
    normed_cols = lax.all_gather(normed, "row", axis=0, tiled=True).reshape(
        row_devices, row_count, feat_width
    )
    slot_pairs = tile_list.reshape(-1, 2)
    slot_total = slot_pairs.shape[0]
    slot_alive = slot_pairs[:, 0] >= 0
    row_pick = jnp.maximum(slot_pairs[:, 0], 0)
    col_pick = jnp.maximum(slot_pairs[:, 1], 0)
    slot_count = jnp.sum(slot_alive.astype(jnp.int32))
    diagonal = jnp.eye(row_count, dtype=bool)

    def build_group(group_index, kernels):
        offset = group_index * 8
        rows_now = lax.dynamic_slice_in_dim(row_pick, offset, 8)
        cols_now = lax.dynamic_slice_in_dim(col_pick, offset, 8)
        alive_now = lax.dynamic_slice_in_dim(slot_alive, offset, 8)
        scores = jnp.einsum(
            "sie,sje->sij",
            normed_rows[rows_now],
            normed_cols[cols_now],
            preferred_element_type=jnp.float32,
        )
        kernel = jnp.exp(sharpness * (scores - 1.0))
        self_pair = (rows_now == col_index) & (cols_now == row_index)
        masked = self_pair[:, None, None] & diagonal[None] | ~alive_now[:, None, None]
        kernel = jnp.where(masked, 0.0, kernel)
        return lax.dynamic_update_slice_in_dim(kernels, kernel, offset, 0)

    kernels = lax.fori_loop(
        0,
        (slot_count + 7) // 8,
        build_group,
        jnp.zeros((slot_total, row_count, row_count), jnp.float32),
    )
    row_table = slot_table(row_pick, slot_alive, col_devices)
    col_table = slot_table(col_pick, slot_alive, row_devices)
    degree = settle(
        jnp.dot(row_table, jnp.sum(kernels, axis=2), precision=highest),
        jnp.dot(col_table, jnp.sum(kernels, axis=1), precision=highest),
        col_index,
    )
    weight = lax.rsqrt(degree)[:, :, None]
    seeded = (seeds[:, None] == jnp.arange(CLASSES, dtype=jnp.int32)[None, :]).astype(jnp.float32)
    seeded = lax.all_gather(seeded, "col", axis=0, tiled=True).reshape(
        col_devices, row_count, CLASSES
    )
    labels = seeded
    for sweep in range(ITERS):
        spread = weight * labels
        own_spread = lax.dynamic_index_in_dim(spread, col_index, 0, keepdims=False)
        col_labels = lax.all_gather(own_spread, "row", axis=0, tiled=True).reshape(
            row_devices, row_count, CLASSES
        )
        to_rows = jnp.einsum("sij,sjc->sic", kernels, col_labels[col_pick], precision=highest)
        to_cols = jnp.einsum("sij,sic->sjc", kernels, spread[row_pick], precision=highest)
        summed = settle(
            jnp.einsum("as,sic->aic", row_table, to_rows, precision=highest),
            jnp.einsum("bs,sjc->bjc", col_table, to_cols, precision=highest),
            col_index,
        )
        labels = BLEND * weight * summed + (1.0 - BLEND) * seeded
    labels = lax.dynamic_index_in_dim(labels, col_index, 0, keepdims=False)
    return CLASSES * labels


def solution(mesh):
    return jax.shard_map(
        local,
        mesh=mesh,
        in_specs=(P(("row", "col"), None), P("row", "col", None, None), P(("row", "col"))),
        out_specs=P(("row", "col"), None),
        check_vma=False,
    )
```

profile of v0, /device:TPU:32, one launch (start us, length us, event | category | flops | bytes accessed | tf_op | source)
XLA Modules:
  0.0 956.2 jit_solution(11870929973664269903)
XLA Ops:
  6.5 1.1 fusion.18
  7.6 1.7 fusion.19
  10.2 1.3 convert_reduce_fusion
  12.8 55.4 %all_gather.20 = f32[2048,64]{0,1:T(8,128)S(1)} all-gather(f32[128,64]{0,1:T(8,128)S(1)} %fusion.21), channel_id=1, replica_groups=mesh['row'=16,'col'=16] {'col'}, dimensions={0}, use_global_device_ids=true | all-gather | bytes 557056 | tf_op jit(solution)/shard_map/all_gather | solution.py:84
  69.1 10.2 %all-gather.6.cloned.1.call-done = bf16[2048,768]{1,0:T(8,128)(2,1)} async-done(((bf16[128,768]{1,0:T(8,128)(2,1)}), bf16[2048,768]{1,0:T(8,128)(2,1)}) %all-gather.6.cloned.1.call-update) | async-done | bytes 3145744 | tf_op jit(solution)/shard_map/all_gather | solution.py:38
  79.3 40.6 %all-gather.8.cloned.1.call-done = bf16[2048,768]{1,0:T(8,128)(2,1)} async-done(((bf16[128,768]{1,0:T(8,128)(2,1)}), bf16[2048,768]{1,0:T(8,128)(2,1)}) %all-gather.8.cloned.1.call-update) | async-done | bytes 3145744 | tf_op jit(solution)/shard_map/all_gather | solution.py:41
  120.1 40.6 %while.13 = (s32[]{:T(128)}, f32[32,128,128]{2,1,0:T(8,128)S(1)}, s32[]{:T(128)}, s32[32]{0:T(128)S(1)}, s32[]{:T(128)}, /*index=5*/s32[32]{0:T(128)S(1)}, s32[]...) while((s32[]{:T(128)}, f32[32,128,128]{2,1,0:T(8,128)S(1)}, ...), condition=%wide.region_3.4_spmd.clone, body=%wide.region_2.3_spmd.clone.sunk | while | flops 202000464 | bytes 10003999 | solution.py:69
  120.3 3.7 gather_fusion
  124.0 3.8 gather_fusion.1
  127.8 2.5 fusion.81
  130.5 3.7 gather_fusion
  134.2 3.8 gather_fusion.1
  137.9 2.5 fusion.81
  140.6 3.7 gather_fusion
  144.3 3.8 gather_fusion.1
  148.1 2.5 fusion.81
  150.8 3.7 gather_fusion
  154.4 3.8 gather_fusion.1
  158.2 2.5 fusion.81
  161.5 29.4 %all-reduce = f32[16,128]{1,0:T(8,128)S(1)} all-reduce(f32[16,128]{1,0:T(8,128)S(1)} %fusion.28), channel_id=5, replica_groups=mesh['row'=16,'col'=16] {'row'}, use_global_device_ids=true, to_apply=%region_6.7.clone | all-reduce | flops 2048 | bytes 16384
  191.7 45.0 %psum.28 = f32[16,128]{1,0:T(8,128)S(1)} all-reduce(f32[16,128]{1,0:T(8,128)S(1)} %dynamic_update_slice.18), channel_id=1, replica_groups=mesh['row'=16,'col'=16] {'col'}, use_global_device_ids=true, to_apply=%region_7.8 | all-reduce | flops 2048 | bytes 16384 | tf_op jit(solution)/shard_map/psum | solution.py:23
  237.8 1.6 gather_fusion.3
  239.4 3.2 fusion.55
  242.5 1.1 fusion.14
  245.6 17.6 %all-gather = f32[1,2048,64]{1,0,2:T(1,128)S(1)} all-gather(f32[1,128,64]{1,0,2:T(1,128)S(1)} %constant_dynamic-slice_fusion.3), channel_id=2, replica_groups=mesh['row'=16,'col'=16] {'row'}, dimensions={1}, use_global_device_ids=true | all-gather | bytes 557056 | tf_op jit(solution)/shard_map/all_gather | solution.py:91
  263.4 1.6 gather_fusion.2
  265.0 5.4 fusion.54
  271.4 30.1 %reduce-scatter.4.cloned.1.call-done = f32[1,128,64]{1,2,0:T(8,128)} async-done(((f32[16,128,64]{1,2,0:T(8,128)}), f32[1,128,64]{1,2,0:T(8,128)}) %reduce-scatter.4.cloned.1.call-update) | async-done | bytes 32784 | tf_op jit(solution)/shard_map/reduce_scatter | solution.py:20
  303.5 165.3 %all-reduce.5.cloned.1.call-done = f32[16,128,64]{1,0,2:T(8,128)} async-done(((f32[16,128,64]{1,0,2:T(8,128)}), f32[16,128,64]{1,0,2:T(8,128)}) %all-reduce.5.cloned.1.call-update) | async-done | bytes 524304 | tf_op jit(solution)/shard_map/psum | solution.py:23
  468.8 1.1 add_multiply_fusion.1
  470.9 1.6 gather_fusion.5
  472.5 3.2 fusion.57
  475.7 1.1 fusion.10
  478.8 20.9 %all-gather.1 = f32[1,2048,64]{1,0,2:T(1,128)S(1)} all-gather(f32[1,128,64]{1,0,2:T(1,128)S(1)} %constant_dynamic-slice_fusion.2), channel_id=3, replica_groups=mesh['row'=16,'col'=16] {'row'}, dimensions={1}, use_global_device_ids=true | all-gather | bytes 557056 | tf_op jit(solution)/shard_map/all_gather | solution.py:91
  499.8 1.6 gather_fusion.4
  501.4 5.4 fusion.56
  507.9 32.4 %reduce-scatter.6.cloned.1.call-done = f32[1,128,64]{1,2,0:T(8,128)} async-done(((f32[16,128,64]{1,2,0:T(8,128)}), f32[1,128,64]{1,2,0:T(8,128)}) %reduce-scatter.6.cloned.1.call-update) | async-done | bytes 32784 | tf_op jit(solution)/shard_map/reduce_scatter | solution.py:20
  542.1 165.7 %all-reduce.7.cloned.1.call-done = f32[16,128,64]{1,0,2:T(8,128)} async-done(((f32[16,128,64]{1,0,2:T(8,128)}), f32[16,128,64]{1,0,2:T(8,128)}) %all-reduce.7.cloned.1.call-update) | async-done | bytes 524304 | tf_op jit(solution)/shard_map/psum | solution.py:23
  707.8 1.9 add_multiply_fusion
  710.7 1.6 gather_fusion.7
  712.3 3.2 fusion.59
  718.6 21.1 %all-gather.2 = f32[1,2048,64]{1,0,2:T(1,128)S(1)} all-gather(f32[1,128,64]{1,0,2:T(1,128)S(1)} %constant_dynamic-slice_fusion.1), channel_id=4, replica_groups=mesh['row'=16,'col'=16] {'row'}, dimensions={1}, use_global_device_ids=true | all-gather | bytes 557056 | tf_op jit(solution)/shard_map/all_gather | solution.py:91
  739.8 1.6 gather_fusion.6
  741.4 5.4 fusion.58
  746.8 1.1 fusion.8
  747.9 32.3 %reduce-scatter.8.cloned.1.call-done = f32[1,128,64]{1,2,0:T(8,128)} async-done(((f32[16,128,64]{1,2,0:T(8,128)}), f32[1,128,64]{1,2,0:T(8,128)}) %reduce-scatter.8.cloned.1.call-update) | async-done | bytes 32784 | tf_op jit(solution)/shard_map/reduce_scatter | solution.py:20
  781.9 165.8 %all-reduce.9.cloned.1.call-done = f32[16,128,64]{1,0,2:T(8,128)} async-done(((f32[16,128,64]{1,0,2:T(8,128)}), f32[16,128,64]{1,0,2:T(8,128)}) %all-reduce.9.cloned.1.call-update) | async-done | bytes 524304 | tf_op jit(solution)/shard_map/psum | solution.py:23
  947.7 1.7 fusion.20
  (90 shorter events, 23.0 us)
Async XLA Ops:
  6.5 61.9 %copy-start.7 = (u32[256]{0:T(256)S(1)}, u32[256]{0:T(256)}, u32[]{:S(2)}) copy-start(u32[256]{0:T(256)} %constant.99) | copy-start | bytes 3076
  6.5 62.5 %copy-start.6 = (s32[1,1,32,2]{2,3,1,0:T(2,128)S(1)}, s32[1,1,32,2]{2,3,1,0:T(2,128)}, u32[]{:S(2)}) copy-start(s32[1,1,32,2]{2,3,1,0:T(2,128)} %param.6) | copy-start | bytes 772
  6.5 72.7 %all-gather.6.cloned.1.call-start = ((), (), s32[]{:S(2)}) async-start(), calls=%async_computation.3 | async-start | bytes 3342336 | tf_op jit(solution)/shard_map/all_gather | solution.py:38
  9.4 110.5 %all-gather.8.cloned.1.call-start = ((), (), s32[]{:S(2)}) async-start(), calls=%async_computation.4 | async-start | bytes 3342336 | tf_op jit(solution)/shard_map/all_gather | solution.py:41
  10.1 291.4 %reduce-scatter.4.cloned.1.call-start = ((), (), s32[]{:S(2)}) async-start(), calls=%async_computation.5 | async-start | bytes 557056 | tf_op jit(solution)/shard_map/reduce_scatter | solution.py:20
  236.8 0.8 copy-start.1
  244.6 224.2 %all-reduce.5.cloned.1.call-start = ((), (), s32[]{:S(2)}) async-start(), calls=%async_computation.6 | async-start | bytes 1048576 | tf_op jit(solution)/shard_map/psum | solution.py:23
  302.4 0.8 copy-start.4
  303.2 237.1 %reduce-scatter.6.cloned.1.call-start = ((), (), s32[]{:S(2)}) async-start(), calls=%async_computation.7 | async-start | bytes 557056 | tf_op jit(solution)/shard_map/reduce_scatter | solution.py:20
  469.9 0.8 copy-start
  477.7 230.1 %all-reduce.7.cloned.1.call-start = ((), (), s32[]{:S(2)}) async-start(), calls=%async_computation.8 | async-start | bytes 1048576 | tf_op jit(solution)/shard_map/psum | solution.py:23
  541.3 0.8 copy-start.5
  542.1 238.0 %reduce-scatter.8.cloned.1.call-start = ((), (), s32[]{:S(2)}) async-start(), calls=%async_computation.9 | async-start | bytes 557056 | tf_op jit(solution)/shard_map/reduce_scatter | solution.py:20
  709.8 0.8 copy-start.2
  717.5 230.2 %all-reduce.9.cloned.1.call-start = ((), (), s32[]{:S(2)}) async-start(), calls=%async_computation.10 | async-start | bytes 1048576 | tf_op jit(solution)/shard_map/psum | solution.py:23
  781.1 0.8 copy-start.3
Sparse Core Ops, SparseCore 0:
  9.8 69.4 all-gather.5
  81.1 38.7 all-gather.7
  244.7 56.7 reduce-scatter.3
  303.9 164.8 all-reduce.4
  477.8 62.4 reduce-scatter.5
  542.8 164.9 all-reduce.6
  717.6 62.4 reduce-scatter.7
  782.7 164.9 all-reduce.8
where the time goes:
time: 959 us; the launch traced here: 956 us
  waiting for transfers between devices  643 us (67%)
  blocking collectives  189 us (20%)
  local copies, waits for them, and re-layouts  52.3 us (5%)
  matrix products  42.2 us (4%)
  between operations  14.5 us (2%)
  other arithmetic  14.1 us (1%)
    psum x3, waiting for transfers between devices, settle(): return lax.psum(placed, 'col')  497 us
    reduce_scatter x3, waiting for transfers between devices, settle(): lax.psum_scatter(to_cols, 'row', scatter_dimension=0, tiled=True)  94.7 us
    all_gather x3, blocking collectives, local(): lax.all_gather(own_spread, 'row', axis=0, tiled=True)  59.6 us
    all_gather x1, blocking collectives, local(): lax.all_gather(seeded, 'col', axis=0, tiled=True)  55.4 us
    psum x1, blocking collectives, settle(): return lax.psum(placed, 'col')  45 us
    all_gather x1, waiting for transfers between devices, local(): lax.all_gather(normed, 'row', axis=0, tiled=True)  40.6 us
    unnamed x1, blocking collectives  29.4 us
  transfers between devices with their start and end apart: 8, of which 8 were waited for; matrix products, arithmetic and copies ran while one was open for 3% of the time, Pallas kernels for 0%

commit v1 on v0

v1 whole, which is shorter than its diff:
```python
import jax
import jax.numpy as jnp
import numpy as np
from jax import lax
from jax.experimental import pallas as pl
from jax.experimental.pallas import tpu as pltpu
from jax.sharding import Mesh
from jax.sharding import PartitionSpec as P

CLASSES = 64
BLEND = 0.8
EPSILON = 1e-06
AXES = ("zlo", "x", "core", "zhi", "y")
SIZES = (2, 4, 2, 4, 4)
ROW = ("zlo", "x", "core")
COL = ("zhi", "y")
GROUP = 16
BLOCKS = GROUP * GROUP
ROWS = 128
FEAT = 768
EXTRA = 8
CHUNK = 8
DEPTH = 4
VMEM = pl.BlockSpec(memory_space=pltpu.VMEM)
SMEM = pl.BlockSpec(memory_space=pltpu.SMEM)
ANY = pl.BlockSpec(memory_space=pl.ANY)


def prep_kernel(emb_ref, ids_ref, seeds_ref, out_ref):
    features = emb_ref[...].astype(jnp.float32)
    norm = lax.rsqrt(jnp.sum(features * features, axis=1, keepdims=True) + EPSILON)
    out_ref[:ROWS, :] = (features * norm).astype(jnp.bfloat16)
    lane = lax.broadcasted_iota(jnp.int32, (32, BLOCKS), 1)
    bits = jnp.sum((ids_ref[...] == lane).astype(jnp.float32), axis=0, keepdims=True)
    row = jnp.concatenate(
        [bits, seeds_ref[...].astype(jnp.float32), jnp.zeros((1, FEAT - BLOCKS - ROWS), jnp.float32)],
        axis=1,
    )
    out_ref[ROWS:, :] = jnp.broadcast_to(row, (EXTRA, FEAT)).astype(jnp.bfloat16)


def build_kernel(place_ref, count_ref, own_ref, other_ref, rows_ref,
                 tiles_ref, list_ref, deg_ref, cols_v, rows_v, stage, sums, in_sem, out_sem):
    core, diag_slot = place_ref[0], place_ref[1]
    copies = []
    for k in range(GROUP // 2):
        copies.append((own_ref.at[k, pl.ds(0, ROWS)], cols_v.at[2 * k + core]))
        copies.append((other_ref.at[k, pl.ds(0, ROWS)], cols_v.at[2 * k + 1 - core]))
    for k in range(GROUP):
        copies.append((rows_ref.at[k % 4, k // 4, pl.ds(0, ROWS)], rows_v.at[k]))
    copies = [pltpu.make_async_copy(src, dst, in_sem) for src, dst in copies]
    for copy in copies:
        copy.start()

    def add_slot(slot, found):
        live = count_ref[slot] > 0
        list_ref[found] = slot
        return found + live.astype(jnp.int32)

    found = lax.fori_loop(0, BLOCKS, add_slot, jnp.int32(0), unroll=8)
    chunks = (found + CHUNK - 1) // CHUNK

    def pad_slot(at, carry):
        list_ref[at] = -1
        return carry

    lax.fori_loop(found, chunks * CHUNK, pad_slot, 0)
    list_ref[BLOCKS] = chunks
    sums[...] = jnp.zeros_like(sums)
    sharpness = FEAT**0.5
    on_diag = (
        lax.broadcasted_iota(jnp.int32, (ROWS, ROWS), 0)
        == lax.broadcasted_iota(jnp.int32, (ROWS, ROWS), 1)
    ).astype(jnp.float32)
    for copy in copies:
        copy.wait()

    def out_copy(group):
        half = lax.rem(group, 2)
        return pltpu.make_async_copy(
            stage.at[half], tiles_ref.at[pl.ds(group * CHUNK, CHUNK)], out_sem.at[half]
        )

    def build_chunk(group, carry):
        half = lax.rem(group, 2)

        @pl.when(group >= 2)
        def _():
            out_copy(group - 2).wait()

        for k in range(CHUNK):
            listed = list_ref[group * CHUNK + k]
            slot = jnp.maximum(listed, 0)
            a, b = slot // GROUP, lax.rem(slot, GROUP)
            weight = jnp.where(listed >= 0, count_ref[slot], 0).astype(jnp.float32)
            off = jnp.where(listed == diag_slot, weight, 0.0)
            scores = lax.dot_general(
                cols_v[b], rows_v[a], (((1,), (1,)), ((), ())), preferred_element_type=jnp.float32
            )
            tile = jnp.exp(sharpness * (scores - 1.0)) * (weight - on_diag * off)
            high = tile.astype(jnp.bfloat16)
            stage[half, k, :ROWS, :] = high
            stage[half, k, ROWS:, :] = (tile - high.astype(jnp.float32)).astype(jnp.bfloat16)
            sums[b] += tile
        out_copy(group).start()
        return carry

    lax.fori_loop(0, chunks, build_chunk, 0)
    for back in (2, 1):
        @pl.when(chunks >= back)
        def _():
            out_copy(chunks - back).wait()
    for b in range(GROUP):
        deg_ref[pl.ds(b, 1), :] = jnp.sum(sums[b].T, axis=0, keepdims=True)


def apply_body(list_ref, tiles_ref, out_ref, wide, buf, sem):
    chunks = list_ref[BLOCKS]

    def fetch(group):
        at = lax.rem(group, DEPTH)
        return pltpu.make_async_copy(
            tiles_ref.at[pl.ds(group * CHUNK, CHUNK)], buf.at[at], sem.at[at]
        )

    def start(group):
        @pl.when(group < chunks)
        def _():
            fetch(group).start()

    return chunks, fetch, start


def split_into(wide, b, spread):
    high = spread.astype(jnp.bfloat16)
    low = (spread - high.astype(jnp.float32)).astype(jnp.bfloat16)
    wide[b, :CLASSES, :ROWS] = high
    wide[b, :CLASSES, ROWS:] = high
    wide[b, CLASSES:, :ROWS] = low
    wide[b, CLASSES:, ROWS:] = jnp.zeros_like(low)


def run_apply(list_ref, tiles_ref, out_ref, wide, buf, sem, fill):
    chunks, fetch, start = apply_body(list_ref, tiles_ref, out_ref, wide, buf, sem)
    for group in range(DEPTH - 1):
        start(group)
    fill()
    out_ref[...] = jnp.zeros_like(out_ref)

    def chunk_step(group, carry):
        fetch(group).wait()
        start(group + DEPTH - 1)
        at = lax.rem(group, DEPTH)
        for k in range(CHUNK):
            slot = jnp.maximum(list_ref[group * CHUNK + k], 0)
            a, b = slot // GROUP, lax.rem(slot, GROUP)
            both = jnp.dot(wide[b], buf[at, k], preferred_element_type=jnp.float32)
            out_ref[a] += both[:CLASSES] + both[CLASSES:]
        return carry

    lax.fori_loop(0, chunks, chunk_step, 0)


def first_kernel(list_ref, tiles_ref, seeds_ref, scale_ref, out_ref, wide, buf, sem):
    def fill():
        classes = lax.broadcasted_iota(jnp.int32, (CLASSES, ROWS), 0)
        for b in range(GROUP):
            seeded = classes == seeds_ref[pl.ds(b, 1), :]
            split_into(wide, b, jnp.where(seeded, scale_ref[pl.ds(b, 1), :], 0.0))

    run_apply(list_ref, tiles_ref, out_ref, wide, buf, sem, fill)


def next_kernel(list_ref, tiles_ref, spread_ref, out_ref, wide, buf, sem):
    def fill():
        for b in range(GROUP):
            split_into(wide, b, spread_ref[b])

    run_apply(list_ref, tiles_ref, out_ref, wide, buf, sem, fill)


APPLY = dict(
    out_shape=jax.ShapeDtypeStruct((GROUP, CLASSES, ROWS), jnp.float32),
    out_specs=VMEM,
    scratch_shapes=[
        pltpu.VMEM((GROUP, 2 * CLASSES, 2 * ROWS), jnp.bfloat16),
        pltpu.VMEM((DEPTH, CHUNK, 2 * ROWS, ROWS), jnp.bfloat16),
        pltpu.SemaphoreType.DMA((DEPTH,)),
    ],
    compiler_params=pltpu.CompilerParams(vmem_limit_bytes=48 << 20),
)


def exchange(blocks, axes):
    return lax.all_to_all(blocks, axes, 0, 0)


def gather(block, axes, count):
    return exchange(jnp.broadcast_to(block[None], (count,) + block.shape), axes)


def local(embeddings, tile_list, seeds):
    row_index = lax.axis_index(ROW)
    col_index = lax.axis_index(COL)
    core = lax.axis_index("core")
    slots = tile_list.reshape(-1, 2)
    ids = jnp.where(slots[:, :1] >= 0, slots[:, :1] * GROUP + slots[:, 1:], -1)
    block = pl.pallas_call(
        prep_kernel,
        out_shape=jax.ShapeDtypeStruct((ROWS + EXTRA, FEAT), jnp.bfloat16),
        in_specs=[VMEM] * 3,
        out_specs=VMEM,
    )(embeddings, ids, seeds[None, :])

    own = gather(block, ("zlo", "x"), 8)
    other = lax.ppermute(own, "core", [(0, 1), (1, 0)])
    even = jnp.where(core == 0, own[:, ROWS, : BLOCKS + ROWS], other[:, ROWS, : BLOCKS + ROWS])
    odd = jnp.where(core == 0, other[:, ROWS, : BLOCKS + ROWS], own[:, ROWS, : BLOCKS + ROWS])
    notes = jnp.stack([even, odd], axis=1).reshape(GROUP, BLOCKS + ROWS).astype(jnp.float32)
    seeds_cols = notes[:, BLOCKS:].astype(jnp.int32)
    bits = notes[:, :BLOCKS].reshape(GROUP, GROUP, GROUP)
    is_row = jnp.arange(GROUP) == row_index
    passed_on = jnp.sum(jnp.where(is_row, bits, 0.0), axis=2)
    mine = lax.dynamic_index_in_dim(notes, row_index, 0, keepdims=False)[:BLOCKS]

    passed_row = jnp.zeros((EXTRA, FEAT), jnp.float32)
    passed_row = passed_row.at[:, :GROUP].set(passed_on[:EXTRA])
    passed_row = passed_row.at[:, ROWS : ROWS + GROUP].set(passed_on[EXTRA:])
    block = jnp.concatenate([block[:ROWS], passed_row.astype(jnp.bfloat16)], axis=0)
    planes = lax.all_gather(block, "zhi")
    rows = gather(planes, "y", 4)
    passed = jnp.swapaxes(rows[:, :, ROWS:, : 2 * ROWS], 0, 1).reshape(GROUP, EXTRA, 2 * ROWS)
    passed = passed.astype(jnp.float32)
    is_col = jnp.arange(ROWS) == col_index
    low = jnp.sum(jnp.where(is_col, passed[:, :, :ROWS], 0.0), axis=2)
    high = jnp.sum(jnp.where(is_col, passed[:, :, ROWS:], 0.0), axis=2)
    mirrored = jnp.concatenate([low, high], axis=1)
    counts = (mine + mirrored.reshape(BLOCKS)).astype(jnp.int32)

    place = jnp.stack([core, col_index * GROUP + row_index]).astype(jnp.int32)
    tiles, listing, partial_degree = pl.pallas_call(
        build_kernel,
        out_shape=(
            jax.ShapeDtypeStruct((BLOCKS, 2 * ROWS, ROWS), jnp.bfloat16),
            jax.ShapeDtypeStruct((BLOCKS + 1,), jnp.int32),
            jax.ShapeDtypeStruct((GROUP, ROWS), jnp.float32),
        ),
        in_specs=[SMEM, SMEM, ANY, ANY, ANY],
        out_specs=(ANY, SMEM, VMEM),
        scratch_shapes=[
            pltpu.VMEM((GROUP, ROWS, FEAT), jnp.bfloat16),
            pltpu.VMEM((GROUP, ROWS, FEAT), jnp.bfloat16),
            pltpu.VMEM((2, CHUNK, 2 * ROWS, ROWS), jnp.bfloat16),
            pltpu.VMEM((GROUP, ROWS, ROWS), jnp.float32),
            pltpu.SemaphoreType.DMA,
            pltpu.SemaphoreType.DMA((2,)),
        ],
        compiler_params=pltpu.CompilerParams(vmem_limit_bytes=48 << 20),
    )(place, counts, own, other, rows)

    degree = jnp.sum(gather(partial_degree, ROW, GROUP), axis=0)
    scale = lax.rsqrt(degree)
    own_scale = lax.dynamic_index_in_dim(scale, row_index, 0)
    own_seeded = (seeds[None, :] == jnp.arange(CLASSES, dtype=jnp.int32)[:, None]).astype(jnp.float32)

    partial = pl.pallas_call(first_kernel, in_specs=[SMEM, ANY, VMEM, VMEM], **APPLY)(
        listing, tiles, seeds_cols, scale
    )
    labels = None
    for sweep in range(3):
        if sweep:
            spread = gather(own_scale * labels, ROW, GROUP)
            partial = pl.pallas_call(next_kernel, in_specs=[SMEM, ANY, VMEM], **APPLY)(
                listing, tiles, spread
            )
        summed = jnp.sum(exchange(partial, COL), axis=0)
        labels = BLEND * own_scale * summed + (1.0 - BLEND) * own_seeded
    return (CLASSES * labels).T


def solution(mesh):
    fine = Mesh(mesh.devices.reshape(SIZES), AXES)
    return jax.shard_map(
        local,
        mesh=fine,
        in_specs=(P(AXES, None), P(ROW, COL, None, None), P(AXES)),
        out_specs=P(AXES, None),
        check_vma=False,
    )
```

time: 959 us -> 245 us (0.26)
  waiting for transfers between devices: 643 us -> 61.5 us
  blocking collectives: 189 us -> 120 us
  local copies, waits for them, and re-layouts: 52.3 us -> 8.4 us
  matrix products: 42.2 us -> 0 us
  Pallas kernels: 0 us -> 29.3 us
  starting transfers between devices: 0.47 us -> 16.8 us
  between operations: 14.5 us -> 0.22 us
    psum x3 -> x0, waiting for transfers between devices: 497 us -> none  [settle(): return lax.psum(placed, 'col')]
    all_to_all x0 -> x5, blocking collectives: none -> 98.4 us  [exchange(): return lax.all_to_all(blocks, axes, 0, 0)]
    reduce_scatter x3 -> x0, waiting for transfers between devices: 94.7 us -> none  [settle(): lax.psum_scatter(to_cols, 'row', scatter_dimension=0, tiled=True)]
    all_gather x4 -> x1, blocking collectives: 115 us -> 21.3 us  [local(): planes = lax.all_gather(block, 'zhi')]
    all_to_all x0 -> x3, waiting for transfers between devices: none -> 59.8 us  [exchange(): return lax.all_to_all(blocks, axes, 0, 0)]
    all_gather x2 -> x0, waiting for transfers between devices: 50.8 us -> none  [the longest x1 40.6 us: local(): lax.all_gather(normed, 'row', axis=0, tiled=True)]
    psum x1 -> x0, blocking collectives: 45 us -> none  [settle(): return lax.psum(placed, 'col')]
    dot_general x18 -> x0, matrix products: 42.2 us -> none  [the longest x3 16.1 us: local(): jnp.einsum('sij,sjc->sic', kernels, col_labels[col_pick], precision=highest)]
  transfers between devices with their start and end apart: 8 -> 4, of which waited for: 8 -> 4; matrix products, arithmetic and copies ran while one was open for 3% -> 1% of each run, Pallas kernels for 0% -> 0%
where the time goes in v1:
time: 245 us; the launch traced here: 244 us
  blocking collectives  120 us (49%)
  waiting for transfers between devices  61.5 us (25%)
  Pallas kernels  29.3 us (12%)
  starting transfers between devices  16.8 us (7%)
  local copies, waits for them, and re-layouts  8.4 us (3%)
  other arithmetic  7.95 us (3%)
    all_to_all x5, blocking collectives, exchange(): return lax.all_to_all(blocks, axes, 0, 0)  98.4 us
    all_to_all x3, waiting for transfers between devices, exchange(): return lax.all_to_all(blocks, axes, 0, 0)  59.8 us
    all_gather x1, blocking collectives, local(): planes = lax.all_gather(block, 'zhi')  21.3 us
    all_to_all x3, starting transfers between devices, exchange(): return lax.all_to_all(blocks, axes, 0, 0)  16.8 us
    pallas_call x1, Pallas kernels, local(): pl.pallas_call(build_kernel, out_shape=(jax.ShapeDtypeStruct((BLOCKS, 2 *...  13.4 us
    pallas_call x2, Pallas kernels, local(): pl.pallas_call(next_kernel, in_specs=[SMEM, ANY, VMEM], **APPLY)  8.93 us
    pallas_call x1, Pallas kernels, local(): pl.pallas_call(first_kernel, in_specs=[SMEM, ANY, VMEM, VMEM], **APPLY)  5.26 us
  transfers between devices with their start and end apart: 4, of which 4 were waited for; matrix products, arithmetic and copies ran while one was open for 1% of the time, Pallas kernels for 0%

profile of v1, /device:TPU:32, one launch (start us, length us, event | category | flops | bytes accessed | tf_op | source)
XLA Modules:
  0.0 244.0 jit_solution(5150684840386613193)
XLA Ops:
  0.0 0.8 fusion.6
  0.8 0.1 copy.12
  0.8 0.1 copy.13
  0.9 0.6 add_select_fusion.ids_ref
  1.5 1.8 shard_map.37
  3.3 1.0 broadcast_in_dim.60
  4.3 0.0 slice-start
  4.4 26.8 %all_to_all.40.own_ref = bf16[8,136,768]{2,1,0:T(8,128)(2,1)S(1)} all-to-all(bf16[8,136,768]{2,1,0:T(8,128)(2,1)S(1)} %broadcast_in_dim.60), channel_id=1, replica_groups=mesh['zlo'=2,'x'=4,'core'=2,'zhi'=4,'y'=4] {'zlo','x'}, dimensions={0} | all-to-all | bytes 3342336 | tf_op jit(solution)/shard_map/all_to_all | solution.py:195
  31.2 0.0 collective-permute-start
  31.2 0.7 compare_reduce_fusion.1
  31.9 0.6 compare_reduce_fusion
  32.5 0.5 iota_compare_fusion.2
  33.0 1.7 collective-permute-done.other_ref
  34.8 0.6 maximum_convert_fusion
  35.4 1.4 reshape.184
  36.8 0.7 slice.95
  37.5 0.7 reshape.182
  38.2 1.0 select_reduce_fusion
  39.3 1.2 slice_select_fusion.2
  40.5 0.2 scatter.9
  40.6 0.0 slice-done
  40.7 21.3 %all-gather = bf16[544,768]{1,0:T(8,128)(2,1)S(1)} all-gather(bf16[136,768]{1,0:T(8,128)(2,1)S(1)} %pad_maximum_fusion), channel_id=2, replica_groups=mesh['zlo'=2,'x'=4,'core'=2,'zhi'=4,'y'=4] {'zhi'}, dimensions={0}, use_global_device_ids=true | all-gather | bytes 1044480 | tf_op jit(solution)/shard_map/all_gather | solution.py:230
  62.0 1.9 broadcast_in_dim.64
  63.9 4.7 %all-to-all-start.1 = ((bf16[4,4,136,768]{3,2,1,0:T(8,128)(2,1)}), bf16[4,4,136,768]{3,2,1,0:T(8,128)(2,1)}, u32[]{:S(2)}, u32[]{:S(2)}) async-start(bf16[4,4,136,768]{3,2,1,0:T(8,128)(2,1)} %broadcast_in_dim.64), calls=%async_computation.1 | async-start | bytes 6684672 | tf_op jit(solution)/shard_map/all_to_all | solution.py:195
  68.7 0.1 pad_add_fusion.place_ref
  68.7 0.7 constant_dynamic-slice_fusion.1
  69.4 36.8 %all-to-all-done.1.rows_ref = bf16[4,4,136,768]{3,2,1,0:T(8,128)(2,1)} async-done(((bf16[4,4,136,768]{3,2,1,0:T(8,128)(2,1)}), bf16[4,4,136,768]{3,2,1,0:T(8,128)(2,1)}, u32[]{:S(2)}, u32[]{:S(2)}) %all-to-all-start.1) | async-done | bytes 3342368 | tf_op jit(solution)/shard_map/all_to_all | solution.py:195
  106.2 0.8 convert_bitcast_fusion
  107.1 0.1 fusion.1
  107.2 0.1 pad_maximum_fusion.1
  107.2 0.1 reshape.183
  107.3 13.4 %shard_map.38 = (bf16[256,256,128]{2,1,0:T(8,128)(2,1)}, s32[257]{0:T(512)S(1)}, f32[16,128]{1,0:T(8,128)S(1)}) custom-call(s32[2]{0:T(128)S(1)} %pad_add_fusion.place_ref, s32[256]{0:T(256)S(1)} %add_convert_fusion.count_ref, bf16[8,136,768]{2,1,0:T(8,128)(2,1)S(1)} %all_to_all.40.own_ref, bf16[8,136,768]{2,1,0:T(8,128)(2,1)S(1)} %collective-permute-done.other_ref, ...), custom_call_target="tpu_custom_call" | custom-call | tf_op jit(solution)/shard_map/pallas_call | solution.py:241
  120.7 0.6 broadcast_in_dim.66
  121.4 7.6 %all-to-all-start.2 = ((f32[16,16,128]{2,1,0:T(8,128)}), f32[16,16,128]{2,1,0:T(8,128)S(1)}, u32[]{:S(2)}, u32[]{:S(2)}) async-start(f32[16,16,128]{2,1,0:T(8,128)} %broadcast_in_dim.66), calls=%async_computation.2 | async-start | bytes 262144 | tf_op jit(solution)/shard_map/all_to_all | solution.py:195
  128.9 0.7 slice_convert_fusion.seeds_ref
  129.6 4.6 %all-to-all-done.2 = f32[16,16,128]{2,1,0:T(8,128)S(1)} async-done(((f32[16,16,128]{2,1,0:T(8,128)}), f32[16,16,128]{2,1,0:T(8,128)S(1)}, u32[]{:S(2)}, u32[]{:S(2)}) %all-to-all-start.2) | async-done | bytes 131104 | tf_op jit(solution)/shard_map/all_to_all | solution.py:195
  134.3 0.0 copy-start
  134.3 5.3 %shard_map.39 = f32[16,64,128]{2,1,0:T(8,128)} custom-call(s32[257]{0:T(512)S(1)} %get-tuple-element.33.list_ref, bf16[256,256,128]{2,1,0:T(8,128)(2,1)} %get-tuple-element.34.tiles_ref, s32[16,128]{1,0:T(8,128)S(1)} %slice_convert_fusion.seeds_ref, f32[16,128]{1,0:T(8,128)S(1)} %rsqrt.3.scale_ref), custom_call_target="tpu_custom_call" | custom-call | tf_op jit(solution)/shard_map/pallas_call | solution.py:266
  139.6 4.5 %all-to-all-start.3 = ((f32[16,64,128]{2,1,0:T(8,128)}), f32[16,64,128]{2,1,0:T(8,128)S(1)}, u32[]{:S(2)}, u32[]{:S(2)}) async-start(f32[16,64,128]{2,1,0:T(8,128)} %shard_map.39), calls=%async_computation.3 | async-start | bytes 1048576 | tf_op jit(solution)/shard_map/all_to_all | solution.py:195
  144.1 18.5 %all-to-all-done.3 = f32[16,64,128]{2,1,0:T(8,128)S(1)} async-done(((f32[16,64,128]{2,1,0:T(8,128)}), f32[16,64,128]{2,1,0:T(8,128)S(1)}, u32[]{:S(2)}, u32[]{:S(2)}) %all-to-all-start.3) | async-done | bytes 524320 | tf_op jit(solution)/shard_map/all_to_all | solution.py:195
  162.6 0.0 copy-done
  162.7 13.5 %all_to_all.41.spread_ref = f32[16,64,128]{2,1,0:T(8,128)S(1)} all-to-all(f32[16,64,128]{2,1,0:T(8,128)S(1)} %broadcast_in_dim.67), channel_id=1, replica_groups=mesh['zlo'=2,'x'=4,'core'=2,'zhi'=4,'y'=4] {'zlo','x','core'}, dimensions={0} | all-to-all | bytes 1048576 | tf_op jit(solution)/shard_map/all_to_all | solution.py:195
  176.2 4.5 %shard_map.40 = f32[16,64,128]{2,1,0:T(8,128)S(1)} custom-call(s32[257]{0:T(512)S(1)} %get-tuple-element.33.list_ref, bf16[256,256,128]{2,1,0:T(8,128)(2,1)} %get-tuple-element.34.tiles_ref, f32[16,64,128]{2,1,0:T(8,128)S(1)} %all_to_all.41.spread_ref), custom_call_target="tpu_custom_call" | custom-call | tf_op jit(solution)/shard_map/pallas_call | solution.py:273
  180.7 21.6 %all_to_all.42 = f32[16,64,128]{2,1,0:T(8,128)S(1)} all-to-all(f32[16,64,128]{2,1,0:T(8,128)S(1)} %shard_map.40), channel_id=1, replica_groups=mesh['zlo'=2,'x'=4,'core'=2,'zhi'=4,'y'=4] {'zhi','y'}, dimensions={0} | all-to-all | bytes 1048576 | tf_op jit(solution)/shard_map/all_to_all | solution.py:195
  202.4 14.7 %all_to_all.43.spread_ref = f32[16,64,128]{2,1,0:T(8,128)S(1)} all-to-all(f32[16,64,128]{2,1,0:T(8,128)S(1)} %broadcast_in_dim.68), channel_id=1, replica_groups=mesh['zlo'=2,'x'=4,'core'=2,'zhi'=4,'y'=4] {'zlo','x','core'}, dimensions={0} | all-to-all | bytes 1048576 | tf_op jit(solution)/shard_map/all_to_all | solution.py:195
  217.1 4.5 %shard_map.41 = f32[16,64,128]{2,1,0:T(8,128)S(1)} custom-call(s32[257]{0:T(512)S(1)} %get-tuple-element.33.list_ref, bf16[256,256,128]{2,1,0:T(8,128)(2,1)} %get-tuple-element.34.tiles_ref, f32[16,64,128]{2,1,0:T(8,128)S(1)} %all_to_all.43.spread_ref), custom_call_target="tpu_custom_call" | custom-call | tf_op jit(solution)/shard_map/pallas_call | solution.py:273
  221.6 21.8 %all_to_all.44 = f32[16,64,128]{2,1,0:T(8,128)S(1)} all-to-all(f32[16,64,128]{2,1,0:T(8,128)S(1)} %shard_map.41), channel_id=1, replica_groups=mesh['zlo'=2,'x'=4,'core'=2,'zhi'=4,'y'=4] {'zhi','y'}, dimensions={0} | all-to-all | bytes 1048576 | tf_op jit(solution)/shard_map/all_to_all | solution.py:195
  243.3 0.6 fusion.4
  (16 shorter events, 0.3 us)
Async XLA Ops:
  4.3 36.3 %slice-start = ((bf16[136,768]{1,0:T(8,128)(2,1)}), bf16[128,768]{1,0:T(8,128)(2,1)S(1)}, s32[]{:S(2)}) async-start(bf16[136,768]{1,0:T(8,128)(2,1)} %shard_map.37), calls=%async_computation.8 | async-start | bytes 393216 | tf_op jit(solution)/shard_map/slice | solution.py:229
  31.2 3.6 %collective-permute-start = (bf16[8,136,768]{2,1,0:T(8,128)(2,1)S(1)}, bf16[8,136,768]{2,1,0:T(8,128)(2,1)S(1)}, u32[]{:S(2)}, u32[]{:S(2)}) collective-permute-start(bf16[8,136,768]{2,1,0:T(8,128)(2,1)S(1)} %all_to_all.40.own_ref), channel_id=1, source_target_pairs={{0,16},{16,0},{1,17},{17,1},{2,18},{18,2},{3,19},{19,3},{4,20},{20... | collective-permute-start | bytes 5013512 | tf_op jit(solution)/shard_map/ppermute | solution.py:216
  63.9 42.3 %all-to-all-start.1 = ((bf16[4,4,136,768]{3,2,1,0:T(8,128)(2,1)}), bf16[4,4,136,768]{3,2,1,0:T(8,128)(2,1)}, u32[]{:S(2)}, u32[]{:S(2)}) async-start(bf16[4,4,136,768]{3,2,1,0:T(8,128)(2,1)} %broadcast_in_dim.64), calls=%async_computation.1 | async-start | bytes 6684672 | tf_op jit(solution)/shard_map/all_to_all | solution.py:195
  121.4 12.9 %all-to-all-start.2 = ((f32[16,16,128]{2,1,0:T(8,128)}), f32[16,16,128]{2,1,0:T(8,128)S(1)}, u32[]{:S(2)}, u32[]{:S(2)}) async-start(f32[16,16,128]{2,1,0:T(8,128)} %broadcast_in_dim.66), calls=%async_computation.2 | async-start | bytes 262144 | tf_op jit(solution)/shard_map/all_to_all | solution.py:195
  134.3 28.3 %copy-start = (s32[128]{0:T(128)S(1)}, s32[128]{0:T(128)}, u32[]{:S(2)}) copy-start(s32[128]{0:T(128)} %param.9) | copy-start | bytes 1540
  139.6 23.0 %all-to-all-start.3 = ((f32[16,64,128]{2,1,0:T(8,128)}), f32[16,64,128]{2,1,0:T(8,128)S(1)}, u32[]{:S(2)}, u32[]{:S(2)}) async-start(f32[16,64,128]{2,1,0:T(8,128)} %shard_map.39), calls=%async_computation.3 | async-start | bytes 1048576 | tf_op jit(solution)/shard_map/all_to_all | solution.py:195

commit v2 on v1

--- a/solution.py
+++ b/solution.py
@@ -26,22 +26,74 @@
 ANY = pl.BlockSpec(memory_space=pl.ANY)
 
 
-def prep_kernel(emb_ref, ids_ref, seeds_ref, out_ref):
+def prep_kernel(place_ref, emb_ref, slots_ref, seeds_ref, out_ref, bits_ref):
     features = emb_ref[...].astype(jnp.float32)
     norm = lax.rsqrt(jnp.sum(features * features, axis=1, keepdims=True) + EPSILON)
     out_ref[:ROWS, :] = (features * norm).astype(jnp.bfloat16)
-    lane = lax.broadcasted_iota(jnp.int32, (32, BLOCKS), 1)
-    bits = jnp.sum((ids_ref[...] == lane).astype(jnp.float32), axis=0, keepdims=True)
-    row = jnp.concatenate(
-        [bits, seeds_ref[...].astype(jnp.float32), jnp.zeros((1, FEAT - BLOCKS - ROWS), jnp.float32)],
-        axis=1,
+    first, second = slots_ref[0:1, :], slots_ref[1:2, :]
+    ids = jnp.where(first >= 0, first * GROUP + second, -1)
+    hits = (lax.broadcasted_iota(jnp.int32, (BLOCKS, 32), 0) == ids).astype(jnp.float32)
+    bits = lax.dot_general(
+        jnp.ones((EXTRA, 32), jnp.float32), hits, (((1,), (1,)), ((), ())),
+        preferred_element_type=jnp.float32,
     )
-    out_ref[ROWS:, :] = jnp.broadcast_to(row, (EXTRA, FEAT)).astype(jnp.bfloat16)
-
-
-def build_kernel(place_ref, count_ref, own_ref, other_ref, rows_ref,
-                 tiles_ref, list_ref, deg_ref, cols_v, rows_v, stage, sums, in_sem, out_sem):
+    bits_ref[...] = bits.astype(jnp.int32)
+    out_ref[ROWS:, :BLOCKS] = bits.astype(jnp.bfloat16)
+    out_ref[ROWS:, BLOCKS : BLOCKS + ROWS] = jnp.broadcast_to(
+        seeds_ref[...].astype(jnp.float32), (EXTRA, ROWS)
+    ).astype(jnp.bfloat16)
+    out_ref[ROWS:, BLOCKS + ROWS :] = jnp.zeros((EXTRA, FEAT - BLOCKS - ROWS), jnp.bfloat16)
+
+
+def relay_kernel(place_ref, block_ref, own_ref, other_ref, out_ref, seeds_ref, notes, sem, block_sem):
+    core, row_index = place_ref[0], place_ref[2]
+    keep = pltpu.make_async_copy(
+        block_ref.at[pl.ds(0, ROWS)], out_ref.at[pl.ds(0, ROWS)], block_sem
+    )
+    keep.start()
+    area = (pl.ds(ROWS, EXTRA), pl.ds(0, BLOCKS + ROWS))
+    copies = []
+    for k in range(GROUP // 2):
+        copies.append((own_ref.at[(k, *area)], notes.at[2 * k + core]))
+        copies.append((other_ref.at[(k, *area)], notes.at[2 * k + 1 - core]))
+    copies = [pltpu.make_async_copy(src, dst, sem) for src, dst in copies]
+    for copy in copies:
+        copy.start()
+    slot = lax.broadcasted_iota(jnp.int32, (BLOCKS, ROWS), 0)
+    lane = lax.broadcasted_iota(jnp.int32, (BLOCKS, ROWS), 1)
+    pick = (slot == lane * GROUP + row_index) & (lane < GROUP)
+    pick = pick.astype(jnp.float32).astype(jnp.bfloat16)
+    line = lax.broadcasted_iota(jnp.int32, (EXTRA, ROWS), 0)
+    for copy in copies:
+        copy.wait()
+    for half in range(2):
+        passed = jnp.zeros((EXTRA, ROWS), jnp.float32)
+        seeds = jnp.zeros((EXTRA, ROWS), jnp.float32)
+        for k in range(EXTRA):
+            note = notes[half * EXTRA + k]
+            picked = jnp.dot(note[:, :BLOCKS], pick, preferred_element_type=jnp.float32)
+            passed = jnp.where(line == k, picked, passed)
+            seeds = jnp.where(line == k, note[:, BLOCKS:].astype(jnp.float32), seeds)
+        seeds_ref[half * EXTRA : (half + 1) * EXTRA, :] = seeds.astype(jnp.int32)
+        out_ref[ROWS:, half * ROWS : (half + 1) * ROWS] = passed.astype(jnp.bfloat16)
+    out_ref[ROWS:, 2 * ROWS :] = jnp.zeros((EXTRA, FEAT - 2 * ROWS), jnp.bfloat16)
+    keep.wait()
+
+
+def build_kernel(place_ref, bits_ref, own_ref, other_ref, rows_ref,
+                 tiles_ref, list_ref, deg_ref, cols_v, rows_v, stage, sums,
+                 notes, mirror_v, mirror_ref, count_ref, in_sem, out_sem, note_sem, mirror_sem):
     core, diag_slot = place_ref[0], place_ref[1]
+    note_copies = [
+        pltpu.make_async_copy(
+            rows_ref.at[k % 4, k // 4, pl.ds(ROWS, EXTRA), pl.ds(0, 2 * ROWS)],
+            notes.at[pl.ds(k * EXTRA, EXTRA)],
+            note_sem,
+        )
+        for k in range(GROUP)
+    ]
+    for copy in note_copies:
+        copy.start()
     copies = []
     for k in range(GROUP // 2):
         copies.append((own_ref.at[k, pl.ds(0, ROWS)], cols_v.at[2 * k + core]))
@@ -52,10 +104,25 @@
     for copy in copies:
         copy.start()
 
+    line = lax.broadcasted_iota(jnp.int32, (EXTRA, 2 * ROWS), 0)
+    lane = lax.broadcasted_iota(jnp.int32, (EXTRA, 2 * ROWS), 1)
+    pick = ((lane == line * ROWS + place_ref[3]) & (line < 2)).astype(jnp.float32)
+    for copy in note_copies:
+        copy.wait()
+    mirror_v[...] = lax.dot_general(
+        pick.astype(jnp.bfloat16), notes[...], (((1,), (1,)), ((), ())),
+        preferred_element_type=jnp.float32,
+    ).astype(jnp.int32)
+    mirror_copy = pltpu.make_async_copy(mirror_v, mirror_ref, mirror_sem)
+    mirror_copy.start()
+    mirror_copy.wait()
+
     def add_slot(slot, found):
-        live = count_ref[slot] > 0
+        a, b = slot // GROUP, lax.rem(slot, GROUP)
+        count = bits_ref[0, slot] + mirror_ref[b // EXTRA, a * EXTRA + lax.rem(b, EXTRA)]
+        count_ref[slot] = count
         list_ref[found] = slot
-        return found + live.astype(jnp.int32)
+        return found + (count > 0).astype(jnp.int32)
 
     found = lax.fori_loop(0, BLOCKS, add_slot, jnp.int32(0), unroll=8)
     chunks = (found + CHUNK - 1) // CHUNK
@@ -161,33 +228,45 @@
     lax.fori_loop(0, chunks, chunk_step, 0)
 
 
-def first_kernel(list_ref, tiles_ref, seeds_ref, scale_ref, out_ref, wide, buf, sem):
+def seeded_block(seeds_ref, b):
+    classes = lax.broadcasted_iota(jnp.int32, (CLASSES, ROWS), 0)
+    return classes == seeds_ref[pl.ds(b, 1), :]
+
+
+def first_kernel(place_ref, list_ref, tiles_ref, seeds_ref, parts_ref,
+                 out_ref, scale_ref, own_ref, total, wide, buf, sem):
     def fill():
-        classes = lax.broadcasted_iota(jnp.int32, (CLASSES, ROWS), 0)
+        scale_ref[...] = lax.rsqrt(jnp.sum(parts_ref[...], axis=0))
+        own_ref[...] = scale_ref[pl.ds(place_ref[2], 1), :]
         for b in range(GROUP):
-            seeded = classes == seeds_ref[pl.ds(b, 1), :]
-            split_into(wide, b, jnp.where(seeded, scale_ref[pl.ds(b, 1), :], 0.0))
-
-    run_apply(list_ref, tiles_ref, out_ref, wide, buf, sem, fill)
-
-
-def next_kernel(list_ref, tiles_ref, spread_ref, out_ref, wide, buf, sem):
+            split_into(wide, b, jnp.where(seeded_block(seeds_ref, b), scale_ref[b : b + 1, :], 0.0))
+
+    run_apply(list_ref, tiles_ref, total, wide, buf, sem, fill)
+    out_ref[...] = total[...].astype(jnp.bfloat16)
+
+
+def next_kernel(list_ref, tiles_ref, seeds_ref, scale_ref, smooth_ref,
+                out_ref, total, wide, buf, sem):
     def fill():
         for b in range(GROUP):
-            split_into(wide, b, spread_ref[b])
-
-    run_apply(list_ref, tiles_ref, out_ref, wide, buf, sem, fill)
-
-
+            seed_part = jnp.where(
+                seeded_block(seeds_ref, b), (1.0 - BLEND) * scale_ref[b : b + 1, :], 0.0
+            )
+            split_into(wide, b, smooth_ref[b].astype(jnp.float32) + seed_part)
+
+    run_apply(list_ref, tiles_ref, total, wide, buf, sem, fill)
+    out_ref[...] = total[...].astype(jnp.bfloat16)
+
+
+PARTIAL = jax.ShapeDtypeStruct((GROUP, CLASSES, ROWS), jnp.bfloat16)
 APPLY = dict(
-    out_shape=jax.ShapeDtypeStruct((GROUP, CLASSES, ROWS), jnp.float32),
-    out_specs=VMEM,
     scratch_shapes=[
+        pltpu.VMEM((GROUP, CLASSES, ROWS), jnp.float32),
         pltpu.VMEM((GROUP, 2 * CLASSES, 2 * ROWS), jnp.bfloat16),
         pltpu.VMEM((DEPTH, CHUNK, 2 * ROWS, ROWS), jnp.bfloat16),
         pltpu.SemaphoreType.DMA((DEPTH,)),
     ],
-    compiler_params=pltpu.CompilerParams(vmem_limit_bytes=48 << 20),
+    compiler_params=pltpu.CompilerParams(vmem_limit_bytes=8 << 20),
 )
 
 
@@ -202,42 +281,41 @@
 def local(embeddings, tile_list, seeds):
     row_index = lax.axis_index(ROW)
     col_index = lax.axis_index(COL)
-    core = lax.axis_index("core")
-    slots = tile_list.reshape(-1, 2)
-    ids = jnp.where(slots[:, :1] >= 0, slots[:, :1] * GROUP + slots[:, 1:], -1)
-    block = pl.pallas_call(
+    place = jnp.stack(
+        [lax.axis_index("core"), col_index * GROUP + row_index, row_index, col_index]
+    ).astype(jnp.int32)
+    block, bits = pl.pallas_call(
         prep_kernel,
-        out_shape=jax.ShapeDtypeStruct((ROWS + EXTRA, FEAT), jnp.bfloat16),
-        in_specs=[VMEM] * 3,
-        out_specs=VMEM,
-    )(embeddings, ids, seeds[None, :])
+        out_shape=(
+            jax.ShapeDtypeStruct((ROWS + EXTRA, FEAT), jnp.bfloat16),
+            jax.ShapeDtypeStruct((EXTRA, BLOCKS), jnp.int32),
+        ),
+        in_specs=[SMEM] + [VMEM] * 3,
+        out_specs=(VMEM, VMEM),
+        compiler_params=pltpu.CompilerParams(vmem_limit_bytes=4 << 20),
+    )(place, embeddings, tile_list.reshape(-1, 2).T, seeds[None, :])
 
     own = gather(block, ("zlo", "x"), 8)
     other = lax.ppermute(own, "core", [(0, 1), (1, 0)])
-    even = jnp.where(core == 0, own[:, ROWS, : BLOCKS + ROWS], other[:, ROWS, : BLOCKS + ROWS])
-    odd = jnp.where(core == 0, other[:, ROWS, : BLOCKS + ROWS], own[:, ROWS, : BLOCKS + ROWS])
-    notes = jnp.stack([even, odd], axis=1).reshape(GROUP, BLOCKS + ROWS).astype(jnp.float32)
-    seeds_cols = notes[:, BLOCKS:].astype(jnp.int32)
-    bits = notes[:, :BLOCKS].reshape(GROUP, GROUP, GROUP)
-    is_row = jnp.arange(GROUP) == row_index
-    passed_on = jnp.sum(jnp.where(is_row, bits, 0.0), axis=2)
-    mine = lax.dynamic_index_in_dim(notes, row_index, 0, keepdims=False)[:BLOCKS]
-
-    passed_row = jnp.zeros((EXTRA, FEAT), jnp.float32)
-    passed_row = passed_row.at[:, :GROUP].set(passed_on[:EXTRA])
-    passed_row = passed_row.at[:, ROWS : ROWS + GROUP].set(passed_on[EXTRA:])
-    block = jnp.concatenate([block[:ROWS], passed_row.astype(jnp.bfloat16)], axis=0)
+    block, seeds_cols = pl.pallas_call(
+        relay_kernel,
+        out_shape=(
+            jax.ShapeDtypeStruct((ROWS + EXTRA, FEAT), jnp.bfloat16),
+            jax.ShapeDtypeStruct((GROUP, ROWS), jnp.int32),
+        ),
+        in_specs=[SMEM, ANY, ANY, ANY],
+        out_specs=(VMEM, VMEM),
+        scratch_shapes=[
+            pltpu.VMEM((GROUP, EXTRA, BLOCKS + ROWS), jnp.bfloat16),
+            pltpu.SemaphoreType.DMA,
+            pltpu.SemaphoreType.DMA,
+        ],
+        compiler_params=pltpu.CompilerParams(vmem_limit_bytes=4 << 20),
+    )(place, block, own, other)
+
     planes = lax.all_gather(block, "zhi")
     rows = gather(planes, "y", 4)
-    passed = jnp.swapaxes(rows[:, :, ROWS:, : 2 * ROWS], 0, 1).reshape(GROUP, EXTRA, 2 * ROWS)
-    passed = passed.astype(jnp.float32)
-    is_col = jnp.arange(ROWS) == col_index
-    low = jnp.sum(jnp.where(is_col, passed[:, :, :ROWS], 0.0), axis=2)
-    high = jnp.sum(jnp.where(is_col, passed[:, :, ROWS:], 0.0), axis=2)
-    mirrored = jnp.concatenate([low, high], axis=1)
-    counts = (mine + mirrored.reshape(BLOCKS)).astype(jnp.int32)
-
-    place = jnp.stack([core, col_index * GROUP + row_index]).astype(jnp.int32)
+
     tiles, listing, partial_degree = pl.pallas_call(
         build_kernel,
         out_shape=(
@@ -252,29 +330,43 @@
             pltpu.VMEM((GROUP, ROWS, FEAT), jnp.bfloat16),
             pltpu.VMEM((2, CHUNK, 2 * ROWS, ROWS), jnp.bfloat16),
             pltpu.VMEM((GROUP, ROWS, ROWS), jnp.float32),
+            pltpu.VMEM((GROUP * EXTRA, 2 * ROWS), jnp.bfloat16),
+            pltpu.VMEM((EXTRA, ROWS), jnp.int32),
+            pltpu.SMEM((EXTRA, ROWS), jnp.int32),
+            pltpu.SMEM((BLOCKS,), jnp.int32),
             pltpu.SemaphoreType.DMA,
             pltpu.SemaphoreType.DMA((2,)),
+            pltpu.SemaphoreType.DMA,
+            pltpu.SemaphoreType.DMA,
         ],
-        compiler_params=pltpu.CompilerParams(vmem_limit_bytes=48 << 20),
-    )(place, counts, own, other, rows)
-
-    degree = jnp.sum(gather(partial_degree, ROW, GROUP), axis=0)
-    scale = lax.rsqrt(degree)
-    own_scale = lax.dynamic_index_in_dim(scale, row_index, 0)
-    own_seeded = (seeds[None, :] == jnp.arange(CLASSES, dtype=jnp.int32)[:, None]).astype(jnp.float32)
-
-    partial = pl.pallas_call(first_kernel, in_specs=[SMEM, ANY, VMEM, VMEM], **APPLY)(
-        listing, tiles, seeds_cols, scale
-    )
-    labels = None
+        compiler_params=pltpu.CompilerParams(vmem_limit_bytes=14 << 20),
+    )(place, bits, own, other, rows)
+
+    partial, scale, own_scale = pl.pallas_call(
+        first_kernel,
+        out_shape=(
+            PARTIAL,
+            jax.ShapeDtypeStruct((GROUP, ROWS), jnp.float32),
+            jax.ShapeDtypeStruct((1, ROWS), jnp.float32),
+        ),
+        in_specs=[SMEM, SMEM, ANY, VMEM, VMEM],
+        out_specs=(VMEM, VMEM, VMEM),
+        **APPLY,
+    )(place, listing, tiles, seeds_cols, gather(partial_degree, ROW, GROUP))
     for sweep in range(3):
         if sweep:
-            spread = gather(own_scale * labels, ROW, GROUP)
-            partial = pl.pallas_call(next_kernel, in_specs=[SMEM, ANY, VMEM], **APPLY)(
-                listing, tiles, spread
-            )
-        summed = jnp.sum(exchange(partial, COL), axis=0)
-        labels = BLEND * own_scale * summed + (1.0 - BLEND) * own_seeded
+            smooth = gather((BLEND * own_scale * own_scale * summed).astype(jnp.bfloat16), ROW, GROUP)
+            partial = pl.pallas_call(
+                next_kernel,
+                out_shape=PARTIAL,
+                in_specs=[SMEM, ANY, VMEM, VMEM, VMEM],
+                out_specs=VMEM,
+                **APPLY,
+            )(listing, tiles, seeds_cols, scale, smooth)
+        summed, own_scale, seeds = lax.optimization_barrier((exchange(partial, COL), own_scale, seeds))
+        summed = jnp.sum(summed.astype(jnp.float32), axis=0)
+    seeded = seeds[None, :] == jnp.arange(CLASSES, dtype=jnp.int32)[:, None]
+    labels = BLEND * own_scale * summed + (1.0 - BLEND) * seeded.astype(jnp.float32)
     return (CLASSES * labels).T
 
 

time: 245 us -> 214 us (0.87)
  waiting for transfers between devices: 61.5 us -> 3.55 us
  blocking collectives: 120 us -> 175 us
  starting transfers between devices: 16.8 us -> 0.01 us
  other arithmetic: 7.95 us -> 0.85 us
  local copies, waits for them, and re-layouts: 8.4 us -> 2.69 us
  Pallas kernels: 29.3 us -> 31.8 us
    all_to_all x3 -> x0, waiting for transfers between devices: 59.8 us -> none  [exchange(): return lax.all_to_all(blocks, axes, 0, 0)]
    all_to_all x5 -> x8, blocking collectives: 98.4 us -> 153 us  [exchange(): return lax.all_to_all(blocks, axes, 0, 0)]
    all_to_all x3 -> x0, starting transfers between devices: 16.8 us -> none  [exchange(): return lax.all_to_all(blocks, axes, 0, 0)]
    pallas_call x1, Pallas kernels: 13.4 us -> 19.4 us  [local(): pl.pallas_call(build_kernel, out_shape=(jax.ShapeDtypeStruct((BLOCKS, 2 *...]
    pallas_call x4 -> x5, Pallas kernels: 16 us -> 12.4 us  [the longest x2 7.05 us: local(): pl.pallas_call(next_kernel, out_shape=PARTIAL, in_specs=[SMEM, ANY, VMEM,...]
    broadcast_in_dim x5, local copies, waits for them, and re-layouts: 3.67 us -> 0.42 us  [gather(): return exchange(jnp.broadcast_to(block[None], (count,) + block.shape), axes)]
    another operation x4 -> x1, other arithmetic: 2.56 us -> 0.08 us  [local(): jnp.stack([lax.axis_index('core'), col_index * GROUP + row_index, row_ind...]
  transfers between devices with their start and end apart: 4 -> 1, of which waited for: 4 -> 1; matrix products, arithmetic and copies ran while one was open for 1% -> 0% of each run, Pallas kernels for 0% -> 0%
where the time goes in v2:
time: 214 us
  blocking collectives  175 us (82%)
  Pallas kernels  31.8 us (15%)
  waiting for transfers between devices  3.55 us (2%)
  local copies, waits for them, and re-layouts  2.69 us (1%)
    all_to_all x8, blocking collectives, exchange(): return lax.all_to_all(blocks, axes, 0, 0)  153 us
    all_gather x1, blocking collectives, local(): planes = lax.all_gather(block, 'zhi')  21.3 us
    pallas_call x1, Pallas kernels, local(): pl.pallas_call(build_kernel, out_shape=(jax.ShapeDtypeStruct((BLOCKS, 2 *...  19.4 us
    pallas_call x2, Pallas kernels, local(): pl.pallas_call(next_kernel, out_shape=PARTIAL, in_specs=[SMEM, ANY, VMEM,...  7.05 us
  transfers between devices with their start and end apart: 1, of which 1 were waited for; matrix products, arithmetic and copies ran while one was open for 0% of the time, Pallas kernels for 0%

profile of v2, /device:TPU:32, one launch (start us, length us, event | category | flops | bytes accessed | tf_op | source)
XLA Modules:
  0.0 213.7 jit_solution(14874046647096533906)
XLA Ops:
  0.0 0.1 pad_add_fusion.place_ref
  0.1 0.0 copy-start
  0.1 0.9 copy-done
  1.0 0.0 copy-start.1
  1.0 0.7 copy-done.1
  1.7 0.0 copy-start.3
  1.7 0.7 copy-done.3
  2.3 0.7 shard_map.37
  3.0 0.1 broadcast_in_dim.13
  3.1 26.7 %all_to_all.40.own_ref = bf16[8,136,768]{2,1,0:T(8,128)(2,1)S(1)} all-to-all(bf16[8,136,768]{2,1,0:T(8,128)(2,1)S(1)} %broadcast_in_dim.13), channel_id=1, replica_groups=mesh['zlo'=2,'x'=4,'core'=2,'zhi'=4,'y'=4] {'zlo','x'}, dimensions={0} | all-to-all | bytes 3342336 | tf_op jit(solution)/shard_map/all_to_all | solution.py:274
  29.9 0.0 collective-permute-start
  29.9 3.5 %collective-permute-done.other_ref = bf16[8,136,768]{2,1,0:T(8,128)(2,1)S(1)} collective-permute-done((bf16[8,136,768]{2,1,0:T(8,128)(2,1)S(1)}, bf16[8,136,768]{2,1,0:T(8,128)(2,1)S(1)}, u32[]{:S(2)}, u32[]{:S(2)}) %collective-permute-start) | collective-permute-done | bytes 1671200 | tf_op jit(solution)/shard_map/ppermute | solution.py:299
  33.4 1.2 shard_map.38
  34.6 21.3 %all-gather = bf16[544,768]{1,0:T(8,128)(2,1)S(1)} all-gather(bf16[136,768]{1,0:T(8,128)(2,1)S(1)} %get-tuple-element.26), channel_id=2, replica_groups=mesh['zlo'=2,'x'=4,'core'=2,'zhi'=4,'y'=4] {'zhi'}, dimensions={0}, use_global_device_ids=true | all-gather | bytes 1044480 | tf_op jit(solution)/shard_map/all_gather | solution.py:316
  56.0 0.2 broadcast_in_dim.14
  56.2 41.5 %all_to_all.41.rows_ref = bf16[4,4,136,768]{3,2,1,0:T(8,128)(2,1)S(1)} all-to-all(bf16[4,4,136,768]{3,2,1,0:T(8,128)(2,1)S(1)} %broadcast_in_dim.14), channel_id=1, replica_groups=mesh['zlo'=2,'x'=4,'core'=2,'zhi'=4,'y'=4] {'y'}, dimensions={0} | all-to-all | bytes 6684672 | tf_op jit(solution)/shard_map/all_to_all | solution.py:274
  97.7 19.4 %shard_map.39 = (bf16[256,256,128]{2,1,0:T(8,128)(2,1)S(1)}, s32[257]{0:T(512)S(1)}, f32[16,128]{1,0:T(8,128)S(1)}) custom-call(s32[4]{0:T(128)S(1)} %pad_add_fusion.place_ref, s32[8,256]{1,0:T(8,128)S(1)} %get-tuple-element.24.bits_ref, bf16[8,136,768]{2,1,0:T(8,128)(2,1)S(1)} %all_to_all.40.own_ref, ...), custom_call_target="tpu_custom_call" | custom-call | tf_op jit(solution)/shard_map/pallas_call | solution.py:319
  117.1 12.7 %all_to_all.42.parts_ref = f32[16,16,128]{2,1,0:T(8,128)S(1)} all-to-all(f32[16,16,128]{2,1,0:T(8,128)S(1)} %broadcast_in_dim.15), channel_id=1, replica_groups=mesh['zlo'=2,'x'=4,'core'=2,'zhi'=4,'y'=4] {'zlo','x','core'}, dimensions={0} | all-to-all | bytes 262144 | tf_op jit(solution)/shard_map/all_to_all | solution.py:274
  129.8 3.5 %shard_map.40 = (bf16[16,64,128]{2,1,0:T(8,128)(2,1)S(1)}, f32[16,128]{1,0:T(8,128)S(1)}, f32[1,128]{1,0:T(1,128)S(1)}) custom-call(s32[4]{0:T(128)S(1)} %pad_add_fusion.place_ref, s32[257]{0:T(512)S(1)} %get-tuple-element.27.list_ref, bf16[256,256,128]{2,1,0:T(8,128)(2,1)S(1)} %get-tuple-element.28.tiles_ref, s32[16,128]{1,0:T(8,128)S(1)} %get-tuple-element.29.seeds_ref, ...), custom_call_target="tpu_custom_call" | custom-call | tf_op jit(solution)/shard_map/pallas_call | solution.py:345
  133.3 17.3 %all_to_all.43 = bf16[16,64,128]{2,1,0:T(8,128)(2,1)S(1)} all-to-all(bf16[16,64,128]{2,1,0:T(8,128)(2,1)S(1)} %get-tuple-element.32), channel_id=1, replica_groups=mesh['zlo'=2,'x'=4,'core'=2,'zhi'=4,'y'=4] {'zhi','y'}, dimensions={0} | all-to-all | bytes 524288 | tf_op jit(solution)/shard_map/all_to_all | solution.py:274
  150.7 11.4 %all_to_all.44.smooth_ref = bf16[16,64,128]{2,1,0:T(8,128)(2,1)S(1)} all-to-all(bf16[16,64,128]{2,1,0:T(8,128)(2,1)S(1)} %broadcast_in_dim.16), channel_id=1, replica_groups=mesh['zlo'=2,'x'=4,'core'=2,'zhi'=4,'y'=4] {'zlo','x','core'}, dimensions={0} | all-to-all | bytes 524288 | tf_op jit(solution)/shard_map/all_to_all | solution.py:274
  162.1 3.5 %shard_map.41 = bf16[16,64,128]{2,1,0:T(8,128)(2,1)S(1)} custom-call(s32[257]{0:T(512)S(1)} %get-tuple-element.27.list_ref, bf16[256,256,128]{2,1,0:T(8,128)(2,1)S(1)} %get-tuple-element.28.tiles_ref, s32[16,128]{1,0:T(8,128)S(1)} %get-tuple-element.29.seeds_ref, f32[16,128]{1,0:T(8,128)S(1)} %get-tuple-element.31.scale_ref, ...), custom_call_target="tpu_custom_call" | custom-call | tf_op jit(solution)/shard_map/pallas_call | solution.py:359
  165.6 16.3 %all_to_all.45 = bf16[16,64,128]{2,1,0:T(8,128)(2,1)S(1)} all-to-all(bf16[16,64,128]{2,1,0:T(8,128)(2,1)S(1)} %shard_map.41), channel_id=1, replica_groups=mesh['zlo'=2,'x'=4,'core'=2,'zhi'=4,'y'=4] {'zhi','y'}, dimensions={0} | all-to-all | bytes 524288 | tf_op jit(solution)/shard_map/all_to_all | solution.py:274
  182.0 10.7 %all_to_all.46.smooth_ref = bf16[16,64,128]{2,1,0:T(8,128)(2,1)S(1)} all-to-all(bf16[16,64,128]{2,1,0:T(8,128)(2,1)S(1)} %broadcast_in_dim.17), channel_id=1, replica_groups=mesh['zlo'=2,'x'=4,'core'=2,'zhi'=4,'y'=4] {'zlo','x','core'}, dimensions={0} | all-to-all | bytes 524288 | tf_op jit(solution)/shard_map/all_to_all | solution.py:274
  192.7 0.0 copy-start.2
  192.7 3.5 %shard_map.42 = bf16[16,64,128]{2,1,0:T(8,128)(2,1)S(1)} custom-call(s32[257]{0:T(512)S(1)} %get-tuple-element.27.list_ref, bf16[256,256,128]{2,1,0:T(8,128)(2,1)S(1)} %get-tuple-element.28.tiles_ref, s32[16,128]{1,0:T(8,128)S(1)} %get-tuple-element.29.seeds_ref, f32[16,128]{1,0:T(8,128)S(1)} %get-tuple-element.31.scale_ref, ...), custom_call_target="tpu_custom_call" | custom-call | tf_op jit(solution)/shard_map/pallas_call | solution.py:359
  196.2 16.8 %all_to_all.47 = bf16[16,64,128]{2,1,0:T(8,128)(2,1)S(1)} all-to-all(bf16[16,64,128]{2,1,0:T(8,128)(2,1)S(1)} %shard_map.42), channel_id=1, replica_groups=mesh['zlo'=2,'x'=4,'core'=2,'zhi'=4,'y'=4] {'zhi','y'}, dimensions={0} | all-to-all | bytes 524288 | tf_op jit(solution)/shard_map/all_to_all | solution.py:274
  213.1 0.0 copy-done.2
  213.1 0.6 fusion
  (11 shorter events, 0.2 us)
Async XLA Ops:
  0.1 0.9 copy-start
  1.0 0.7 copy-start.1
  1.7 0.7 copy-start.3
  29.9 3.6 %collective-permute-start = (bf16[8,136,768]{2,1,0:T(8,128)(2,1)S(1)}, bf16[8,136,768]{2,1,0:T(8,128)(2,1)S(1)}, u32[]{:S(2)}, u32[]{:S(2)}) collective-permute-start(bf16[8,136,768]{2,1,0:T(8,128)(2,1)S(1)} %all_to_all.40.own_ref), channel_id=1, source_target_pairs={{0,16},{16,0},{1,17},{17,1},{2,18},{18,2},{3,19},{19,3},{4,20},{20... | collective-permute-start | bytes 5013512 | tf_op jit(solution)/shard_map/ppermute | solution.py:299
  192.7 20.4 %copy-start.2 = (s32[128]{0:T(128)S(1)}, s32[128]{0:T(128)}, u32[]{:S(2)}) copy-start(s32[128]{0:T(128)} %param.5) | copy-start | bytes 1540

commit v3 on v0

v3 whole, which is shorter than its diff:
```python
import jax
import jax.numpy as jnp
from jax import lax
from jax.experimental import pallas as pl
from jax.experimental.pallas import tpu as pltpu
from jax.sharding import Mesh
from jax.sharding import PartitionSpec as P

CLASSES = 64
BLEND = 0.8
EPSILON = 1e-06
AXES = ("zlo", "x", "core", "zhi", "y")
SIZES = (2, 4, 2, 4, 4)
ROW = ("zlo", "x", "core")
COL = ("zhi", "y")
PLANE = ("x", "y")
LINE = ("zlo", "core", "zhi")
GROUP = 16
BLOCKS = GROUP * GROUP
ROWS = 128
FEAT = 768
EXTRA = 8
CHUNK = 8
VMEM = pl.BlockSpec(memory_space=pltpu.VMEM)
SMEM = pl.BlockSpec(memory_space=pltpu.SMEM)
ANY = pl.BlockSpec(memory_space=pl.ANY)


def prep_kernel(place_ref, emb_ref, slots_ref, seeds_ref, block_ref, noted_ref, seeds_out):
    features = emb_ref[...].astype(jnp.float32)
    norm = lax.rsqrt(jnp.sum(features * features, axis=1, keepdims=True) + EPSILON)
    normed = (features * norm).astype(jnp.bfloat16)
    block_ref[...] = normed
    noted_ref[:ROWS, :] = normed
    first, second = slots_ref[0:1, :], slots_ref[1:2, :]
    ids = jnp.where(first >= 0, first * GROUP + second, -1)
    hits = (lax.broadcasted_iota(jnp.int32, (BLOCKS, 32), 0) == ids).astype(jnp.float32)
    bits = lax.dot_general(
        jnp.ones((EXTRA, 32), jnp.float32), hits, (((1,), (1,)), ((), ())),
        preferred_element_type=jnp.float32,
    )
    noted_ref[ROWS:, :BLOCKS] = bits.astype(jnp.bfloat16)
    noted_ref[ROWS:, BLOCKS:] = jnp.zeros((EXTRA, FEAT - BLOCKS), jnp.bfloat16)
    seeds_out[...] = seeds_ref[...].astype(jnp.float32)


def relay_kernel(place_ref, plane_ref, seeds_ref, out_ref):
    x, y = place_ref[0], place_ref[1]
    row = lax.broadcasted_iota(jnp.int32, (EXTRA, BLOCKS), 0)
    passed = jnp.zeros((EXTRA, BLOCKS), jnp.float32)
    for k in range(4):
        for at, line in ((k * 4 + y, k), (x * 4 + k, 4 + k)):
            note = plane_ref[at, ROWS:, :BLOCKS].astype(jnp.float32)
            passed = jnp.where(row == line, note, passed)
    out_ref[:, :BLOCKS] = passed
    out_ref[:, BLOCKS:] = jnp.broadcast_to(seeds_ref[...], (EXTRA, ROWS))


def make_list(place_ref, notes_ref, list_v):
    x, y, zlo, core, zhi = (place_ref[k] for k in range(5))
    shape = (BLOCKS, BLOCKS)
    row = lax.broadcasted_iota(jnp.int32, shape, 0)
    lane = lax.broadcasted_iota(jnp.int32, shape, 1)
    u_zhi, u_x = row >> 6, (row >> 4) & 3
    v_zlo, v_core, v_y = (row >> 3) & 1, (row >> 2) & 1, row & 3
    a_zhi, a_y = lane >> 6, (lane >> 4) & 3
    b_zlo, b_x, b_core = (lane >> 3) & 1, (lane >> 1) & 3, lane & 1
    forward = (a_zhi == zhi) & (b_x == x) & (a_y == v_y) & (b_zlo == v_zlo) & (b_core == v_core)
    mirror = (a_zhi == u_zhi) & (a_y == y) & (b_zlo == zlo) & (b_x == u_x) & (b_core == core)
    ahead = []
    for u in range(GROUP):
        note = notes_ref[zlo * 8 + core * 4 + u // 4, u % 4 : u % 4 + 1, :BLOCKS]
        ahead.append(jnp.broadcast_to(note, (GROUP, BLOCKS)))
    back = [notes_ref[at * 4 + zhi, 4:8, :BLOCKS] for at in range(4)]
    ahead = jnp.concatenate(ahead, axis=0)
    back = jnp.concatenate(back * GROUP, axis=0)
    hits = jnp.where(forward, ahead, 0.0) + jnp.where(mirror, back, 0.0)
    counts = jnp.dot(
        hits.astype(jnp.bfloat16), jnp.ones(shape, jnp.bfloat16), preferred_element_type=jnp.float32
    )
    live = (counts > 0.0).astype(jnp.float32)
    upto = jnp.dot(
        (lane <= row).astype(jnp.float32).astype(jnp.bfloat16), live.astype(jnp.bfloat16),
        preferred_element_type=jnp.float32,
    )
    spot = jnp.where(lane.astype(jnp.float32) == upto - 1.0, live, 0.0)
    slot_lane = lax.broadcasted_iota(jnp.int32, (EXTRA, BLOCKS), 1)
    code = (
        (((slot_lane >> 4) & 3) * 4 + (slot_lane & 3)) * GROUP
        + ((slot_lane >> 3) & 1) * 8 + ((slot_lane >> 2) & 1) * 4 + (slot_lane >> 6)
    ).astype(jnp.float32).astype(jnp.bfloat16)
    ones = jnp.ones((EXTRA, BLOCKS), jnp.bfloat16)
    codes = jnp.dot(code, spot.astype(jnp.bfloat16), preferred_element_type=jnp.float32)
    weights = jnp.dot(ones, (spot * counts).astype(jnp.bfloat16), preferred_element_type=jnp.float32)
    found = jnp.dot(ones, live.astype(jnp.bfloat16), preferred_element_type=jnp.float32)
    line = lax.broadcasted_iota(jnp.int32, (EXTRA, BLOCKS), 0)
    table = jnp.where(line == 0, codes, jnp.where(line == 1, weights, found))
    list_v[...] = (table + 0.5).astype(jnp.int32)


def build_kernel(place_ref, notes_ref, plane_ref, own_ref, mate_ref, far_ref, far_mate_ref,
                 tiles_ref, list_ref, deg_ref, seeds_ref, line_v, sums, list_v, list_sem, line_sem):
    mine = place_ref[5]
    parts = [
        pltpu.make_async_copy(part, line_v.at[pl.ds(at * 4, 4)], line_sem)
        for at, part in enumerate((own_ref, mate_ref, far_ref, far_mate_ref))
    ]
    for part in parts:
        part.start()
    make_list(place_ref, notes_ref, list_v)
    list_copy = pltpu.make_async_copy(list_v, list_ref, list_sem)
    list_copy.start()
    for b in range(GROUP):
        seeds_ref[b : b + 1, :] = notes_ref[b, 0:1, BLOCKS:].astype(jnp.int32)
    sums[...] = jnp.zeros_like(sums)
    sharpness = FEAT**0.5
    diag_slot = place_ref[6]
    on_diag = (
        lax.broadcasted_iota(jnp.int32, (ROWS, ROWS), 0)
        == lax.broadcasted_iota(jnp.int32, (ROWS, ROWS), 1)
    ).astype(jnp.float32)
    list_copy.wait()
    for part in parts:
        part.wait()

    def build_chunk(group, carry):
        for k in range(CHUNK):
            at = group * CHUNK + k
            slot = list_ref[0, at]
            a, b = slot >> 4, slot & 15
            weight = list_ref[1, at].astype(jnp.float32)
            off = jnp.where(slot == diag_slot, weight, 0.0)
            scores = lax.dot_general(
                line_v[b ^ mine], plane_ref[a, :ROWS, :], (((1,), (1,)), ((), ())),
                preferred_element_type=jnp.float32,
            )
            tile = jnp.exp(sharpness * (scores - 1.0)) * (weight - on_diag * off)
            high = tile.astype(jnp.bfloat16)
            tiles_ref[at, :ROWS, :] = high
            tiles_ref[at, ROWS:, :] = (tile - high.astype(jnp.float32)).astype(jnp.bfloat16)
            sums[b] += tile
        return carry

    lax.fori_loop(0, (list_ref[2, 0] + CHUNK - 1) // CHUNK, build_chunk, 0)
    for b in range(GROUP):
        deg_ref[b : b + 1, :] = jnp.sum(sums[b].T, axis=0, keepdims=True)


def split_into(wide, b, spread):
    high = spread.astype(jnp.bfloat16)
    low = (spread - high.astype(jnp.float32)).astype(jnp.bfloat16)
    wide[b, :CLASSES, :ROWS] = high
    wide[b, :CLASSES, ROWS:] = high
    wide[b, CLASSES:, :ROWS] = low
    wide[b, CLASSES:, ROWS:] = jnp.zeros_like(low)


def run_apply(list_ref, tiles_ref, out_ref, total, wide):
    total[...] = jnp.zeros_like(total)

    def chunk_step(group, carry):
        for k in range(CHUNK):
            at = group * CHUNK + k
            slot = list_ref[0, at]
            both = jnp.dot(wide[slot & 15], tiles_ref[at], preferred_element_type=jnp.float32)
            total[slot >> 4] += both[:CLASSES] + both[CLASSES:]
        return carry

    lax.fori_loop(0, (list_ref[2, 0] + CHUNK - 1) // CHUNK, chunk_step, 0)
    out_ref[...] = total[...].astype(jnp.bfloat16)


def seeded_block(seeds_ref, b):
    classes = lax.broadcasted_iota(jnp.int32, (CLASSES, ROWS), 0)
    return classes == seeds_ref[b : b + 1, :]


def first_kernel(place_ref, list_ref, tiles_ref, seeds_ref, parts_ref,
                 out_ref, scale_ref, own_ref, total, wide):
    scale_ref[...] = lax.rsqrt(jnp.sum(parts_ref[...], axis=0))
    own_ref[...] = scale_ref[pl.ds(place_ref[5], 1), :]
    for b in range(GROUP):
        split_into(wide, b, jnp.where(seeded_block(seeds_ref, b), scale_ref[b : b + 1, :], 0.0))
    run_apply(list_ref, tiles_ref, out_ref, total, wide)


def next_kernel(list_ref, tiles_ref, seeds_ref, scale_ref, smooth_ref, out_ref, total, wide):
    for b in range(GROUP):
        seed_part = jnp.where(
            seeded_block(seeds_ref, b), (1.0 - BLEND) * scale_ref[b : b + 1, :], 0.0
        )
        split_into(wide, b, smooth_ref[b].astype(jnp.float32) + seed_part)
    run_apply(list_ref, tiles_ref, out_ref, total, wide)


def call(kernel, outs, ins, out_specs, scratch=(), limit=8):
    return pl.pallas_call(
        kernel,
        out_shape=outs,
        in_specs=ins,
        out_specs=out_specs,
        scratch_shapes=list(scratch),
        compiler_params=pltpu.CompilerParams(vmem_limit_bytes=limit << 20),
    )


def array(*shape, dtype=jnp.float32):
    return jax.ShapeDtypeStruct(shape, dtype)


def exchange(blocks, axes):
    return lax.all_to_all(blocks, axes, 0, 0)


def gather(block, axes):
    return exchange(jnp.broadcast_to(block[None], (GROUP,) + block.shape), axes)


def pairs(count, step):
    return [(k, k ^ step) for k in range(count)]


def local(embeddings, tile_list, seeds):
    x, y, zlo, core, zhi = (lax.axis_index(name) for name in ("x", "y", "zlo", "core", "zhi"))
    mine = zlo * 8 + core * 4 + zhi
    place = jnp.stack([x, y, zlo, core, zhi, mine, (x * 4 + y) * GROUP + mine]).astype(jnp.int32)
    block, noted, own_seeds = call(
        prep_kernel,
        (
            array(ROWS, FEAT, dtype=jnp.bfloat16),
            array(ROWS + EXTRA, FEAT, dtype=jnp.bfloat16),
            array(1, ROWS),
        ),
        [SMEM] + [VMEM] * 3,
        (VMEM,) * 3,
        limit=4,
    )(place, embeddings, tile_list.reshape(-1, 2).T, seeds[None, :])

    hops = [lax.ppermute(block, "zhi", pairs(4, step)) for step in (1, 2, 3)]
    plane = gather(noted, PLANE)
    own = jnp.stack([block] + hops)
    mate = lax.ppermute(own, "core", pairs(2, 1))
    far = lax.ppermute(own, "zlo", pairs(2, 1))
    note = call(
        relay_kernel, array(EXTRA, BLOCKS + ROWS), [SMEM, VMEM, VMEM], VMEM, limit=4
    )(place, plane, own_seeds)
    notes = gather(note, LINE)
    far_mate = lax.ppermute(far, "core", pairs(2, 1))

    tiles, listing, partial_degree, line_seeds = call(
        build_kernel,
        (
            array(BLOCKS, 2 * ROWS, ROWS, dtype=jnp.bfloat16),
            array(EXTRA, BLOCKS, dtype=jnp.int32),
            array(GROUP, ROWS),
            array(GROUP, ROWS, dtype=jnp.int32),
        ),
        [SMEM] + [VMEM] * 2 + [ANY] * 4,
        (VMEM, SMEM, VMEM, VMEM),
        (
            pltpu.VMEM((GROUP, ROWS, FEAT), jnp.bfloat16),
            pltpu.VMEM((GROUP, ROWS, ROWS), jnp.float32),
            pltpu.VMEM((EXTRA, BLOCKS), jnp.int32),
            pltpu.SemaphoreType.DMA,
            pltpu.SemaphoreType.DMA,
        ),
        limit=14,
    )(place, notes, plane, own, mate, far, far_mate)

    scratch = (
        pltpu.VMEM((GROUP, CLASSES, ROWS), jnp.float32),
        pltpu.VMEM((GROUP, 2 * CLASSES, 2 * ROWS), jnp.bfloat16),
    )
    sums_out = array(GROUP, CLASSES, ROWS, dtype=jnp.bfloat16)
    partial, scale, own_scale = call(
        first_kernel,
        (sums_out, array(GROUP, ROWS), array(1, ROWS)),
        [SMEM, SMEM, VMEM, VMEM, VMEM],
        (VMEM,) * 3,
        scratch,
        limit=6,
    )(place, listing, tiles, line_seeds, gather(partial_degree, LINE))
    for sweep in range(3):
        if sweep:
            smooth = gather((BLEND * own_scale * own_scale * summed).astype(jnp.bfloat16), LINE)
            partial = call(
                next_kernel, sums_out, [SMEM] + [VMEM] * 4, VMEM, scratch, limit=6
            )(listing, tiles, line_seeds, scale, smooth)
        summed, own_scale, seeds = lax.optimization_barrier((exchange(partial, PLANE), own_scale, seeds))
        summed = jnp.sum(summed.astype(jnp.float32), axis=0)
    seeded = seeds[None, :] == jnp.arange(CLASSES, dtype=jnp.int32)[:, None]
    labels = BLEND * own_scale * summed + (1.0 - BLEND) * seeded.astype(jnp.float32)
    return (CLASSES * labels).T


def solution(mesh):
    fine = Mesh(mesh.devices.reshape(SIZES), AXES)
    return jax.shard_map(
        local,
        mesh=fine,
        in_specs=(P(AXES, None), P(ROW, COL, None, None), P(AXES)),
        out_specs=P(AXES, None),
        check_vma=False,
    )
```

time: 959 us -> 181 us (0.19)
  waiting for transfers between devices: 643 us -> 43 us
  blocking collectives: 189 us -> 85.5 us
  local copies, waits for them, and re-layouts: 52.3 us -> 5.06 us
  matrix products: 42.2 us -> 0 us
  starting transfers between devices: 0.47 us -> 25 us
  Pallas kernels: 0 us -> 17.5 us
  between operations: 14.5 us -> 0.14 us
  other arithmetic: 14.1 us -> 1.78 us
    psum x3 -> x0, waiting for transfers between devices: 497 us -> none  [settle(): return lax.psum(placed, 'col')]
    all_gather x4 -> x0, blocking collectives: 115 us -> none  [the longest x3 59.6 us: local(): lax.all_gather(own_spread, 'row', axis=0, tiled=True)]
    reduce_scatter x3 -> x0, waiting for transfers between devices: 94.7 us -> none  [settle(): lax.psum_scatter(to_cols, 'row', scatter_dimension=0, tiled=True)]
    all_to_all x0 -> x6, blocking collectives: none -> 85.5 us  [exchange(): return lax.all_to_all(blocks, axes, 0, 0)]
    all_gather x2 -> x0, waiting for transfers between devices: 50.8 us -> none  [the longest x1 40.6 us: local(): lax.all_gather(normed, 'row', axis=0, tiled=True)]
    psum x1 -> x0, blocking collectives: 45 us -> none  [settle(): return lax.psum(placed, 'col')]
    dot_general x18 -> x0, matrix products: 42.2 us -> none  [the longest x3 16.1 us: local(): jnp.einsum('sij,sjc->sic', kernels, col_labels[col_pick], precision=highest)]
    gather x14 -> x0, local copies, waits for them, and re-layouts: 39.3 us -> none  [the longest x4 15.1 us: build_group(): normed_cols[cols_now]]
  transfers between devices with their start and end apart: 8 -> 8, of which waited for: 8 -> 4; matrix products, arithmetic and copies ran while one was open for 3% -> 1% of each run, Pallas kernels for 0% -> 0%
where the time goes in v3:
time: 181 us; the launch traced here: 178 us
  blocking collectives  85.5 us (47%)
  waiting for transfers between devices  43 us (24%)
  starting transfers between devices  25 us (14%)
  Pallas kernels  17.5 us (10%)
  local copies, waits for them, and re-layouts  5.06 us (3%)
    all_to_all x6, blocking collectives, exchange(): return lax.all_to_all(blocks, axes, 0, 0)  85.5 us
    ppermute x1, waiting for transfers between devices, local(): far = lax.ppermute(own, 'zlo', pairs(2, 1))  18 us
    ppermute x3, waiting for transfers between devices, local(): hops = [lax.ppermute(block, 'zhi', pairs(4, step)) for step in (1, 2, 3)]  16.3 us
    all_to_all x2, starting transfers between devices, exchange(): return lax.all_to_all(blocks, axes, 0, 0)  14.9 us
    all_to_all x2, waiting for transfers between devices, exchange(): return lax.all_to_all(blocks, axes, 0, 0)  8.66 us
    ppermute x3, starting transfers between devices, local(): hops = [lax.ppermute(block, 'zhi', pairs(4, step)) for step in (1, 2, 3)]  7.95 us
    pallas_call x1, Pallas kernels, local(): call(build_kernel, (array(BLOCKS, 2 * ROWS, ROWS, dtype=jnp.bfloat16), ar...  7.42 us
    pallas_call x2, Pallas kernels, local(): call(next_kernel, sums_out, [SMEM] + [VMEM] * 4, VMEM, scratch, limit=6)  5.89 us
  transfers between devices with their start and end apart: 8, of which 4 were waited for; matrix products, arithmetic and copies ran while one was open for 1% of the time, Pallas kernels for 0%

profile of v3, /device:TPU:32, one launch (start us, length us, event | category | flops | bytes accessed | tf_op | source)
XLA Modules:
  0.0 177.9 jit_solution(14399026821525310966)
XLA Ops:
  0.0 0.1 stack.46.place_ref
  0.1 0.0 copy-start
  0.1 0.9 copy-done
  1.0 0.0 copy-start.1
  1.0 0.7 copy-done.1
  1.7 0.0 copy-start.3
  1.7 0.7 copy-done.3
  2.3 0.7 shard_map.37
  3.0 1.9 %broadcast_in_dim.13 = bf16[16,136,768]{2,1,0:T(8,128)(2,1)} broadcast(bf16[136,768]{1,0:T(8,128)(2,1)S(1)} %get-tuple-element.24), dimensions={1,2} | broadcast | bytes 3551232 | tf_op jit(solution)/shard_map/broadcast_in_dim | solution.py:216
  5.0 7.0 %all-to-all-start = ((bf16[16,136,768]{2,1,0:T(8,128)(2,1)}), bf16[16,136,768]{2,1,0:T(8,128)(2,1)S(1)}, u32[]{:S(2)}, u32[]{:S(2)}) async-start(bf16[16,136,768]{2,1,0:T(8,128)(2,1)} %broadcast_in_dim.13), calls=%async_computation | async-start | bytes 6684672 | tf_op jit(solution)/shard_map/all_to_all | solution.py:212
  12.0 5.5 %collective-permute-start.2 = (bf16[128,768]{1,0:T(8,128)(2,1)S(1)}, bf16[128,768]{1,0:T(8,128)(2,1)S(1)}, u32[]{:S(2)}, u32[]{:S(2)}) collective-permute-start(bf16[128,768]{1,0:T(8,128)(2,1)S(1)} %get-tuple-element.26), channel_id=1, source_target_pairs={{0,12},{4,8},{8,4},{12,0},{1,13},{5,9},{9,5},{13,1},{2,14},{6,10},... | collective-permute-start | bytes 589832 | tf_op jit(solution)/shard_map/ppermute | solution.py:239
  17.5 1.4 collective-permute-start.1
  18.9 1.0 collective-permute-start
  20.0 14.8 %collective-permute-done.2 = bf16[128,768]{1,0:T(8,128)(2,1)S(1)} collective-permute-done((bf16[128,768]{1,0:T(8,128)(2,1)S(1)}, bf16[128,768]{1,0:T(8,128)(2,1)S(1)}, u32[]{:S(2)}, u32[]{:S(2)}) %collective-permute-start.2) | collective-permute-done | bytes 196640 | tf_op jit(solution)/shard_map/ppermute | solution.py:239
  34.8 0.0 collective-permute-done.1
  34.8 1.5 collective-permute-done
  36.3 1.0 pad_maximum_fusion.own_ref
  37.3 2.1 %collective-permute-start.4 = (bf16[4,128,768]{2,1,0:T(8,128)(2,1)}, bf16[4,128,768]{2,1,0:T(8,128)(2,1)}, u32[]{:S(2)}, u32[]{:S(2)}) collective-permute-start(bf16[4,128,768]{2,1,0:T(8,128)(2,1)} %pad_maximum_fusion.own_ref), channel_id=1, source_target_pairs={{0,128},{128,0},{1,129},{129,1},{2,130},{130,2},{3,131},{131,3},{4... | collective-permute-start | bytes 2359304 | tf_op jit(solution)/shard_map/ppermute | solution.py:243
  39.4 0.0 collective-permute-start.3
  39.5 18.0 %collective-permute-done.4.far_ref = bf16[4,128,768]{2,1,0:T(8,128)(2,1)} collective-permute-done((bf16[4,128,768]{2,1,0:T(8,128)(2,1)}, bf16[4,128,768]{2,1,0:T(8,128)(2,1)}, u32[]{:S(2)}, u32[]{:S(2)}) %collective-permute-start.4) | collective-permute-done | bytes 786464 | tf_op jit(solution)/shard_map/ppermute | solution.py:243
  57.5 0.0 collective-permute-start.5
  57.5 0.0 all-to-all-done.plane_ref
  57.5 0.6 shard_map.38
  58.1 0.7 broadcast_in_dim.14
  58.7 7.8 %all-to-all-start.1 = ((f32[16,8,384]{2,1,0:T(8,128)}), f32[16,8,384]{2,1,0:T(8,128)S(1)}, u32[]{:S(2)}, u32[]{:S(2)}) async-start(f32[16,8,384]{2,1,0:T(8,128)} %broadcast_in_dim.14), calls=%async_computation.1 | async-start | bytes 393216 | tf_op jit(solution)/shard_map/all_to_all | solution.py:212
  66.6 0.0 collective-permute-done.3.mate_ref
  66.6 0.0 collective-permute-done.5.far_mate_ref
  66.6 8.7 %all-to-all-done.1.notes_ref = f32[16,8,384]{2,1,0:T(8,128)S(1)} async-done(((f32[16,8,384]{2,1,0:T(8,128)}), f32[16,8,384]{2,1,0:T(8,128)S(1)}, u32[]{:S(2)}, u32[]{:S(2)}) %all-to-all-start.1) | async-done | bytes 196640 | tf_op jit(solution)/shard_map/all_to_all | solution.py:212
  75.2 7.4 %shard_map.39 = (bf16[256,256,128]{2,1,0:T(8,128)(2,1)S(1)}, s32[8,256]{1,0:T(8,128)S(1)}, f32[16,128]{1,0:T(8,128)S(1)}, s32[16,128]{1,0:T(8,128)S(1)}) custom-call(s32[7]{0:T(128)S(1)} %stack.46.place_ref, f32[16,8,384]{2,1,0:T(8,128)S(1)} %all-to-all-done.1.notes_ref, bf16[16,136,768]{2,1,0:T(8,128)(2,1)S(1)} %all-to-all-done.plane_ref, ...), custom_call_target="tpu_custom_call" | custom-call | tf_op jit(solution)/shard_map/pallas_call | solution.py:250
  82.7 11.8 %all_to_all.40.parts_ref = f32[16,16,128]{2,1,0:T(8,128)S(1)} all-to-all(f32[16,16,128]{2,1,0:T(8,128)S(1)} %broadcast_in_dim.15), channel_id=1, replica_groups=mesh['zlo'=2,'x'=4,'core'=2,'zhi'=4,'y'=4] {'zlo','core','zhi'}, dimensions={0} | all-to-all | bytes 262144 | tf_op jit(solution)/shard_map/all_to_all | solution.py:212
  94.5 2.9 %shard_map.40 = (bf16[16,64,128]{2,1,0:T(8,128)(2,1)S(1)}, f32[16,128]{1,0:T(8,128)S(1)}, f32[1,128]{1,0:T(1,128)S(1)}) custom-call(s32[7]{0:T(128)S(1)} %stack.46.place_ref, s32[8,256]{1,0:T(8,128)S(1)} %get-tuple-element.27.list_ref, bf16[256,256,128]{2,1,0:T(8,128)(2,1)S(1)} %get-tuple-element.28.tiles_ref, s32[16,128]{1,0:T(8,128)S(1)} %get-tuple-element.29.seeds_ref, ...), custom_call_target="tpu_custom_call" | custom-call | tf_op jit(solution)/shard_map/pallas_call | solution.py:275
  97.4 21.4 %all_to_all.41 = bf16[16,64,128]{2,1,0:T(8,128)(2,1)S(1)} all-to-all(bf16[16,64,128]{2,1,0:T(8,128)(2,1)S(1)} %get-tuple-element.32), channel_id=1, replica_groups=mesh['zlo'=2,'x'=4,'core'=2,'zhi'=4,'y'=4] {'x','y'}, dimensions={0} | all-to-all | bytes 524288 | tf_op jit(solution)/shard_map/all_to_all | solution.py:212
  119.0 12.5 %all_to_all.42.smooth_ref = bf16[16,64,128]{2,1,0:T(8,128)(2,1)S(1)} all-to-all(bf16[16,64,128]{2,1,0:T(8,128)(2,1)S(1)} %broadcast_in_dim.16), channel_id=1, replica_groups=mesh['zlo'=2,'x'=4,'core'=2,'zhi'=4,'y'=4] {'zlo','core','zhi'}, dimensions={0} | all-to-all | bytes 524288 | tf_op jit(solution)/shard_map/all_to_all | solution.py:212
  131.5 2.9 %shard_map.41 = bf16[16,64,128]{2,1,0:T(8,128)(2,1)S(1)} custom-call(s32[8,256]{1,0:T(8,128)S(1)} %get-tuple-element.27.list_ref, bf16[256,256,128]{2,1,0:T(8,128)(2,1)S(1)} %get-tuple-element.28.tiles_ref, s32[16,128]{1,0:T(8,128)S(1)} %get-tuple-element.29.seeds_ref, f32[16,128]{1,0:T(8,128)S(1)} %get-tuple-element.31.scale_ref, ...), custom_call_target="tpu_custom_call" | custom-call | tf_op jit(solution)/shard_map/pallas_call | solution.py:286
  134.4 12.6 %all_to_all.43 = bf16[16,64,128]{2,1,0:T(8,128)(2,1)S(1)} all-to-all(bf16[16,64,128]{2,1,0:T(8,128)(2,1)S(1)} %shard_map.41), channel_id=1, replica_groups=mesh['zlo'=2,'x'=4,'core'=2,'zhi'=4,'y'=4] {'x','y'}, dimensions={0} | all-to-all | bytes 524288 | tf_op jit(solution)/shard_map/all_to_all | solution.py:212
  147.2 14.5 %all_to_all.44.smooth_ref = bf16[16,64,128]{2,1,0:T(8,128)(2,1)S(1)} all-to-all(bf16[16,64,128]{2,1,0:T(8,128)(2,1)S(1)} %broadcast_in_dim.17), channel_id=1, replica_groups=mesh['zlo'=2,'x'=4,'core'=2,'zhi'=4,'y'=4] {'zlo','core','zhi'}, dimensions={0} | all-to-all | bytes 524288 | tf_op jit(solution)/shard_map/all_to_all | solution.py:212
  161.7 0.0 copy-start.2
  161.7 2.9 %shard_map.42 = bf16[16,64,128]{2,1,0:T(8,128)(2,1)S(1)} custom-call(s32[8,256]{1,0:T(8,128)S(1)} %get-tuple-element.27.list_ref, bf16[256,256,128]{2,1,0:T(8,128)(2,1)S(1)} %get-tuple-element.28.tiles_ref, s32[16,128]{1,0:T(8,128)S(1)} %get-tuple-element.29.seeds_ref, f32[16,128]{1,0:T(8,128)S(1)} %get-tuple-element.31.scale_ref, ...), custom_call_target="tpu_custom_call" | custom-call | tf_op jit(solution)/shard_map/pallas_call | solution.py:286
  164.7 12.6 %all_to_all.45 = bf16[16,64,128]{2,1,0:T(8,128)(2,1)S(1)} all-to-all(bf16[16,64,128]{2,1,0:T(8,128)(2,1)S(1)} %shard_map.42), channel_id=1, replica_groups=mesh['zlo'=2,'x'=4,'core'=2,'zhi'=4,'y'=4] {'x','y'}, dimensions={0} | all-to-all | bytes 524288 | tf_op jit(solution)/shard_map/all_to_all | solution.py:212
  177.3 0.0 copy-done.2
  177.3 0.6 fusion
  (11 shorter events, 0.2 us)
Async XLA Ops:
  0.1 0.9 copy-start
  1.0 0.7 copy-start.1
  1.7 0.7 copy-start.3
  5.0 52.5 %all-to-all-start = ((bf16[16,136,768]{2,1,0:T(8,128)(2,1)}), bf16[16,136,768]{2,1,0:T(8,128)(2,1)S(1)}, u32[]{:S(2)}, u32[]{:S(2)}) async-start(bf16[16,136,768]{2,1,0:T(8,128)(2,1)} %broadcast_in_dim.13), calls=%async_computation | async-start | bytes 6684672 | tf_op jit(solution)/shard_map/all_to_all | solution.py:212
  12.0 22.8 %collective-permute-start.2 = (bf16[128,768]{1,0:T(8,128)(2,1)S(1)}, bf16[128,768]{1,0:T(8,128)(2,1)S(1)}, u32[]{:S(2)}, u32[]{:S(2)}) collective-permute-start(bf16[128,768]{1,0:T(8,128)(2,1)S(1)} %get-tuple-element.26), channel_id=1, source_target_pairs={{0,12},{4,8},{8,4},{12,0},{1,13},{5,9},{9,5},{13,1},{2,14},{6,10},... | collective-permute-start | bytes 589832 | tf_op jit(solution)/shard_map/ppermute | solution.py:239
  17.5 17.3 %collective-permute-start.1 = (bf16[128,768]{1,0:T(8,128)(2,1)S(1)}, bf16[128,768]{1,0:T(8,128)(2,1)S(1)}, u32[]{:S(2)}, u32[]{:S(2)}) collective-permute-start(bf16[128,768]{1,0:T(8,128)(2,1)S(1)} %get-tuple-element.26), channel_id=1, source_target_pairs={{0,8},{4,12},{8,0},{12,4},{1,9},{5,13},{9,1},{13,5},{2,10},{6,14},... | collective-permute-start | bytes 589832 | tf_op jit(solution)/shard_map/ppermute | solution.py:239
  18.9 17.4 %collective-permute-start = (bf16[128,768]{1,0:T(8,128)(2,1)S(1)}, bf16[128,768]{1,0:T(8,128)(2,1)S(1)}, u32[]{:S(2)}, u32[]{:S(2)}) collective-permute-start(bf16[128,768]{1,0:T(8,128)(2,1)S(1)} %get-tuple-element.26), channel_id=1, source_target_pairs={{0,4},{4,0},{8,12},{12,8},{1,5},{5,1},{9,13},{13,9},{2,6},{6,2},{1... | collective-permute-start | bytes 589832 | tf_op jit(solution)/shard_map/ppermute | solution.py:239
  37.3 20.2 %collective-permute-start.4 = (bf16[4,128,768]{2,1,0:T(8,128)(2,1)}, bf16[4,128,768]{2,1,0:T(8,128)(2,1)}, u32[]{:S(2)}, u32[]{:S(2)}) collective-permute-start(bf16[4,128,768]{2,1,0:T(8,128)(2,1)} %pad_maximum_fusion.own_ref), channel_id=1, source_target_pairs={{0,128},{128,0},{1,129},{129,1},{2,130},{130,2},{3,131},{131,3},{4... | collective-permute-start | bytes 2359304 | tf_op jit(solution)/shard_map/ppermute | solution.py:243
  39.4 27.1 %collective-permute-start.3 = (bf16[4,128,768]{2,1,0:T(8,128)(2,1)}, bf16[4,128,768]{2,1,0:T(8,128)(2,1)}, u32[]{:S(2)}, u32[]{:S(2)}) collective-permute-start(bf16[4,128,768]{2,1,0:T(8,128)(2,1)} %pad_maximum_fusion.own_ref), channel_id=1, source_target_pairs={{0,16},{16,0},{1,17},{17,1},{2,18},{18,2},{3,19},{19,3},{4,20},{20... | collective-permute-start | bytes 2359304 | tf_op jit(solution)/shard_map/ppermute | solution.py:242
  57.5 9.1 %collective-permute-start.5 = (bf16[4,128,768]{2,1,0:T(8,128)(2,1)}, bf16[4,128,768]{2,1,0:T(8,128)(2,1)}, u32[]{:S(2)}, u32[]{:S(2)}) collective-permute-start(bf16[4,128,768]{2,1,0:T(8,128)(2,1)} %collective-permute-done.4.far_ref), channel_id=1, source_target_pairs={{0,16},{16,0},{1,17},{17,1},{2,18},{18,2},{3,19},{19,3},{4,20},{20... | collective-permute-start | bytes 2359304 | tf_op jit(solution)/shard_map/ppermute | solution.py:248
  58.7 16.5 %all-to-all-start.1 = ((f32[16,8,384]{2,1,0:T(8,128)}), f32[16,8,384]{2,1,0:T(8,128)S(1)}, u32[]{:S(2)}, u32[]{:S(2)}) async-start(f32[16,8,384]{2,1,0:T(8,128)} %broadcast_in_dim.14), calls=%async_computation.1 | async-start | bytes 393216 | tf_op jit(solution)/shard_map/all_to_all | solution.py:212
  161.7 15.6 %copy-start.2 = (s32[128]{0:T(128)S(1)}, s32[128]{0:T(128)}, u32[]{:S(2)}) copy-start(s32[128]{0:T(128)} %param.5) | copy-start | bytes 1540

commit v4 on v3

--- a/solution.py
+++ b/solution.py
@@ -5,6 +5,7 @@
 from jax.experimental.pallas import tpu as pltpu
 from jax.sharding import Mesh
 from jax.sharding import PartitionSpec as P
+
 
 CLASSES = 64
 BLEND = 0.8
@@ -26,7 +27,17 @@
 ANY = pl.BlockSpec(memory_space=pl.ANY)
 
 
-def prep_kernel(place_ref, emb_ref, slots_ref, seeds_ref, block_ref, noted_ref, seeds_out):
+def prep_kernel(place_ref, emb_hbm, slots_hbm, seeds_hbm, block_ref, noted_ref, seeds_out,
+                emb_ref, slots_ref, seeds_ref, emb_sem, slots_sem, seeds_sem):
+    copies = [
+        pltpu.make_async_copy(emb_hbm, emb_ref, emb_sem),
+        pltpu.make_async_copy(slots_hbm, slots_ref, slots_sem),
+        pltpu.make_async_copy(seeds_hbm, seeds_ref, seeds_sem),
+    ]
+    for copy in copies:
+        copy.start()
+    for copy in copies:
+        copy.wait()
     features = emb_ref[...].astype(jnp.float32)
     norm = lax.rsqrt(jnp.sum(features * features, axis=1, keepdims=True) + EPSILON)
     normed = (features * norm).astype(jnp.bfloat16)
@@ -231,12 +242,20 @@
             array(ROWS + EXTRA, FEAT, dtype=jnp.bfloat16),
             array(1, ROWS),
         ),
-        [SMEM] + [VMEM] * 3,
+        [SMEM] + [ANY] * 3,
         (VMEM,) * 3,
-        limit=4,
+        (
+            pltpu.VMEM((ROWS, FEAT), jnp.bfloat16),
+            pltpu.VMEM((2, 32), jnp.int32),
+            pltpu.VMEM((1, ROWS), jnp.int32),
+        )
+        + (pltpu.SemaphoreType.DMA,) * 3,
+        limit=62,
     )(place, embeddings, tile_list.reshape(-1, 2).T, seeds[None, :])
 
-    hops = [lax.ppermute(block, "zhi", pairs(4, step)) for step in (1, 2, 3)]
+    hops = []
+    for step in (1, 2, 3):
+        hops.append(lax.ppermute(block, "zhi", pairs(4, step)))
     plane = gather(noted, PLANE)
     own = jnp.stack([block] + hops)
     mate = lax.ppermute(own, "core", pairs(2, 1))
@@ -245,6 +264,7 @@
         relay_kernel, array(EXTRA, BLOCKS + ROWS), [SMEM, VMEM, VMEM], VMEM, limit=4
     )(place, plane, own_seeds)
     notes = gather(note, LINE)
+    far, notes = lax.optimization_barrier((far, notes))
     far_mate = lax.ppermute(far, "core", pairs(2, 1))
 
     tiles, listing, partial_degree, line_seeds = call(

time: 181 us -> 186 us (1.028)
  blocking collectives: 85.5 us -> 89.9 us
  starting transfers between devices: 25 us -> 27 us
    ppermute x1, waiting for transfers between devices: 18 us -> 0.01 us  [local(): far = lax.ppermute(own, 'zlo', pairs(2, 1))]
    all_to_all x2, waiting for transfers between devices: 8.66 us -> 25.8 us  [exchange(): return lax.all_to_all(blocks, axes, 0, 0)]
    all_to_all x6, blocking collectives: 85.5 us -> 89.9 us  [exchange(): return lax.all_to_all(blocks, axes, 0, 0)]
    unnamed x8, local copies, waits for them, and re-layouts: 2.26 us -> 0.01 us
    ppermute x1, waiting for transfers between devices: 0.01 us -> 2.12 us  [local(): far_mate = lax.ppermute(far, 'core', pairs(2, 1))]
  transfers between devices with their start and end apart: 8 -> 8, of which waited for: 4 -> 5; matrix products, arithmetic and copies ran while one was open for 1% -> 1% of each run, Pallas kernels for 0% -> 0%
where the time goes in v4:
time: 186 us; the launch traced here: 183 us
  blocking collectives  89.9 us (48%)
  waiting for transfers between devices  44.3 us (24%)
  starting transfers between devices  27 us (15%)
  Pallas kernels  16.1 us (9%)
  local copies, waits for them, and re-layouts  4.24 us (2%)
    all_to_all x6, blocking collectives, exchange(): return lax.all_to_all(blocks, axes, 0, 0)  89.9 us
    all_to_all x2, waiting for transfers between devices, exchange(): return lax.all_to_all(blocks, axes, 0, 0)  25.8 us
    ppermute x3, waiting for transfers between devices, local(): hops.append(lax.ppermute(block, 'zhi', pairs(4, step)))  16.3 us
    all_to_all x2, starting transfers between devices, exchange(): return lax.all_to_all(blocks, axes, 0, 0)  15.8 us
    ppermute x3, starting transfers between devices, local(): hops.append(lax.ppermute(block, 'zhi', pairs(4, step)))  7.95 us
    pallas_call x1, Pallas kernels, local(): call(build_kernel, (array(BLOCKS, 2 * ROWS, ROWS, dtype=jnp.bfloat16), ar...  5.95 us
    pallas_call x2, Pallas kernels, local(): call(next_kernel, sums_out, [SMEM] + [VMEM] * 4, VMEM, scratch, limit=6)  4.71 us
  transfers between devices with their start and end apart: 8, of which 5 were waited for; matrix products, arithmetic and copies ran while one was open for 1% of the time, Pallas kernels for 0%

profile of v4, /device:TPU:32, one launch (start us, length us, event | category | flops | bytes accessed | tf_op | source)
XLA Modules:
  0.0 183.4 jit_solution(16173419847080674104)
XLA Ops:
  0.0 0.6 stack.46.place_ref
  0.6 2.5 %shard_map.37 = (bf16[128,768]{1,0:T(8,128)(2,1)}, bf16[136,768]{1,0:T(8,128)(2,1)}, f32[1,128]{1,0:T(1,128)}) custom-call(s32[7]{0:T(128)} %stack.46.place_ref, bf16[128,768]{1,0:T(8,128)(2,1)} %emb_hbm.1, s32[2,32]{1,0:T(2,128)} %bitcast.30, s32[1,128]{1,0:T(1,128)} %bitcast.29), custom_call_target="tpu_custom_call" | custom-call | tf_op jit(solution)/shard_map/pallas_call | solution.py:238
  3.1 2.9 %broadcast_in_dim.13 = bf16[16,136,768]{2,1,0:T(8,128)(2,1)} broadcast(bf16[136,768]{1,0:T(8,128)(2,1)} %get-tuple-element.27), dimensions={1,2} | broadcast | bytes 3551232 | tf_op jit(solution)/shard_map/broadcast_in_dim | solution.py:227
  6.0 0.0 copy-start.2
  6.0 0.0 copy-start
  6.0 0.0 copy-start.1
  6.0 7.2 %all-to-all-start = ((bf16[16,136,768]{2,1,0:T(8,128)(2,1)}), bf16[16,136,768]{2,1,0:T(8,128)(2,1)S(1)}, u32[]{:S(2)}, u32[]{:S(2)}) async-start(bf16[16,136,768]{2,1,0:T(8,128)(2,1)} %broadcast_in_dim.13), calls=%async_computation | async-start | bytes 6684672 | tf_op jit(solution)/shard_map/all_to_all | solution.py:223
  13.2 0.0 copy-done.2
  13.2 5.5 %collective-permute-start.2 = (bf16[128,768]{1,0:T(8,128)(2,1)S(1)}, bf16[128,768]{1,0:T(8,128)(2,1)S(1)}, u32[]{:S(2)}, u32[]{:S(2)}) collective-permute-start(bf16[128,768]{1,0:T(8,128)(2,1)S(1)} %copy-done.2), channel_id=1, source_target_pairs={{0,12},{4,8},{8,4},{12,0},{1,13},{5,9},{9,5},{13,1},{2,14},{6,10},... | collective-permute-start | bytes 589832 | tf_op jit(solution)/shard_map/ppermute | solution.py:258
  18.7 1.4 collective-permute-start.1
  20.1 1.0 collective-permute-start
  21.1 14.8 %collective-permute-done.2 = bf16[128,768]{1,0:T(8,128)(2,1)S(1)} collective-permute-done((bf16[128,768]{1,0:T(8,128)(2,1)S(1)}, bf16[128,768]{1,0:T(8,128)(2,1)S(1)}, u32[]{:S(2)}, u32[]{:S(2)}) %collective-permute-start.2) | collective-permute-done | bytes 196640 | tf_op jit(solution)/shard_map/ppermute | solution.py:258
  35.9 0.0 collective-permute-done.1
  35.9 1.5 collective-permute-done
  37.5 1.0 pad_maximum_fusion.own_ref
  38.5 2.1 %collective-permute-start.3 = (bf16[4,128,768]{2,1,0:T(8,128)(2,1)}, bf16[4,128,768]{2,1,0:T(8,128)(2,1)}, u32[]{:S(2)}, u32[]{:S(2)}) collective-permute-start(bf16[4,128,768]{2,1,0:T(8,128)(2,1)} %pad_maximum_fusion.own_ref), channel_id=1, source_target_pairs={{0,128},{128,0},{1,129},{129,1},{2,130},{130,2},{3,131},{131,3},{4... | collective-permute-start | bytes 2359304 | tf_op jit(solution)/shard_map/ppermute | solution.py:262
  40.6 17.3 %all-to-all-done.plane_ref = bf16[16,136,768]{2,1,0:T(8,128)(2,1)S(1)} async-done(((bf16[16,136,768]{2,1,0:T(8,128)(2,1)}), bf16[16,136,768]{2,1,0:T(8,128)(2,1)S(1)}, u32[]{:S(2)}, u32[]{:S(2)}) %all-to-all-start) | async-done | bytes 3342368 | tf_op jit(solution)/shard_map/all_to_all | solution.py:223
  57.9 0.0 copy-done
  57.9 0.0 copy-done.1
  57.9 0.6 shard_map.38
  58.4 0.7 broadcast_in_dim.14
  59.1 8.6 %all-to-all-start.1 = ((f32[16,8,384]{2,1,0:T(8,128)}), f32[16,8,384]{2,1,0:T(8,128)S(1)}, u32[]{:S(2)}, u32[]{:S(2)}) async-start(f32[16,8,384]{2,1,0:T(8,128)} %broadcast_in_dim.14), calls=%async_computation.1 | async-start | bytes 393216 | tf_op jit(solution)/shard_map/all_to_all | solution.py:223
  67.7 0.1 collective-permute-start.4
  67.8 0.0 collective-permute-done.3.far_ref
  67.8 8.6 %all-to-all-done.1.notes_ref = f32[16,8,384]{2,1,0:T(8,128)S(1)} async-done(((f32[16,8,384]{2,1,0:T(8,128)}), f32[16,8,384]{2,1,0:T(8,128)S(1)}, u32[]{:S(2)}, u32[]{:S(2)}) %all-to-all-start.1) | async-done | bytes 196640 | tf_op jit(solution)/shard_map/all_to_all | solution.py:223
  76.4 1.0 collective-permute-start.5
  77.4 0.0 collective-permute-done.4.mate_ref
  77.4 2.1 %collective-permute-done.5.far_mate_ref = bf16[4,128,768]{2,1,0:T(8,128)(2,1)S(1)} collective-permute-done((bf16[4,128,768]{2,1,0:T(8,128)(2,1)}, bf16[4,128,768]{2,1,0:T(8,128)(2,1)S(1)}, u32[]{:S(2)}, u32[]{:S(2)}) %collective-permute-start.5) | collective-permute-done | bytes 786464 | tf_op jit(solution)/shard_map/ppermute | solution.py:268
  79.5 5.9 %shard_map.39 = (bf16[256,256,128]{2,1,0:T(8,128)(2,1)S(1)}, s32[8,256]{1,0:T(8,128)S(1)}, f32[16,128]{1,0:T(8,128)S(1)}, s32[16,128]{1,0:T(8,128)S(1)}) custom-call(s32[7]{0:T(128)S(1)} %copy-done, f32[16,8,384]{2,1,0:T(8,128)S(1)} %all-to-all-done.1.notes_ref, bf16[16,136,768]{2,1,0:T(8,128)(2,1)S(1)} %all-to-all-done.plane_ref, ...), custom_call_target="tpu_custom_call" | custom-call | tf_op jit(solution)/shard_map/pallas_call | solution.py:270
  85.5 13.2 %all_to_all.40.parts_ref = f32[16,16,128]{2,1,0:T(8,128)S(1)} all-to-all(f32[16,16,128]{2,1,0:T(8,128)S(1)} %broadcast_in_dim.15), channel_id=1, replica_groups=mesh['zlo'=2,'x'=4,'core'=2,'zhi'=4,'y'=4] {'zlo','core','zhi'}, dimensions={0} | all-to-all | bytes 262144 | tf_op jit(solution)/shard_map/all_to_all | solution.py:223
  98.7 2.3 %shard_map.40 = (bf16[16,64,128]{2,1,0:T(8,128)(2,1)S(1)}, f32[16,128]{1,0:T(8,128)S(1)}, f32[1,128]{1,0:T(1,128)S(1)}) custom-call(s32[7]{0:T(128)S(1)} %copy-done, s32[8,256]{1,0:T(8,128)S(1)} %get-tuple-element.31.list_ref, bf16[256,256,128]{2,1,0:T(8,128)(2,1)S(1)} %get-tuple-element.32.tiles_ref, s32[16,128]{1,0:T(8,128)S(1)} %get-tuple-element.33.seeds_ref, ...), custom_call_target="tpu_custom_call" | custom-call | tf_op jit(solution)/shard_map/pallas_call | solution.py:295
  101.0 22.0 %all_to_all.41 = bf16[16,64,128]{2,1,0:T(8,128)(2,1)S(1)} all-to-all(bf16[16,64,128]{2,1,0:T(8,128)(2,1)S(1)} %get-tuple-element.36), channel_id=1, replica_groups=mesh['zlo'=2,'x'=4,'core'=2,'zhi'=4,'y'=4] {'x','y'}, dimensions={0} | all-to-all | bytes 524288 | tf_op jit(solution)/shard_map/all_to_all | solution.py:223
  123.1 12.9 %all_to_all.42.smooth_ref = bf16[16,64,128]{2,1,0:T(8,128)(2,1)S(1)} all-to-all(bf16[16,64,128]{2,1,0:T(8,128)(2,1)S(1)} %broadcast_in_dim.16), channel_id=1, replica_groups=mesh['zlo'=2,'x'=4,'core'=2,'zhi'=4,'y'=4] {'zlo','core','zhi'}, dimensions={0} | all-to-all | bytes 524288 | tf_op jit(solution)/shard_map/all_to_all | solution.py:223
  136.0 2.4 %shard_map.41 = bf16[16,64,128]{2,1,0:T(8,128)(2,1)S(1)} custom-call(s32[8,256]{1,0:T(8,128)S(1)} %get-tuple-element.31.list_ref, bf16[256,256,128]{2,1,0:T(8,128)(2,1)S(1)} %get-tuple-element.32.tiles_ref, s32[16,128]{1,0:T(8,128)S(1)} %get-tuple-element.33.seeds_ref, f32[16,128]{1,0:T(8,128)S(1)} %get-tuple-element.35.scale_ref, ...), custom_call_target="tpu_custom_call" | custom-call | tf_op jit(solution)/shard_map/pallas_call | solution.py:306
  138.4 13.5 %all_to_all.43 = bf16[16,64,128]{2,1,0:T(8,128)(2,1)S(1)} all-to-all(bf16[16,64,128]{2,1,0:T(8,128)(2,1)S(1)} %shard_map.41), channel_id=1, replica_groups=mesh['zlo'=2,'x'=4,'core'=2,'zhi'=4,'y'=4] {'x','y'}, dimensions={0} | all-to-all | bytes 524288 | tf_op jit(solution)/shard_map/all_to_all | solution.py:223
  152.0 14.8 %all_to_all.44.smooth_ref = bf16[16,64,128]{2,1,0:T(8,128)(2,1)S(1)} all-to-all(bf16[16,64,128]{2,1,0:T(8,128)(2,1)S(1)} %broadcast_in_dim.17), channel_id=1, replica_groups=mesh['zlo'=2,'x'=4,'core'=2,'zhi'=4,'y'=4] {'zlo','core','zhi'}, dimensions={0} | all-to-all | bytes 524288 | tf_op jit(solution)/shard_map/all_to_all | solution.py:223
  166.8 0.0 copy-start.3
  166.8 2.4 %shard_map.42 = bf16[16,64,128]{2,1,0:T(8,128)(2,1)S(1)} custom-call(s32[8,256]{1,0:T(8,128)S(1)} %get-tuple-element.31.list_ref, bf16[256,256,128]{2,1,0:T(8,128)(2,1)S(1)} %get-tuple-element.32.tiles_ref, s32[16,128]{1,0:T(8,128)S(1)} %get-tuple-element.33.seeds_ref, f32[16,128]{1,0:T(8,128)S(1)} %get-tuple-element.35.scale_ref, ...), custom_call_target="tpu_custom_call" | custom-call | tf_op jit(solution)/shard_map/pallas_call | solution.py:306
  169.1 13.6 %all_to_all.45 = bf16[16,64,128]{2,1,0:T(8,128)(2,1)S(1)} all-to-all(bf16[16,64,128]{2,1,0:T(8,128)(2,1)S(1)} %shard_map.42), channel_id=1, replica_groups=mesh['zlo'=2,'x'=4,'core'=2,'zhi'=4,'y'=4] {'x','y'}, dimensions={0} | all-to-all | bytes 524288 | tf_op jit(solution)/shard_map/all_to_all | solution.py:223
  182.8 0.0 copy-done.3
  182.8 0.6 fusion
  (11 shorter events, 0.2 us)
Async XLA Ops:
  6.0 7.2 %copy-start.2 = (bf16[128,768]{1,0:T(8,128)(2,1)S(1)}, bf16[128,768]{1,0:T(8,128)(2,1)}, u32[]{:S(2)}) copy-start(bf16[128,768]{1,0:T(8,128)(2,1)} %get-tuple-element.26) | copy-start | bytes 589828
  6.0 51.9 %copy-start = (s32[7]{0:T(128)S(1)}, s32[7]{0:T(128)}, u32[]{:S(2)}) copy-start(s32[7]{0:T(128)} %stack.46.place_ref) | copy-start | bytes 88
  6.0 51.9 %copy-start.1 = (f32[1,128]{1,0:T(1,128)S(1)}, f32[1,128]{1,0:T(1,128)}, u32[]{:S(2)}) copy-start(f32[1,128]{1,0:T(1,128)} %get-tuple-element.28.seeds_ref) | copy-start | bytes 1540
  6.0 51.9 %all-to-all-start = ((bf16[16,136,768]{2,1,0:T(8,128)(2,1)}), bf16[16,136,768]{2,1,0:T(8,128)(2,1)S(1)}, u32[]{:S(2)}, u32[]{:S(2)}) async-start(bf16[16,136,768]{2,1,0:T(8,128)(2,1)} %broadcast_in_dim.13), calls=%async_computation | async-start | bytes 6684672 | tf_op jit(solution)/shard_map/all_to_all | solution.py:223
  13.2 22.8 %collective-permute-start.2 = (bf16[128,768]{1,0:T(8,128)(2,1)S(1)}, bf16[128,768]{1,0:T(8,128)(2,1)S(1)}, u32[]{:S(2)}, u32[]{:S(2)}) collective-permute-start(bf16[128,768]{1,0:T(8,128)(2,1)S(1)} %copy-done.2), channel_id=1, source_target_pairs={{0,12},{4,8},{8,4},{12,0},{1,13},{5,9},{9,5},{13,1},{2,14},{6,10},... | collective-permute-start | bytes 589832 | tf_op jit(solution)/shard_map/ppermute | solution.py:258
  18.7 17.3 %collective-permute-start.1 = (bf16[128,768]{1,0:T(8,128)(2,1)S(1)}, bf16[128,768]{1,0:T(8,128)(2,1)S(1)}, u32[]{:S(2)}, u32[]{:S(2)}) collective-permute-start(bf16[128,768]{1,0:T(8,128)(2,1)S(1)} %copy-done.2), channel_id=1, source_target_pairs={{0,8},{4,12},{8,0},{12,4},{1,9},{5,13},{9,1},{13,5},{2,10},{6,14},... | collective-permute-start | bytes 589832 | tf_op jit(solution)/shard_map/ppermute | solution.py:258
  20.1 17.4 %collective-permute-start = (bf16[128,768]{1,0:T(8,128)(2,1)S(1)}, bf16[128,768]{1,0:T(8,128)(2,1)S(1)}, u32[]{:S(2)}, u32[]{:S(2)}) collective-permute-start(bf16[128,768]{1,0:T(8,128)(2,1)S(1)} %copy-done.2), channel_id=1, source_target_pairs={{0,4},{4,0},{8,12},{12,8},{1,5},{5,1},{9,13},{13,9},{2,6},{6,2},{1... | collective-permute-start | bytes 589832 | tf_op jit(solution)/shard_map/ppermute | solution.py:258
  38.5 29.4 %collective-permute-start.3 = (bf16[4,128,768]{2,1,0:T(8,128)(2,1)}, bf16[4,128,768]{2,1,0:T(8,128)(2,1)}, u32[]{:S(2)}, u32[]{:S(2)}) collective-permute-start(bf16[4,128,768]{2,1,0:T(8,128)(2,1)} %pad_maximum_fusion.own_ref), channel_id=1, source_target_pairs={{0,128},{128,0},{1,129},{129,1},{2,130},{130,2},{3,131},{131,3},{4... | collective-permute-start | bytes 2359304 | tf_op jit(solution)/shard_map/ppermute | solution.py:262
  59.1 17.3 %all-to-all-start.1 = ((f32[16,8,384]{2,1,0:T(8,128)}), f32[16,8,384]{2,1,0:T(8,128)S(1)}, u32[]{:S(2)}, u32[]{:S(2)}) async-start(f32[16,8,384]{2,1,0:T(8,128)} %broadcast_in_dim.14), calls=%async_computation.1 | async-start | bytes 393216 | tf_op jit(solution)/shard_map/all_to_all | solution.py:223
  67.7 9.7 %collective-permute-start.4 = (bf16[4,128,768]{2,1,0:T(8,128)(2,1)}, bf16[4,128,768]{2,1,0:T(8,128)(2,1)}, u32[]{:S(2)}, u32[]{:S(2)}) collective-permute-start(bf16[4,128,768]{2,1,0:T(8,128)(2,1)} %pad_maximum_fusion.own_ref), channel_id=1, source_target_pairs={{0,16},{16,0},{1,17},{17,1},{2,18},{18,2},{3,19},{19,3},{4,20},{20... | collective-permute-start | bytes 2359304 | tf_op jit(solution)/shard_map/ppermute | solution.py:261
  76.4 3.1 %collective-permute-start.5 = (bf16[4,128,768]{2,1,0:T(8,128)(2,1)}, bf16[4,128,768]{2,1,0:T(8,128)(2,1)S(1)}, u32[]{:S(2)}, u32[]{:S(2)}) collective-permute-start(bf16[4,128,768]{2,1,0:T(8,128)(2,1)} %collective-permute-done.3.far_ref), channel_id=1, source_target_pairs={{0,16},{16,0},{1,17},{17,1},{2,18},{18,2},{3,19},{19,3},{4,20},{20... | collective-permute-start | bytes 2359304 | tf_op jit(solution)/shard_map/ppermute | solution.py:268
  166.8 16.0 %copy-start.3 = (s32[128]{0:T(128)S(1)}, s32[128]{0:T(128)}, u32[]{:S(2)}) copy-start(s32[128]{0:T(128)} %param.5) | copy-start | bytes 1540

commit v5 on v3

--- a/solution.py
+++ b/solution.py
@@ -26,12 +26,18 @@
 ANY = pl.BlockSpec(memory_space=pl.ANY)
 
 
-def prep_kernel(place_ref, emb_ref, slots_ref, seeds_ref, block_ref, noted_ref, seeds_out):
+def prep_kernel(emb_hbm, slots_hbm, block_ref, bits_ref, emb_ref, slots_ref, emb_sem, slots_sem):
+    copies = [
+        pltpu.make_async_copy(emb_hbm, emb_ref, emb_sem),
+        pltpu.make_async_copy(slots_hbm, slots_ref, slots_sem),
+    ]
+    for copy in copies:
+        copy.start()
+    for copy in copies:
+        copy.wait()
     features = emb_ref[...].astype(jnp.float32)
     norm = lax.rsqrt(jnp.sum(features * features, axis=1, keepdims=True) + EPSILON)
-    normed = (features * norm).astype(jnp.bfloat16)
-    block_ref[...] = normed
-    noted_ref[:ROWS, :] = normed
+    block_ref[...] = (features * norm).astype(jnp.bfloat16)
     first, second = slots_ref[0:1, :], slots_ref[1:2, :]
     ids = jnp.where(first >= 0, first * GROUP + second, -1)
     hits = (lax.broadcasted_iota(jnp.int32, (BLOCKS, 32), 0) == ids).astype(jnp.float32)
@@ -39,41 +45,24 @@
         jnp.ones((EXTRA, 32), jnp.float32), hits, (((1,), (1,)), ((), ())),
         preferred_element_type=jnp.float32,
     )
-    noted_ref[ROWS:, :BLOCKS] = bits.astype(jnp.bfloat16)
-    noted_ref[ROWS:, BLOCKS:] = jnp.zeros((EXTRA, FEAT - BLOCKS), jnp.bfloat16)
-    seeds_out[...] = seeds_ref[...].astype(jnp.float32)
-
-
-def relay_kernel(place_ref, plane_ref, seeds_ref, out_ref):
-    x, y = place_ref[0], place_ref[1]
-    row = lax.broadcasted_iota(jnp.int32, (EXTRA, BLOCKS), 0)
-    passed = jnp.zeros((EXTRA, BLOCKS), jnp.float32)
-    for k in range(4):
-        for at, line in ((k * 4 + y, k), (x * 4 + k, 4 + k)):
-            note = plane_ref[at, ROWS:, :BLOCKS].astype(jnp.float32)
-            passed = jnp.where(row == line, note, passed)
-    out_ref[:, :BLOCKS] = passed
-    out_ref[:, BLOCKS:] = jnp.broadcast_to(seeds_ref[...], (EXTRA, ROWS))
-
-
-def make_list(place_ref, notes_ref, list_v):
+    bits_ref[...] = bits[0:1]
+
+
+def make_list(place_ref, ahead_ref, back_ref, list_v):
     x, y, zlo, core, zhi = (place_ref[k] for k in range(5))
     shape = (BLOCKS, BLOCKS)
     row = lax.broadcasted_iota(jnp.int32, shape, 0)
     lane = lax.broadcasted_iota(jnp.int32, shape, 1)
-    u_zhi, u_x = row >> 6, (row >> 4) & 3
-    v_zlo, v_core, v_y = (row >> 3) & 1, (row >> 2) & 1, row & 3
+    u_zhi, u_x = (row >> 6) ^ zhi, ((row >> 4) & 3) ^ x
+    v_zlo, v_core, v_y = ((row >> 3) & 1) ^ zlo, ((row >> 2) & 1) ^ core, (row & 3) ^ y
     a_zhi, a_y = lane >> 6, (lane >> 4) & 3
     b_zlo, b_x, b_core = (lane >> 3) & 1, (lane >> 1) & 3, lane & 1
     forward = (a_zhi == zhi) & (b_x == x) & (a_y == v_y) & (b_zlo == v_zlo) & (b_core == v_core)
     mirror = (a_zhi == u_zhi) & (a_y == y) & (b_zlo == zlo) & (b_x == u_x) & (b_core == core)
-    ahead = []
-    for u in range(GROUP):
-        note = notes_ref[zlo * 8 + core * 4 + u // 4, u % 4 : u % 4 + 1, :BLOCKS]
-        ahead.append(jnp.broadcast_to(note, (GROUP, BLOCKS)))
-    back = [notes_ref[at * 4 + zhi, 4:8, :BLOCKS] for at in range(4)]
-    ahead = jnp.concatenate(ahead, axis=0)
-    back = jnp.concatenate(back * GROUP, axis=0)
+    ahead = jnp.concatenate(
+        [jnp.broadcast_to(ahead_ref[u : u + 1, :], (GROUP, BLOCKS)) for u in range(GROUP)], axis=0
+    )
+    back = jnp.concatenate([back_ref[...]] * GROUP, axis=0)
     hits = jnp.where(forward, ahead, 0.0) + jnp.where(mirror, back, 0.0)
     counts = jnp.dot(
         hits.astype(jnp.bfloat16), jnp.ones(shape, jnp.bfloat16), preferred_element_type=jnp.float32
@@ -88,7 +77,8 @@
     code = (
         (((slot_lane >> 4) & 3) * 4 + (slot_lane & 3)) * GROUP
         + ((slot_lane >> 3) & 1) * 8 + ((slot_lane >> 2) & 1) * 4 + (slot_lane >> 6)
-    ).astype(jnp.float32).astype(jnp.bfloat16)
+    )
+    code = (code ^ ((x * 4 + y) * GROUP + place_ref[5])).astype(jnp.float32).astype(jnp.bfloat16)
     ones = jnp.ones((EXTRA, BLOCKS), jnp.bfloat16)
     codes = jnp.dot(code, spot.astype(jnp.bfloat16), preferred_element_type=jnp.float32)
     weights = jnp.dot(ones, (spot * counts).astype(jnp.bfloat16), preferred_element_type=jnp.float32)
@@ -98,8 +88,8 @@
     list_v[...] = (table + 0.5).astype(jnp.int32)
 
 
-def build_kernel(place_ref, notes_ref, plane_ref, own_ref, mate_ref, far_ref, far_mate_ref,
-                 tiles_ref, list_ref, deg_ref, seeds_ref, line_v, sums, list_v, list_sem, line_sem):
+def build_kernel(place_ref, ahead_ref, back_ref, seeds_ref, plane_ref, own_ref, mate_ref, far_ref, far_mate_ref,
+                 tiles_ref, list_ref, deg_ref, line_v, sums, list_v, list_sem, line_sem):
     mine = place_ref[5]
     parts = [
         pltpu.make_async_copy(part, line_v.at[pl.ds(at * 4, 4)], line_sem)
@@ -107,11 +97,9 @@
     ]
     for part in parts:
         part.start()
-    make_list(place_ref, notes_ref, list_v)
+    make_list(place_ref, ahead_ref, back_ref, list_v)
     list_copy = pltpu.make_async_copy(list_v, list_ref, list_sem)
     list_copy.start()
-    for b in range(GROUP):
-        seeds_ref[b : b + 1, :] = notes_ref[b, 0:1, BLOCKS:].astype(jnp.int32)
     sums[...] = jnp.zeros_like(sums)
     sharpness = FEAT**0.5
     diag_slot = place_ref[6]
@@ -131,7 +119,7 @@
             weight = list_ref[1, at].astype(jnp.float32)
             off = jnp.where(slot == diag_slot, weight, 0.0)
             scores = lax.dot_general(
-                line_v[b ^ mine], plane_ref[a, :ROWS, :], (((1,), (1,)), ((), ())),
+                line_v[b ^ mine], plane_ref[a], (((1,), (1,)), ((), ())),
                 preferred_element_type=jnp.float32,
             )
             tile = jnp.exp(sharpness * (scores - 1.0)) * (weight - on_diag * off)
@@ -144,6 +132,7 @@
     lax.fori_loop(0, (list_ref[2, 0] + CHUNK - 1) // CHUNK, build_chunk, 0)
     for b in range(GROUP):
         deg_ref[b : b + 1, :] = jnp.sum(sums[b].T, axis=0, keepdims=True)
+    deg_ref[GROUP:, :] = jnp.broadcast_to(seeds_ref[...].astype(jnp.float32), (EXTRA, ROWS))
 
 
 def split_into(wide, b, spread):
@@ -175,9 +164,11 @@
     return classes == seeds_ref[b : b + 1, :]
 
 
-def first_kernel(place_ref, list_ref, tiles_ref, seeds_ref, parts_ref,
-                 out_ref, scale_ref, own_ref, total, wide):
-    scale_ref[...] = lax.rsqrt(jnp.sum(parts_ref[...], axis=0))
+def first_kernel(place_ref, list_ref, tiles_ref, parts_ref,
+                 out_ref, scale_ref, own_ref, seeds_ref, total, wide):
+    scale_ref[...] = lax.rsqrt(jnp.sum(parts_ref[:, :GROUP, :], axis=0))
+    for b in range(GROUP):
+        seeds_ref[b : b + 1, :] = parts_ref[b, GROUP : GROUP + 1, :].astype(jnp.int32)
     own_ref[...] = scale_ref[pl.ds(place_ref[5], 1), :]
     for b in range(GROUP):
         split_into(wide, b, jnp.where(seeded_block(seeds_ref, b), scale_ref[b : b + 1, :], 0.0))
@@ -220,43 +211,52 @@
     return [(k, k ^ step) for k in range(count)]
 
 
+def doubling(rows, steps):
+    for axis, count, step in steps:
+        rows = jnp.concatenate([rows, lax.ppermute(rows, axis, pairs(count, step))], axis=0)
+    return rows
+
+
 def local(embeddings, tile_list, seeds):
     x, y, zlo, core, zhi = (lax.axis_index(name) for name in ("x", "y", "zlo", "core", "zhi"))
     mine = zlo * 8 + core * 4 + zhi
     place = jnp.stack([x, y, zlo, core, zhi, mine, (x * 4 + y) * GROUP + mine]).astype(jnp.int32)
-    block, noted, own_seeds = call(
+    block, bits = call(
         prep_kernel,
+        (array(ROWS, FEAT, dtype=jnp.bfloat16), array(1, BLOCKS)),
+        [ANY] * 2,
+        (VMEM,) * 2,
         (
-            array(ROWS, FEAT, dtype=jnp.bfloat16),
-            array(ROWS + EXTRA, FEAT, dtype=jnp.bfloat16),
-            array(1, ROWS),
+            pltpu.VMEM((ROWS, FEAT), jnp.bfloat16),
+            pltpu.VMEM((2, 32), jnp.int32),
+            pltpu.SemaphoreType.DMA,
+            pltpu.SemaphoreType.DMA,
         ),
-        [SMEM] + [VMEM] * 3,
-        (VMEM,) * 3,
-        limit=4,
-    )(place, embeddings, tile_list.reshape(-1, 2).T, seeds[None, :])
-
+        limit=60,
+    )(embeddings, tile_list.reshape(-1, 2).T)
+
+    plane = gather(block, PLANE)
     hops = [lax.ppermute(block, "zhi", pairs(4, step)) for step in (1, 2, 3)]
-    plane = gather(noted, PLANE)
+    ahead = doubling(bits, (("x", 4, 1), ("x", 4, 2)))
+    back = doubling(bits, (("y", 4, 1), ("y", 4, 2)))
+    hops, ahead, back = lax.optimization_barrier((hops, ahead, back))
     own = jnp.stack([block] + hops)
     mate = lax.ppermute(own, "core", pairs(2, 1))
     far = lax.ppermute(own, "zlo", pairs(2, 1))
-    note = call(
-        relay_kernel, array(EXTRA, BLOCKS + ROWS), [SMEM, VMEM, VMEM], VMEM, limit=4
-    )(place, plane, own_seeds)
-    notes = gather(note, LINE)
+    ahead = doubling(ahead, (("zhi", 4, 1), ("zhi", 4, 2)))
+    back = doubling(back, (("core", 2, 1), ("zlo", 2, 1)))
+    far, ahead, back = lax.optimization_barrier((far, ahead, back))
     far_mate = lax.ppermute(far, "core", pairs(2, 1))
 
-    tiles, listing, partial_degree, line_seeds = call(
+    tiles, listing, parts = call(
         build_kernel,
         (
             array(BLOCKS, 2 * ROWS, ROWS, dtype=jnp.bfloat16),
             array(EXTRA, BLOCKS, dtype=jnp.int32),
-            array(GROUP, ROWS),
-            array(GROUP, ROWS, dtype=jnp.int32),
+            array(GROUP + EXTRA, ROWS),
         ),
-        [SMEM] + [VMEM] * 2 + [ANY] * 4,
-        (VMEM, SMEM, VMEM, VMEM),
+        [SMEM] + [VMEM] * 4 + [ANY] * 4,
+        (VMEM, SMEM, VMEM),
         (
             pltpu.VMEM((GROUP, ROWS, FEAT), jnp.bfloat16),
             pltpu.VMEM((GROUP, ROWS, ROWS), jnp.float32),
@@ -265,21 +265,21 @@
             pltpu.SemaphoreType.DMA,
         ),
         limit=14,
-    )(place, notes, plane, own, mate, far, far_mate)
+    )(place, ahead, back, seeds[None, :], plane, own, mate, far, far_mate)
 
     scratch = (
         pltpu.VMEM((GROUP, CLASSES, ROWS), jnp.float32),
         pltpu.VMEM((GROUP, 2 * CLASSES, 2 * ROWS), jnp.bfloat16),
     )
     sums_out = array(GROUP, CLASSES, ROWS, dtype=jnp.bfloat16)
-    partial, scale, own_scale = call(
+    partial, scale, own_scale, line_seeds = call(
         first_kernel,
-        (sums_out, array(GROUP, ROWS), array(1, ROWS)),
-        [SMEM, SMEM, VMEM, VMEM, VMEM],
-        (VMEM,) * 3,
+        (sums_out, array(GROUP, ROWS), array(1, ROWS), array(GROUP, ROWS, dtype=jnp.int32)),
+        [SMEM, SMEM, VMEM, VMEM],
+        (VMEM,) * 4,
         scratch,
         limit=6,
-    )(place, listing, tiles, line_seeds, gather(partial_degree, LINE))
+    )(place, listing, tiles, gather(parts, LINE))
     for sweep in range(3):
         if sweep:
             smooth = gather((BLEND * own_scale * own_scale * summed).astype(jnp.bfloat16), LINE)

time: 181 us -> 198 us (1.094)
  starting transfers between devices: 25 us -> 37.7 us
  blocking collectives: 85.5 us -> 90.5 us
  waiting for transfers between devices: 43 us -> 47 us
    ppermute x0 -> x8, waiting for transfers between devices: none -> 44.5 us  [doubling(): lax.ppermute(rows, axis, pairs(count, step))]
    ppermute x0 -> x8, starting transfers between devices: none -> 22.1 us  [doubling(): lax.ppermute(rows, axis, pairs(count, step))]
    ppermute x1, waiting for transfers between devices: 18 us -> 0.01 us  [local(): far = lax.ppermute(own, 'zlo', pairs(2, 1))]
    ppermute x3, waiting for transfers between devices: 16.3 us -> 0.01 us  [local(): hops = [lax.ppermute(block, 'zhi', pairs(4, step)) for step in (1, 2, 3)]]
    all_to_all x2 -> x1, waiting for transfers between devices: 8.66 us -> 0.01 us  [exchange(): return lax.all_to_all(blocks, axes, 0, 0)]
    all_to_all x2 -> x1, starting transfers between devices: 14.9 us -> 7.17 us  [exchange(): return lax.all_to_all(blocks, axes, 0, 0)]
    all_to_all x6, blocking collectives: 85.5 us -> 90.5 us  [exchange(): return lax.all_to_all(blocks, axes, 0, 0)]
    ppermute x1, waiting for transfers between devices: 0.01 us -> 2.51 us  [local(): far_mate = lax.ppermute(far, 'core', pairs(2, 1))]
  transfers between devices with their start and end apart: 8 -> 15, of which waited for: 4 -> 6; matrix products, arithmetic and copies ran while one was open for 1% -> 1% of each run, Pallas kernels for 0% -> 0%
where the time goes in v5:
time: 198 us; the launch traced here: 197 us
  blocking collectives  90.5 us (46%)
  waiting for transfers between devices  47 us (24%)
  starting transfers between devices  37.7 us (19%)
  Pallas kernels  16.4 us (8%)
  local copies, waits for them, and re-layouts  3.08 us (2%)
    all_to_all x6, blocking collectives, exchange(): return lax.all_to_all(blocks, axes, 0, 0)  90.5 us
    ppermute x8, waiting for transfers between devices, doubling(): lax.ppermute(rows, axis, pairs(count, step))  44.5 us
    ppermute x8, starting transfers between devices, doubling(): lax.ppermute(rows, axis, pairs(count, step))  22.1 us
    ppermute x3, starting transfers between devices, local(): hops = [lax.ppermute(block, 'zhi', pairs(4, step)) for step in (1, 2, 3)]  7.77 us
    all_to_all x1, starting transfers between devices, exchange(): return lax.all_to_all(blocks, axes, 0, 0)  7.17 us
    pallas_call x1, Pallas kernels, local(): call(build_kernel, (array(BLOCKS, 2 * ROWS, ROWS, dtype=jnp.bfloat16), ar...  6.68 us
    pallas_call x2, Pallas kernels, local(): call(next_kernel, sums_out, [SMEM] + [VMEM] * 4, VMEM, scratch, limit=6)  5.31 us
  transfers between devices with their start and end apart: 15, of which 6 were waited for; matrix products, arithmetic and copies ran while one was open for 1% of the time, Pallas kernels for 0%

profile of v5, /device:TPU:32, one launch (start us, length us, event | category | flops | bytes accessed | tf_op | source)
XLA Modules:
  0.0 196.8 jit_solution(6929763850305325935)
XLA Ops:
  0.0 1.8 shard_map.37
  1.8 2.9 %broadcast_in_dim.11 = bf16[16,128,768]{2,1,0:T(8,128)(2,1)} broadcast(bf16[128,768]{1,0:T(8,128)(2,1)} %get-tuple-element.31), dimensions={1,2} | broadcast | bytes 3342336 | tf_op jit(solution)/shard_map/broadcast_in_dim | solution.py:207
  4.7 7.2 %all-to-all-start = ((bf16[16,128,768]{2,1,0:T(8,128)(2,1)}), bf16[16,128,768]{2,1,0:T(8,128)(2,1)S(1)}, u32[]{:S(2)}, u32[]{:S(2)}) async-start(bf16[16,128,768]{2,1,0:T(8,128)(2,1)} %broadcast_in_dim.11), calls=%async_computation | async-start | bytes 6291456 | tf_op jit(solution)/shard_map/all_to_all | solution.py:203
  11.8 0.0 copy-done.2
  11.9 2.0 %collective-permute-start.5 = (f32[1,256]{1,0:T(1,128)S(1)}, f32[1,256]{1,0:T(1,128)S(1)}, u32[]{:S(2)}, u32[]{:S(2)}) collective-permute-start(f32[1,256]{1,0:T(1,128)S(1)} %copy-done.2), channel_id=1, source_target_pairs={{0,1},{1,0},{2,3},{3,2},{4,5},{5,4},{6,7},{7,6},{8,9},{9,8},{10,11... | collective-permute-start | bytes 3080 | tf_op jit(solution)/shard_map/ppermute | solution.py:216
  13.9 1.5 collective-permute-start.3
  15.3 0.0 copy-done.1
  15.3 5.4 %collective-permute-start.2 = (bf16[128,768]{1,0:T(8,128)(2,1)S(1)}, bf16[128,768]{1,0:T(8,128)(2,1)S(1)}, u32[]{:S(2)}, u32[]{:S(2)}) collective-permute-start(bf16[128,768]{1,0:T(8,128)(2,1)S(1)} %copy-done.1), channel_id=1, source_target_pairs={{0,12},{4,8},{8,4},{12,0},{1,13},{5,9},{9,5},{13,1},{2,14},{6,10},... | collective-permute-start | bytes 589832 | tf_op jit(solution)/shard_map/ppermute | solution.py:239
  20.7 1.4 collective-permute-start.1
  22.2 0.9 collective-permute-start
  23.1 15.4 %collective-permute-done.5 = f32[1,256]{1,0:T(1,128)S(1)} collective-permute-done((f32[1,256]{1,0:T(1,128)S(1)}, f32[1,256]{1,0:T(1,128)S(1)}, u32[]{:S(2)}, u32[]{:S(2)}) %collective-permute-start.5) | collective-permute-done | bytes 1056 | tf_op jit(solution)/shard_map/ppermute | solution.py:216
  38.5 12.3 %collective-permute-done.3 = f32[1,256]{1,0:T(1,128)S(1)} collective-permute-done((f32[1,256]{1,0:T(1,128)S(1)}, f32[1,256]{1,0:T(1,128)S(1)}, u32[]{:S(2)}, u32[]{:S(2)}) %collective-permute-start.3) | collective-permute-done | bytes 1056 | tf_op jit(solution)/shard_map/ppermute | solution.py:216
  50.8 5.5 %collective-permute-start.6 = (f32[2,256]{1,0:T(2,128)S(1)}, f32[2,256]{1,0:T(2,128)S(1)}, u32[]{:S(2)}, u32[]{:S(2)}) collective-permute-start(f32[2,256]{1,0:T(2,128)S(1)} %get-tuple-element.59), channel_id=1, source_target_pairs={{0,2},{1,3},{2,0},{3,1},{4,6},{5,7},{6,4},{7,5},{8,10},{9,11},{10,... | collective-permute-start | bytes 6152 | tf_op jit(solution)/shard_map/ppermute | solution.py:216
  56.3 2.5 %collective-permute-start.4 = (f32[2,256]{1,0:T(2,128)S(1)}, f32[2,256]{1,0:T(2,128)S(1)}, u32[]{:S(2)}, u32[]{:S(2)}) collective-permute-start(f32[2,256]{1,0:T(2,128)S(1)} %get-tuple-element.60), channel_id=1, source_target_pairs={{0,64},{32,96},{64,0},{96,32},{1,65},{33,97},{65,1},{97,33},{2,66}... | collective-permute-start | bytes 6152 | tf_op jit(solution)/shard_map/ppermute | solution.py:216
  58.8 0.0 collective-permute-done.6
  58.8 2.6 %collective-permute-done.4 = f32[2,256]{1,0:T(2,128)S(1)} collective-permute-done((f32[2,256]{1,0:T(2,128)S(1)}, f32[2,256]{1,0:T(2,128)S(1)}, u32[]{:S(2)}, u32[]{:S(2)}) %collective-permute-start.4) | collective-permute-done | bytes 2080 | tf_op jit(solution)/shard_map/ppermute | solution.py:216
  61.4 0.0 collective-permute-done.2
  61.4 0.0 collective-permute-done.1
  61.4 0.0 collective-permute-done
  61.4 1.0 pad_maximum_fusion.own_ref
  62.4 0.1 collective-permute-start.7
  62.5 0.0 collective-permute-start.10
  62.5 0.5 collective-permute-start.12
  63.0 3.3 %collective-permute-start.8 = (f32[4,256]{1,0:T(4,128)S(1)}, f32[4,256]{1,0:T(4,128)S(1)}, u32[]{:S(2)}, u32[]{:S(2)}) collective-permute-start(f32[4,256]{1,0:T(4,128)S(1)} %get-tuple-element.36), channel_id=1, source_target_pairs={{0,4},{4,0},{8,12},{12,8},{1,5},{5,1},{9,13},{13,9},{2,6},{6,2},{1... | collective-permute-start | bytes 12296 | tf_op jit(solution)/shard_map/ppermute | solution.py:216
  66.3 0.0 collective-permute-done.10
  66.3 2.0 %collective-permute-start.11 = (f32[8,256]{1,0:T(8,128)S(1)}, f32[8,256]{1,0:T(8,128)S(1)}, u32[]{:S(2)}, u32[]{:S(2)}) collective-permute-start(f32[8,256]{1,0:T(8,128)S(1)} %pad_maximum_fusion.4), channel_id=1, source_target_pairs={{0,128},{128,0},{1,129},{129,1},{2,130},{130,2},{3,131},{131,3},{4... | collective-permute-start | bytes 24584 | tf_op jit(solution)/shard_map/ppermute | solution.py:216
  68.3 12.0 %collective-permute-done.8 = f32[4,256]{1,0:T(4,128)S(1)} collective-permute-done((f32[4,256]{1,0:T(4,128)S(1)}, f32[4,256]{1,0:T(4,128)S(1)}, u32[]{:S(2)}, u32[]{:S(2)}) %collective-permute-start.8) | collective-permute-done | bytes 4128 | tf_op jit(solution)/shard_map/ppermute | solution.py:216
  80.4 5.3 %collective-permute-start.9 = (f32[8,256]{1,0:T(8,128)S(1)}, f32[8,256]{1,0:T(8,128)S(1)}, u32[]{:S(2)}, u32[]{:S(2)}) collective-permute-start(f32[8,256]{1,0:T(8,128)S(1)} %pad_maximum_fusion.3), channel_id=1, source_target_pairs={{0,8},{4,12},{8,0},{12,4},{1,9},{5,13},{9,1},{13,5},{2,10},{6,14},... | collective-permute-start | bytes 24584 | tf_op jit(solution)/shard_map/ppermute | solution.py:216
  85.7 0.0 collective-permute-done.11
  85.7 2.2 %collective-permute-done.9 = f32[8,256]{1,0:T(8,128)S(1)} collective-permute-done((f32[8,256]{1,0:T(8,128)S(1)}, f32[8,256]{1,0:T(8,128)S(1)}, u32[]{:S(2)}, u32[]{:S(2)}) %collective-permute-start.9) | collective-permute-done | bytes 8224 | tf_op jit(solution)/shard_map/ppermute | solution.py:216
  87.9 0.0 collective-permute-done.7.far_ref
  88.0 0.1 collective-permute-start.13
  88.1 0.1 stack.46.place_ref
  88.2 0.0 collective-permute-done.12.mate_ref
  88.2 2.5 %collective-permute-done.13.far_mate_ref = bf16[4,128,768]{2,1,0:T(8,128)(2,1)} collective-permute-done((bf16[4,128,768]{2,1,0:T(8,128)(2,1)}, bf16[4,128,768]{2,1,0:T(8,128)(2,1)}, u32[]{:S(2)}, u32[]{:S(2)}) %collective-permute-start.13) | collective-permute-done | bytes 786464 | tf_op jit(solution)/shard_map/ppermute | solution.py:249
  90.7 0.0 all-to-all-done.plane_ref
  90.7 0.0 copy-done
  90.7 6.7 %shard_map.38 = (bf16[256,256,128]{2,1,0:T(8,128)(2,1)S(1)}, s32[8,256]{1,0:T(8,128)S(1)}, f32[24,128]{1,0:T(8,128)S(1)}) custom-call(s32[7]{0:T(128)S(1)} %stack.46.place_ref, f32[16,256]{1,0:T(8,128)S(1)} %pad_maximum_fusion.1.ahead_ref, f32[16,256]{1,0:T(8,128)S(1)} %pad_maximum_fusion.2.back_ref, s32[1,128]{1,0:T(1,128)S(1)} %bitcast.25, ...), custom_call_target="tpu_custom_call" | custom-call | tf_op jit(solution)/shard_map/pallas_call | solution.py:251
  97.4 16.6 %all_to_all.35.parts_ref = f32[16,24,128]{2,1,0:T(8,128)S(1)} all-to-all(f32[16,24,128]{2,1,0:T(8,128)S(1)} %broadcast_in_dim.12), channel_id=1, replica_groups=mesh['zlo'=2,'x'=4,'core'=2,'zhi'=4,'y'=4] {'zlo','core','zhi'}, dimensions={0} | all-to-all | bytes 393216 | tf_op jit(solution)/shard_map/all_to_all | solution.py:203
  113.9 2.6 %shard_map.39 = (bf16[16,64,128]{2,1,0:T(8,128)(2,1)S(1)}, f32[16,128]{1,0:T(8,128)S(1)}, f32[1,128]{1,0:T(1,128)S(1)}, s32[16,128]{1,0:T(8,128)S(1)}) custom-call(s32[7]{0:T(128)S(1)} %stack.46.place_ref, s32[8,256]{1,0:T(8,128)S(1)} %get-tuple-element.41.list_ref, bf16[256,256,128]{2,1,0:T(8,128)(2,1)S(1)} %get-tuple-element.42.tiles_ref, ...), custom_call_target="tpu_custom_call" | custom-call | tf_op jit(solution)/shard_map/pallas_call | solution.py:275
  116.6 19.6 %all_to_all.36 = bf16[16,64,128]{2,1,0:T(8,128)(2,1)S(1)} all-to-all(bf16[16,64,128]{2,1,0:T(8,128)(2,1)S(1)} %get-tuple-element.46), channel_id=1, replica_groups=mesh['zlo'=2,'x'=4,'core'=2,'zhi'=4,'y'=4] {'x','y'}, dimensions={0} | all-to-all | bytes 524288 | tf_op jit(solution)/shard_map/all_to_all | solution.py:203
  136.3 12.8 %all_to_all.37.smooth_ref = bf16[16,64,128]{2,1,0:T(8,128)(2,1)S(1)} all-to-all(bf16[16,64,128]{2,1,0:T(8,128)(2,1)S(1)} %broadcast_in_dim.13), channel_id=1, replica_groups=mesh['zlo'=2,'x'=4,'core'=2,'zhi'=4,'y'=4] {'zlo','core','zhi'}, dimensions={0} | all-to-all | bytes 524288 | tf_op jit(solution)/shard_map/all_to_all | solution.py:203
  149.2 2.7 %shard_map.40 = bf16[16,64,128]{2,1,0:T(8,128)(2,1)S(1)} custom-call(s32[8,256]{1,0:T(8,128)S(1)} %get-tuple-element.41.list_ref, bf16[256,256,128]{2,1,0:T(8,128)(2,1)S(1)} %get-tuple-element.42.tiles_ref, s32[16,128]{1,0:T(8,128)S(1)} %get-tuple-element.44.seeds_ref, f32[16,128]{1,0:T(8,128)S(1)} %get-tuple-element.45.scale_ref, ...), custom_call_target="tpu_custom_call" | custom-call | tf_op jit(solution)/shard_map/pallas_call | solution.py:286
  151.8 13.6 %all_to_all.38 = bf16[16,64,128]{2,1,0:T(8,128)(2,1)S(1)} all-to-all(bf16[16,64,128]{2,1,0:T(8,128)(2,1)S(1)} %shard_map.40), channel_id=1, replica_groups=mesh['zlo'=2,'x'=4,'core'=2,'zhi'=4,'y'=4] {'x','y'}, dimensions={0} | all-to-all | bytes 524288 | tf_op jit(solution)/shard_map/all_to_all | solution.py:203
  165.5 14.3 %all_to_all.39.smooth_ref = bf16[16,64,128]{2,1,0:T(8,128)(2,1)S(1)} all-to-all(bf16[16,64,128]{2,1,0:T(8,128)(2,1)S(1)} %broadcast_in_dim.14), channel_id=1, replica_groups=mesh['zlo'=2,'x'=4,'core'=2,'zhi'=4,'y'=4] {'zlo','core','zhi'}, dimensions={0} | all-to-all | bytes 524288 | tf_op jit(solution)/shard_map/all_to_all | solution.py:203
  179.8 2.7 %shard_map.41 = bf16[16,64,128]{2,1,0:T(8,128)(2,1)S(1)} custom-call(s32[8,256]{1,0:T(8,128)S(1)} %get-tuple-element.41.list_ref, bf16[256,256,128]{2,1,0:T(8,128)(2,1)S(1)} %get-tuple-element.42.tiles_ref, s32[16,128]{1,0:T(8,128)S(1)} %get-tuple-element.44.seeds_ref, f32[16,128]{1,0:T(8,128)S(1)} %get-tuple-element.45.scale_ref, ...), custom_call_target="tpu_custom_call" | custom-call | tf_op jit(solution)/shard_map/pallas_call | solution.py:286
  182.5 13.6 %all_to_all.40 = bf16[16,64,128]{2,1,0:T(8,128)(2,1)S(1)} all-to-all(bf16[16,64,128]{2,1,0:T(8,128)(2,1)S(1)} %shard_map.41), channel_id=1, replica_groups=mesh['zlo'=2,'x'=4,'core'=2,'zhi'=4,'y'=4] {'x','y'}, dimensions={0} | all-to-all | bytes 524288 | tf_op jit(solution)/shard_map/all_to_all | solution.py:203
  196.1 0.6 fusion
  (20 shorter events, 0.3 us)
Async XLA Ops:
  4.7 7.2 %copy-start.2 = (f32[1,256]{1,0:T(1,128)S(1)}, f32[1,256]{1,0:T(1,128)}, u32[]{:S(2)}) copy-start(f32[1,256]{1,0:T(1,128)} %get-tuple-element.32) | copy-start | bytes 3076
  4.7 10.7 %copy-start.1 = (bf16[128,768]{1,0:T(8,128)(2,1)S(1)}, bf16[128,768]{1,0:T(8,128)(2,1)}, u32[]{:S(2)}) copy-start(bf16[128,768]{1,0:T(8,128)(2,1)} %get-tuple-element.31) | copy-start | bytes 589828
  4.7 86.0 %copy-start = (s32[128]{0:T(128)S(1)}, s32[128]{0:T(128)}, u32[]{:S(2)}) copy-start(s32[128]{0:T(128)} %param.5) | copy-start | bytes 1540
  4.7 86.0 %all-to-all-start = ((bf16[16,128,768]{2,1,0:T(8,128)(2,1)}), bf16[16,128,768]{2,1,0:T(8,128)(2,1)S(1)}, u32[]{:S(2)}, u32[]{:S(2)}) async-start(bf16[16,128,768]{2,1,0:T(8,128)(2,1)} %broadcast_in_dim.11), calls=%async_computation | async-start | bytes 6291456 | tf_op jit(solution)/shard_map/all_to_all | solution.py:203
  11.9 26.6 %collective-permute-start.5 = (f32[1,256]{1,0:T(1,128)S(1)}, f32[1,256]{1,0:T(1,128)S(1)}, u32[]{:S(2)}, u32[]{:S(2)}) collective-permute-start(f32[1,256]{1,0:T(1,128)S(1)} %copy-done.2), channel_id=1, source_target_pairs={{0,1},{1,0},{2,3},{3,2},{4,5},{5,4},{6,7},{7,6},{8,9},{9,8},{10,11... | collective-permute-start | bytes 3080 | tf_op jit(solution)/shard_map/ppermute | solution.py:216
  13.9 36.9 %collective-permute-start.3 = (f32[1,256]{1,0:T(1,128)S(1)}, f32[1,256]{1,0:T(1,128)S(1)}, u32[]{:S(2)}, u32[]{:S(2)}) collective-permute-start(f32[1,256]{1,0:T(1,128)S(1)} %copy-done.2), channel_id=1, source_target_pairs={{0,32},{32,0},{64,96},{96,64},{1,33},{33,1},{65,97},{97,65},{2,34}... | collective-permute-start | bytes 3080 | tf_op jit(solution)/shard_map/ppermute | solution.py:216
  15.3 46.1 %collective-permute-start.2 = (bf16[128,768]{1,0:T(8,128)(2,1)S(1)}, bf16[128,768]{1,0:T(8,128)(2,1)S(1)}, u32[]{:S(2)}, u32[]{:S(2)}) collective-permute-start(bf16[128,768]{1,0:T(8,128)(2,1)S(1)} %copy-done.1), channel_id=1, source_target_pairs={{0,12},{4,8},{8,4},{12,0},{1,13},{5,9},{9,5},{13,1},{2,14},{6,10},... | collective-permute-start | bytes 589832 | tf_op jit(solution)/shard_map/ppermute | solution.py:239
  20.7 40.7 %collective-permute-start.1 = (bf16[128,768]{1,0:T(8,128)(2,1)S(1)}, bf16[128,768]{1,0:T(8,128)(2,1)S(1)}, u32[]{:S(2)}, u32[]{:S(2)}) collective-permute-start(bf16[128,768]{1,0:T(8,128)(2,1)S(1)} %copy-done.1), channel_id=1, source_target_pairs={{0,8},{4,12},{8,0},{12,4},{1,9},{5,13},{9,1},{13,5},{2,10},{6,14},... | collective-permute-start | bytes 589832 | tf_op jit(solution)/shard_map/ppermute | solution.py:239
  22.2 39.2 %collective-permute-start = (bf16[128,768]{1,0:T(8,128)(2,1)S(1)}, bf16[128,768]{1,0:T(8,128)(2,1)S(1)}, u32[]{:S(2)}, u32[]{:S(2)}) collective-permute-start(bf16[128,768]{1,0:T(8,128)(2,1)S(1)} %copy-done.1), channel_id=1, source_target_pairs={{0,4},{4,0},{8,12},{12,8},{1,5},{5,1},{9,13},{13,9},{2,6},{6,2},{1... | collective-permute-start | bytes 589832 | tf_op jit(solution)/shard_map/ppermute | solution.py:239
  50.8 8.0 %collective-permute-start.6 = (f32[2,256]{1,0:T(2,128)S(1)}, f32[2,256]{1,0:T(2,128)S(1)}, u32[]{:S(2)}, u32[]{:S(2)}) collective-permute-start(f32[2,256]{1,0:T(2,128)S(1)} %get-tuple-element.59), channel_id=1, source_target_pairs={{0,2},{1,3},{2,0},{3,1},{4,6},{5,7},{6,4},{7,5},{8,10},{9,11},{10,... | collective-permute-start | bytes 6152 | tf_op jit(solution)/shard_map/ppermute | solution.py:216
  56.3 5.1 %collective-permute-start.4 = (f32[2,256]{1,0:T(2,128)S(1)}, f32[2,256]{1,0:T(2,128)S(1)}, u32[]{:S(2)}, u32[]{:S(2)}) collective-permute-start(f32[2,256]{1,0:T(2,128)S(1)} %get-tuple-element.60), channel_id=1, source_target_pairs={{0,64},{32,96},{64,0},{96,32},{1,65},{33,97},{65,1},{97,33},{2,66}... | collective-permute-start | bytes 6152 | tf_op jit(solution)/shard_map/ppermute | solution.py:216
  62.4 25.5 %collective-permute-start.7 = (bf16[4,128,768]{2,1,0:T(8,128)(2,1)}, bf16[4,128,768]{2,1,0:T(8,128)(2,1)}, u32[]{:S(2)}, u32[]{:S(2)}) collective-permute-start(bf16[4,128,768]{2,1,0:T(8,128)(2,1)} %pad_maximum_fusion.own_ref), channel_id=1, source_target_pairs={{0,128},{128,0},{1,129},{129,1},{2,130},{130,2},{3,131},{131,3},{4... | collective-permute-start | bytes 2359304 | tf_op jit(solution)/shard_map/ppermute | solution.py:245
  62.5 3.8 %collective-permute-start.10 = (f32[4,256]{1,0:T(4,128)S(1)}, f32[4,256]{1,0:T(4,128)S(1)}, u32[]{:S(2)}, u32[]{:S(2)}) collective-permute-start(f32[4,256]{1,0:T(4,128)S(1)} %get-tuple-element.37), channel_id=1, source_target_pairs={{0,16},{16,0},{1,17},{17,1},{2,18},{18,2},{3,19},{19,3},{4,20},{20... | collective-permute-start | bytes 12296 | tf_op jit(solution)/shard_map/ppermute | solution.py:216
  62.5 25.6 %collective-permute-start.12 = (bf16[4,128,768]{2,1,0:T(8,128)(2,1)}, bf16[4,128,768]{2,1,0:T(8,128)(2,1)}, u32[]{:S(2)}, u32[]{:S(2)}) collective-permute-start(bf16[4,128,768]{2,1,0:T(8,128)(2,1)} %pad_maximum_fusion.own_ref), channel_id=1, source_target_pairs={{0,16},{16,0},{1,17},{17,1},{2,18},{18,2},{3,19},{19,3},{4,20},{20... | collective-permute-start | bytes 2359304 | tf_op jit(solution)/shard_map/ppermute | solution.py:244
  63.0 17.3 %collective-permute-start.8 = (f32[4,256]{1,0:T(4,128)S(1)}, f32[4,256]{1,0:T(4,128)S(1)}, u32[]{:S(2)}, u32[]{:S(2)}) collective-permute-start(f32[4,256]{1,0:T(4,128)S(1)} %get-tuple-element.36), channel_id=1, source_target_pairs={{0,4},{4,0},{8,12},{12,8},{1,5},{5,1},{9,13},{13,9},{2,6},{6,2},{1... | collective-permute-start | bytes 12296 | tf_op jit(solution)/shard_map/ppermute | solution.py:216
  66.3 19.4 %collective-permute-start.11 = (f32[8,256]{1,0:T(8,128)S(1)}, f32[8,256]{1,0:T(8,128)S(1)}, u32[]{:S(2)}, u32[]{:S(2)}) collective-permute-start(f32[8,256]{1,0:T(8,128)S(1)} %pad_maximum_fusion.4), channel_id=1, source_target_pairs={{0,128},{128,0},{1,129},{129,1},{2,130},{130,2},{3,131},{131,3},{4... | collective-permute-start | bytes 24584 | tf_op jit(solution)/shard_map/ppermute | solution.py:216
  80.4 7.6 %collective-permute-start.9 = (f32[8,256]{1,0:T(8,128)S(1)}, f32[8,256]{1,0:T(8,128)S(1)}, u32[]{:S(2)}, u32[]{:S(2)}) collective-permute-start(f32[8,256]{1,0:T(8,128)S(1)} %pad_maximum_fusion.3), channel_id=1, source_target_pairs={{0,8},{4,12},{8,0},{12,4},{1,9},{5,13},{9,1},{13,5},{2,10},{6,14},... | collective-permute-start | bytes 24584 | tf_op jit(solution)/shard_map/ppermute | solution.py:216
  88.0 2.7 %collective-permute-start.13 = (bf16[4,128,768]{2,1,0:T(8,128)(2,1)}, bf16[4,128,768]{2,1,0:T(8,128)(2,1)}, u32[]{:S(2)}, u32[]{:S(2)}) collective-permute-start(bf16[4,128,768]{2,1,0:T(8,128)(2,1)} %collective-permute-done.7.far_ref), channel_id=1, source_target_pairs={{0,16},{16,0},{1,17},{17,1},{2,18},{18,2},{3,19},{19,3},{4,20},{20... | collective-permute-start | bytes 2359304 | tf_op jit(solution)/shard_map/ppermute | solution.py:249

commit v6 on v4

--- a/solution.py
+++ b/solution.py
@@ -5,7 +5,6 @@
 from jax.experimental.pallas import tpu as pltpu
 from jax.sharding import Mesh
 from jax.sharding import PartitionSpec as P
-
 
 CLASSES = 64
 BLEND = 0.8
@@ -21,13 +20,14 @@
 ROWS = 128
 FEAT = 768
 EXTRA = 8
+FOLDS = FEAT // ROWS
 CHUNK = 8
 VMEM = pl.BlockSpec(memory_space=pltpu.VMEM)
 SMEM = pl.BlockSpec(memory_space=pltpu.SMEM)
 ANY = pl.BlockSpec(memory_space=pl.ANY)
 
 
-def prep_kernel(place_ref, emb_hbm, slots_hbm, seeds_hbm, block_ref, noted_ref, seeds_out,
+def prep_kernel(emb_hbm, slots_hbm, seeds_hbm, block_ref, folded_ref, seeds_out,
                 emb_ref, slots_ref, seeds_ref, emb_sem, slots_sem, seeds_sem):
     copies = [
         pltpu.make_async_copy(emb_hbm, emb_ref, emb_sem),
@@ -42,7 +42,8 @@
     norm = lax.rsqrt(jnp.sum(features * features, axis=1, keepdims=True) + EPSILON)
     normed = (features * norm).astype(jnp.bfloat16)
     block_ref[...] = normed
-    noted_ref[:ROWS, :] = normed
+    for k in range(FOLDS):
+        folded_ref[k * ROWS : (k + 1) * ROWS, :] = normed[:, k * ROWS : (k + 1) * ROWS]
     first, second = slots_ref[0:1, :], slots_ref[1:2, :]
     ids = jnp.where(first >= 0, first * GROUP + second, -1)
     hits = (lax.broadcasted_iota(jnp.int32, (BLOCKS, 32), 0) == ids).astype(jnp.float32)
@@ -50,8 +51,8 @@
         jnp.ones((EXTRA, 32), jnp.float32), hits, (((1,), (1,)), ((), ())),
         preferred_element_type=jnp.float32,
     )
-    noted_ref[ROWS:, :BLOCKS] = bits.astype(jnp.bfloat16)
-    noted_ref[ROWS:, BLOCKS:] = jnp.zeros((EXTRA, FEAT - BLOCKS), jnp.bfloat16)
+    row = lax.broadcasted_iota(jnp.int32, (EXTRA, ROWS), 0)
+    folded_ref[FEAT:, :] = jnp.where(row < 4, bits[:, :ROWS], bits[:, ROWS:]).astype(jnp.bfloat16)
     seeds_out[...] = seeds_ref[...].astype(jnp.float32)
 
 
@@ -61,7 +62,8 @@
     passed = jnp.zeros((EXTRA, BLOCKS), jnp.float32)
     for k in range(4):
         for at, line in ((k * 4 + y, k), (x * 4 + k, 4 + k)):
-            note = plane_ref[at, ROWS:, :BLOCKS].astype(jnp.float32)
+            note = plane_ref[at, FEAT:, :].astype(jnp.float32)
+            note = jnp.concatenate([note[0:1], note[4:5]], axis=1)
             passed = jnp.where(row == line, note, passed)
     out_ref[:, :BLOCKS] = passed
     out_ref[:, BLOCKS:] = jnp.broadcast_to(seeds_ref[...], (EXTRA, ROWS))
@@ -111,7 +113,7 @@
 
 def build_kernel(place_ref, notes_ref, plane_ref, own_ref, mate_ref, far_ref, far_mate_ref,
                  tiles_ref, list_ref, deg_ref, seeds_ref, line_v, sums, list_v, list_sem, line_sem):
-    mine = place_ref[5]
+    planes = place_ref[5] & 12
     parts = [
         pltpu.make_async_copy(part, line_v.at[pl.ds(at * 4, 4)], line_sem)
         for at, part in enumerate((own_ref, mate_ref, far_ref, far_mate_ref))
@@ -141,14 +143,15 @@
             a, b = slot >> 4, slot & 15
             weight = list_ref[1, at].astype(jnp.float32)
             off = jnp.where(slot == diag_slot, weight, 0.0)
+            left = jnp.concatenate(
+                [plane_ref[a, f * ROWS : (f + 1) * ROWS, :] for f in range(FOLDS)], axis=1
+            )
             scores = lax.dot_general(
-                line_v[b ^ mine], plane_ref[a, :ROWS, :], (((1,), (1,)), ((), ())),
+                line_v[b ^ planes], left, (((1,), (1,)), ((), ())),
                 preferred_element_type=jnp.float32,
             )
             tile = jnp.exp(sharpness * (scores - 1.0)) * (weight - on_diag * off)
-            high = tile.astype(jnp.bfloat16)
-            tiles_ref[at, :ROWS, :] = high
-            tiles_ref[at, ROWS:, :] = (tile - high.astype(jnp.float32)).astype(jnp.bfloat16)
+            tiles_ref[at] = tile.astype(jnp.bfloat16)
             sums[b] += tile
         return carry
 
@@ -157,24 +160,16 @@
         deg_ref[b : b + 1, :] = jnp.sum(sums[b].T, axis=0, keepdims=True)
 
 
-def split_into(wide, b, spread):
-    high = spread.astype(jnp.bfloat16)
-    low = (spread - high.astype(jnp.float32)).astype(jnp.bfloat16)
-    wide[b, :CLASSES, :ROWS] = high
-    wide[b, :CLASSES, ROWS:] = high
-    wide[b, CLASSES:, :ROWS] = low
-    wide[b, CLASSES:, ROWS:] = jnp.zeros_like(low)
-
-
-def run_apply(list_ref, tiles_ref, out_ref, total, wide):
+def run_apply(list_ref, tiles_ref, out_ref, total, spread):
     total[...] = jnp.zeros_like(total)
 
     def chunk_step(group, carry):
         for k in range(CHUNK):
             at = group * CHUNK + k
             slot = list_ref[0, at]
-            both = jnp.dot(wide[slot & 15], tiles_ref[at], preferred_element_type=jnp.float32)
-            total[slot >> 4] += both[:CLASSES] + both[CLASSES:]
+            total[slot >> 4] += jnp.dot(
+                spread[slot & 15], tiles_ref[at], preferred_element_type=jnp.float32
+            )
         return carry
 
     lax.fori_loop(0, (list_ref[2, 0] + CHUNK - 1) // CHUNK, chunk_step, 0)
@@ -187,21 +182,22 @@
 
 
 def first_kernel(place_ref, list_ref, tiles_ref, seeds_ref, parts_ref,
-                 out_ref, scale_ref, own_ref, total, wide):
+                 out_ref, scale_ref, own_ref, total, spread):
     scale_ref[...] = lax.rsqrt(jnp.sum(parts_ref[...], axis=0))
     own_ref[...] = scale_ref[pl.ds(place_ref[5], 1), :]
     for b in range(GROUP):
-        split_into(wide, b, jnp.where(seeded_block(seeds_ref, b), scale_ref[b : b + 1, :], 0.0))
-    run_apply(list_ref, tiles_ref, out_ref, total, wide)
-
-
-def next_kernel(list_ref, tiles_ref, seeds_ref, scale_ref, smooth_ref, out_ref, total, wide):
+        seeded = jnp.where(seeded_block(seeds_ref, b), scale_ref[b : b + 1, :], 0.0)
+        spread[b] = seeded.astype(jnp.bfloat16)
+    run_apply(list_ref, tiles_ref, out_ref, total, spread)
+
+
+def next_kernel(list_ref, tiles_ref, seeds_ref, scale_ref, smooth_ref, out_ref, total, spread):
     for b in range(GROUP):
         seed_part = jnp.where(
             seeded_block(seeds_ref, b), (1.0 - BLEND) * scale_ref[b : b + 1, :], 0.0
         )
-        split_into(wide, b, smooth_ref[b].astype(jnp.float32) + seed_part)
-    run_apply(list_ref, tiles_ref, out_ref, total, wide)
+        spread[b] = (smooth_ref[b].astype(jnp.float32) + seed_part).astype(jnp.bfloat16)
+    run_apply(list_ref, tiles_ref, out_ref, total, spread)
 
 
 def call(kernel, outs, ins, out_specs, scratch=(), limit=8):
@@ -235,14 +231,14 @@
     x, y, zlo, core, zhi = (lax.axis_index(name) for name in ("x", "y", "zlo", "core", "zhi"))
     mine = zlo * 8 + core * 4 + zhi
     place = jnp.stack([x, y, zlo, core, zhi, mine, (x * 4 + y) * GROUP + mine]).astype(jnp.int32)
-    block, noted, own_seeds = call(
+    block, folded, own_seeds = call(
         prep_kernel,
         (
             array(ROWS, FEAT, dtype=jnp.bfloat16),
-            array(ROWS + EXTRA, FEAT, dtype=jnp.bfloat16),
+            array(FEAT + EXTRA, ROWS, dtype=jnp.bfloat16),
             array(1, ROWS),
         ),
-        [SMEM] + [ANY] * 3,
+        [ANY] * 3,
         (VMEM,) * 3,
         (
             pltpu.VMEM((ROWS, FEAT), jnp.bfloat16),
@@ -250,27 +246,26 @@
             pltpu.VMEM((1, ROWS), jnp.int32),
         )
         + (pltpu.SemaphoreType.DMA,) * 3,
-        limit=62,
-    )(place, embeddings, tile_list.reshape(-1, 2).T, seeds[None, :])
-
-    hops = []
-    for step in (1, 2, 3):
-        hops.append(lax.ppermute(block, "zhi", pairs(4, step)))
-    plane = gather(noted, PLANE)
-    own = jnp.stack([block] + hops)
+        limit=60,
+    )(embeddings, tile_list.reshape(-1, 2).T, seeds[None, :])
+
+    plane = gather(folded, PLANE)
+    own = lax.all_gather(block, "zhi")
     mate = lax.ppermute(own, "core", pairs(2, 1))
     far = lax.ppermute(own, "zlo", pairs(2, 1))
+    far_mate = lax.ppermute(far, "core", pairs(2, 1))
+    plane, own_seeds, place, mate, far_mate = lax.optimization_barrier(
+        (plane, own_seeds, place, mate, far_mate)
+    )
     note = call(
         relay_kernel, array(EXTRA, BLOCKS + ROWS), [SMEM, VMEM, VMEM], VMEM, limit=4
     )(place, plane, own_seeds)
     notes = gather(note, LINE)
-    far, notes = lax.optimization_barrier((far, notes))
-    far_mate = lax.ppermute(far, "core", pairs(2, 1))
 
     tiles, listing, partial_degree, line_seeds = call(
         build_kernel,
         (
-            array(BLOCKS, 2 * ROWS, ROWS, dtype=jnp.bfloat16),
+            array(BLOCKS, ROWS, ROWS, dtype=jnp.bfloat16),
             array(EXTRA, BLOCKS, dtype=jnp.int32),
             array(GROUP, ROWS),
             array(GROUP, ROWS, dtype=jnp.int32),
@@ -289,7 +284,7 @@
 
     scratch = (
         pltpu.VMEM((GROUP, CLASSES, ROWS), jnp.float32),
-        pltpu.VMEM((GROUP, 2 * CLASSES, 2 * ROWS), jnp.bfloat16),
+        pltpu.VMEM((GROUP, CLASSES, ROWS), jnp.bfloat16),
     )
     sums_out = array(GROUP, CLASSES, ROWS, dtype=jnp.bfloat16)
     partial, scale, own_scale = call(

time: 186 us -> 174 us (0.935)
  blocking collectives: 89.9 us -> 124 us
  waiting for transfers between devices: 44.3 us -> 18.6 us
  starting transfers between devices: 27 us -> 8.27 us
    all_to_all x2 -> x1, waiting for transfers between devices: 25.8 us -> 0.86 us  [exchange(): return lax.all_to_all(blocks, axes, 0, 0)]
    all_gather x0 -> x1, blocking collectives: none -> 23 us  [local(): own = lax.all_gather(block, 'zhi')]
    ppermute x3 -> x0, waiting for transfers between devices: 16.3 us -> none  [local(): hops.append(lax.ppermute(block, 'zhi', pairs(4, step)))]
    ppermute x1, waiting for transfers between devices: 0.01 us -> 15.2 us  [local(): far = lax.ppermute(own, 'zlo', pairs(2, 1))]
    all_to_all x6 -> x7, blocking collectives: 89.9 us -> 101 us  [exchange(): return lax.all_to_all(blocks, axes, 0, 0)]
    all_to_all x2 -> x1, starting transfers between devices: 15.8 us -> 7.17 us  [exchange(): return lax.all_to_all(blocks, axes, 0, 0)]
    ppermute x3 -> x0, starting transfers between devices: 7.95 us -> none  [local(): hops.append(lax.ppermute(block, 'zhi', pairs(4, step)))]
  transfers between devices with their start and end apart: 8 -> 4, of which waited for: 5 -> 3; matrix products, arithmetic and copies ran while one was open for 1% -> 0% of each run, Pallas kernels for 0% -> 0%
where the time goes in v6:
time: 174 us; the launch traced here: 171 us
  blocking collectives  124 us (71%)
  waiting for transfers between devices  18.6 us (11%)
  Pallas kernels  16.7 us (10%)
  starting transfers between devices  8.27 us (5%)
  local copies, waits for them, and re-layouts  3.2 us (2%)
    all_to_all x7, blocking collectives, exchange(): return lax.all_to_all(blocks, axes, 0, 0)  101 us
    all_gather x1, blocking collectives, local(): own = lax.all_gather(block, 'zhi')  23 us
    ppermute x1, waiting for transfers between devices, local(): far = lax.ppermute(own, 'zlo', pairs(2, 1))  15.2 us
    pallas_call x1, Pallas kernels, local(): call(build_kernel, (array(BLOCKS, ROWS, ROWS, dtype=jnp.bfloat16), array(...  7.44 us
    all_to_all x1, starting transfers between devices, exchange(): return lax.all_to_all(blocks, axes, 0, 0)  7.17 us
    pallas_call x2, Pallas kernels, local(): call(next_kernel, sums_out, [SMEM] + [VMEM] * 4, VMEM, scratch, limit=6)  4.56 us
  transfers between devices with their start and end apart: 4, of which 3 were waited for; matrix products, arithmetic and copies ran while one was open for 0% of the time, Pallas kernels for 0%

profile of v6, /device:TPU:32, one launch (start us, length us, event | category | flops | bytes accessed | tf_op | source)
XLA Modules:
  0.0 171.2 jit_solution(4188252457232180834)
XLA Ops:
  0.0 1.8 %shard_map.37 = (bf16[128,768]{1,0:T(8,128)(2,1)}, bf16[776,128]{1,0:T(8,128)(2,1)}, f32[1,128]{1,0:T(1,128)}) custom-call(bf16[128,768]{1,0:T(8,128)(2,1)} %emb_hbm.1, s32[2,32]{1,0:T(2,128)} %bitcast.23, s32[1,128]{1,0:T(1,128)} %bitcast.22), custom_call_target="tpu_custom_call" | custom-call | tf_op jit(solution)/shard_map/pallas_call | solution.py:234
  1.9 3.0 %broadcast_in_dim.13 = bf16[16,776,128]{2,1,0:T(8,128)(2,1)} broadcast(bf16[776,128]{1,0:T(8,128)(2,1)} %get-tuple-element.29), dimensions={1,2} | broadcast | bytes 3377152 | tf_op jit(solution)/shard_map/broadcast_in_dim | solution.py:223
  4.8 0.0 copy-start.1
  4.8 0.0 copy-start
  4.8 7.2 %all-to-all-start = ((bf16[16,776,128]{2,1,0:T(8,128)(2,1)}), bf16[16,776,128]{2,1,0:T(8,128)(2,1)S(1)}, u32[]{:S(2)}, u32[]{:S(2)}) async-start(bf16[16,776,128]{2,1,0:T(8,128)(2,1)} %broadcast_in_dim.13), calls=%async_computation | async-start | bytes 6356992 | tf_op jit(solution)/shard_map/all_to_all | solution.py:219
  12.0 0.0 copy-done.1
  12.0 23.0 %all-gather = bf16[512,768]{1,0:T(8,128)(2,1)} all-gather(bf16[128,768]{1,0:T(8,128)(2,1)S(1)} %copy-done.1), channel_id=2, replica_groups=mesh['zlo'=2,'x'=4,'core'=2,'zhi'=4,'y'=4] {'zhi'}, dimensions={0}, use_global_device_ids=true | all-gather | bytes 983040 | tf_op jit(solution)/shard_map/all_gather | solution.py:253
  35.0 1.1 collective-permute-start.1
  36.1 0.0 collective-permute-start
  36.1 15.2 %collective-permute-done.1.far_ref = bf16[4,128,768]{2,1,0:T(8,128)(2,1)} collective-permute-done((bf16[4,128,768]{2,1,0:T(8,128)(2,1)}, bf16[4,128,768]{2,1,0:T(8,128)(2,1)}, u32[]{:S(2)}, u32[]{:S(2)}) %collective-permute-start.1) | collective-permute-done | bytes 786464 | tf_op jit(solution)/shard_map/ppermute | solution.py:255
  51.3 0.0 collective-permute-start.2
  51.3 0.1 stack.31.place_ref
  51.4 0.0 collective-permute-done.mate_ref
  51.4 2.5 %collective-permute-done.2.far_mate_ref = bf16[4,128,768]{2,1,0:T(8,128)(2,1)} collective-permute-done((bf16[4,128,768]{2,1,0:T(8,128)(2,1)}, bf16[4,128,768]{2,1,0:T(8,128)(2,1)}, u32[]{:S(2)}, u32[]{:S(2)}) %collective-permute-start.2) | collective-permute-done | bytes 786464 | tf_op jit(solution)/shard_map/ppermute | solution.py:256
  54.0 0.9 all-to-all-done.plane_ref
  54.8 0.0 copy-done
  54.8 0.6 shard_map.38
  55.4 17.1 %all_to_all.40.notes_ref = f32[16,8,384]{2,1,0:T(8,128)S(1)} all-to-all(f32[16,8,384]{2,1,0:T(8,128)S(1)} %broadcast_in_dim.14), channel_id=1, replica_groups=mesh['zlo'=2,'x'=4,'core'=2,'zhi'=4,'y'=4] {'zlo','core','zhi'}, dimensions={0} | all-to-all | bytes 393216 | tf_op jit(solution)/shard_map/all_to_all | solution.py:219
  72.5 7.4 %shard_map.39 = (bf16[256,128,128]{2,1,0:T(8,128)(2,1)S(1)}, s32[8,256]{1,0:T(8,128)S(1)}, f32[16,128]{1,0:T(8,128)S(1)}, s32[16,128]{1,0:T(8,128)S(1)}) custom-call(s32[7]{0:T(128)S(1)} %stack.31.place_ref, f32[16,8,384]{2,1,0:T(8,128)S(1)} %all_to_all.40.notes_ref, bf16[16,776,128]{2,1,0:T(8,128)(2,1)S(1)} %all-to-all-done.plane_ref, ...), custom_call_target="tpu_custom_call" | custom-call | tf_op jit(solution)/shard_map/pallas_call | solution.py:265
  79.9 12.4 %all_to_all.41.parts_ref = f32[16,16,128]{2,1,0:T(8,128)S(1)} all-to-all(f32[16,16,128]{2,1,0:T(8,128)S(1)} %broadcast_in_dim.15), channel_id=1, replica_groups=mesh['zlo'=2,'x'=4,'core'=2,'zhi'=4,'y'=4] {'zlo','core','zhi'}, dimensions={0} | all-to-all | bytes 262144 | tf_op jit(solution)/shard_map/all_to_all | solution.py:219
  92.3 2.3 %shard_map.40 = (bf16[16,64,128]{2,1,0:T(8,128)(2,1)S(1)}, f32[16,128]{1,0:T(8,128)S(1)}, f32[1,128]{1,0:T(1,128)S(1)}) custom-call(s32[7]{0:T(128)S(1)} %stack.31.place_ref, s32[8,256]{1,0:T(8,128)S(1)} %get-tuple-element.37.list_ref, bf16[256,128,128]{2,1,0:T(8,128)(2,1)S(1)} %get-tuple-element.38.tiles_ref, s32[16,128]{1,0:T(8,128)S(1)} %get-tuple-element.39.seeds_ref, ...), custom_call_target="tpu_custom_call" | custom-call | tf_op jit(solution)/shard_map/pallas_call | solution.py:290
  94.6 18.6 %all_to_all.42 = bf16[16,64,128]{2,1,0:T(8,128)(2,1)S(1)} all-to-all(bf16[16,64,128]{2,1,0:T(8,128)(2,1)S(1)} %get-tuple-element.42), channel_id=1, replica_groups=mesh['zlo'=2,'x'=4,'core'=2,'zhi'=4,'y'=4] {'x','y'}, dimensions={0} | all-to-all | bytes 524288 | tf_op jit(solution)/shard_map/all_to_all | solution.py:219
  113.4 12.7 %all_to_all.43.smooth_ref = bf16[16,64,128]{2,1,0:T(8,128)(2,1)S(1)} all-to-all(bf16[16,64,128]{2,1,0:T(8,128)(2,1)S(1)} %broadcast_in_dim.16), channel_id=1, replica_groups=mesh['zlo'=2,'x'=4,'core'=2,'zhi'=4,'y'=4] {'zlo','core','zhi'}, dimensions={0} | all-to-all | bytes 524288 | tf_op jit(solution)/shard_map/all_to_all | solution.py:219
  126.1 2.3 %shard_map.41 = bf16[16,64,128]{2,1,0:T(8,128)(2,1)S(1)} custom-call(s32[8,256]{1,0:T(8,128)S(1)} %get-tuple-element.37.list_ref, bf16[256,128,128]{2,1,0:T(8,128)(2,1)S(1)} %get-tuple-element.38.tiles_ref, s32[16,128]{1,0:T(8,128)S(1)} %get-tuple-element.39.seeds_ref, f32[16,128]{1,0:T(8,128)S(1)} %get-tuple-element.41.scale_ref, ...), custom_call_target="tpu_custom_call" | custom-call | tf_op jit(solution)/shard_map/pallas_call | solution.py:301
  128.3 13.0 %all_to_all.44 = bf16[16,64,128]{2,1,0:T(8,128)(2,1)S(1)} all-to-all(bf16[16,64,128]{2,1,0:T(8,128)(2,1)S(1)} %shard_map.41), channel_id=1, replica_groups=mesh['zlo'=2,'x'=4,'core'=2,'zhi'=4,'y'=4] {'x','y'}, dimensions={0} | all-to-all | bytes 524288 | tf_op jit(solution)/shard_map/all_to_all | solution.py:219
  141.4 13.8 %all_to_all.45.smooth_ref = bf16[16,64,128]{2,1,0:T(8,128)(2,1)S(1)} all-to-all(bf16[16,64,128]{2,1,0:T(8,128)(2,1)S(1)} %broadcast_in_dim.17), channel_id=1, replica_groups=mesh['zlo'=2,'x'=4,'core'=2,'zhi'=4,'y'=4] {'zlo','core','zhi'}, dimensions={0} | all-to-all | bytes 524288 | tf_op jit(solution)/shard_map/all_to_all | solution.py:219
  155.3 0.0 copy-start.2
  155.3 2.3 %shard_map.42 = bf16[16,64,128]{2,1,0:T(8,128)(2,1)S(1)} custom-call(s32[8,256]{1,0:T(8,128)S(1)} %get-tuple-element.37.list_ref, bf16[256,128,128]{2,1,0:T(8,128)(2,1)S(1)} %get-tuple-element.38.tiles_ref, s32[16,128]{1,0:T(8,128)S(1)} %get-tuple-element.39.seeds_ref, f32[16,128]{1,0:T(8,128)S(1)} %get-tuple-element.41.scale_ref, ...), custom_call_target="tpu_custom_call" | custom-call | tf_op jit(solution)/shard_map/pallas_call | solution.py:301
  157.5 13.0 %all_to_all.46 = bf16[16,64,128]{2,1,0:T(8,128)(2,1)S(1)} all-to-all(bf16[16,64,128]{2,1,0:T(8,128)(2,1)S(1)} %shard_map.42), channel_id=1, replica_groups=mesh['zlo'=2,'x'=4,'core'=2,'zhi'=4,'y'=4] {'x','y'}, dimensions={0} | all-to-all | bytes 524288 | tf_op jit(solution)/shard_map/all_to_all | solution.py:219
  170.5 0.0 copy-done.2
  170.6 0.6 fusion
  (12 shorter events, 0.3 us)
Async XLA Ops:
  4.8 7.2 %copy-start.1 = (bf16[128,768]{1,0:T(8,128)(2,1)S(1)}, bf16[128,768]{1,0:T(8,128)(2,1)}, u32[]{:S(2)}) copy-start(bf16[128,768]{1,0:T(8,128)(2,1)} %get-tuple-element.31) | copy-start | bytes 589828
  4.8 50.0 %copy-start = (f32[1,128]{1,0:T(1,128)S(1)}, f32[1,128]{1,0:T(1,128)}, u32[]{:S(2)}) copy-start(f32[1,128]{1,0:T(1,128)} %get-tuple-element.34.seeds_ref) | copy-start | bytes 1540
  4.8 50.0 %all-to-all-start = ((bf16[16,776,128]{2,1,0:T(8,128)(2,1)}), bf16[16,776,128]{2,1,0:T(8,128)(2,1)S(1)}, u32[]{:S(2)}, u32[]{:S(2)}) async-start(bf16[16,776,128]{2,1,0:T(8,128)(2,1)} %broadcast_in_dim.13), calls=%async_computation | async-start | bytes 6356992 | tf_op jit(solution)/shard_map/all_to_all | solution.py:219
  35.0 16.3 %collective-permute-start.1 = (bf16[4,128,768]{2,1,0:T(8,128)(2,1)}, bf16[4,128,768]{2,1,0:T(8,128)(2,1)}, u32[]{:S(2)}, u32[]{:S(2)}) collective-permute-start(bf16[4,128,768]{2,1,0:T(8,128)(2,1)} %bitcast.10.own_ref), channel_id=1, source_target_pairs={{0,128},{128,0},{1,129},{129,1},{2,130},{130,2},{3,131},{131,3},{4... | collective-permute-start | bytes 2359304 | tf_op jit(solution)/shard_map/ppermute | solution.py:255
  36.1 15.3 %collective-permute-start = (bf16[4,128,768]{2,1,0:T(8,128)(2,1)}, bf16[4,128,768]{2,1,0:T(8,128)(2,1)}, u32[]{:S(2)}, u32[]{:S(2)}) collective-permute-start(bf16[4,128,768]{2,1,0:T(8,128)(2,1)} %bitcast.10.own_ref), channel_id=1, source_target_pairs={{0,16},{16,0},{1,17},{17,1},{2,18},{18,2},{3,19},{19,3},{4,20},{20... | collective-permute-start | bytes 2359304 | tf_op jit(solution)/shard_map/ppermute | solution.py:254
  51.3 2.6 %collective-permute-start.2 = (bf16[4,128,768]{2,1,0:T(8,128)(2,1)}, bf16[4,128,768]{2,1,0:T(8,128)(2,1)}, u32[]{:S(2)}, u32[]{:S(2)}) collective-permute-start(bf16[4,128,768]{2,1,0:T(8,128)(2,1)} %collective-permute-done.1.far_ref), channel_id=1, source_target_pairs={{0,16},{16,0},{1,17},{17,1},{2,18},{18,2},{3,19},{19,3},{4,20},{20... | collective-permute-start | bytes 2359304 | tf_op jit(solution)/shard_map/ppermute | solution.py:256
  155.3 15.3 %copy-start.2 = (s32[128]{0:T(128)S(1)}, s32[128]{0:T(128)}, u32[]{:S(2)}) copy-start(s32[128]{0:T(128)} %param.5) | copy-start | bytes 1540

commit v7 on v6

--- a/solution.py
+++ b/solution.py
@@ -19,7 +19,7 @@
 BLOCKS = GROUP * GROUP
 ROWS = 128
 FEAT = 768
-EXTRA = 8
+EXTRA = 24
 FOLDS = FEAT // ROWS
 CHUNK = 8
 VMEM = pl.BlockSpec(memory_space=pltpu.VMEM)
@@ -27,12 +27,10 @@
 ANY = pl.BlockSpec(memory_space=pl.ANY)
 
 
-def prep_kernel(emb_hbm, slots_hbm, seeds_hbm, block_ref, folded_ref, seeds_out,
-                emb_ref, slots_ref, seeds_ref, emb_sem, slots_sem, seeds_sem):
+def prep_kernel(emb_hbm, slots_hbm, folded_ref, bits_ref, emb_ref, slots_ref, emb_sem, slots_sem):
     copies = [
         pltpu.make_async_copy(emb_hbm, emb_ref, emb_sem),
         pltpu.make_async_copy(slots_hbm, slots_ref, slots_sem),
-        pltpu.make_async_copy(seeds_hbm, seeds_ref, seeds_sem),
     ]
     for copy in copies:
         copy.start()
@@ -41,35 +39,35 @@
     features = emb_ref[...].astype(jnp.float32)
     norm = lax.rsqrt(jnp.sum(features * features, axis=1, keepdims=True) + EPSILON)
     normed = (features * norm).astype(jnp.bfloat16)
-    block_ref[...] = normed
     for k in range(FOLDS):
         folded_ref[k * ROWS : (k + 1) * ROWS, :] = normed[:, k * ROWS : (k + 1) * ROWS]
     first, second = slots_ref[0:1, :], slots_ref[1:2, :]
     ids = jnp.where(first >= 0, first * GROUP + second, -1)
     hits = (lax.broadcasted_iota(jnp.int32, (BLOCKS, 32), 0) == ids).astype(jnp.float32)
     bits = lax.dot_general(
-        jnp.ones((EXTRA, 32), jnp.float32), hits, (((1,), (1,)), ((), ())),
+        jnp.ones((8, 32), jnp.float32), hits, (((1,), (1,)), ((), ())),
         preferred_element_type=jnp.float32,
     )
-    row = lax.broadcasted_iota(jnp.int32, (EXTRA, ROWS), 0)
-    folded_ref[FEAT:, :] = jnp.where(row < 4, bits[:, :ROWS], bits[:, ROWS:]).astype(jnp.bfloat16)
-    seeds_out[...] = seeds_ref[...].astype(jnp.float32)
-
-
-def relay_kernel(place_ref, plane_ref, seeds_ref, out_ref):
+    row = lax.broadcasted_iota(jnp.int32, (8, ROWS), 0)
+    bits_ref[...] = jnp.where(row < 4, bits[:, :ROWS], bits[:, ROWS:]).astype(jnp.bfloat16)
+
+
+def relay_kernel(place_ref, folded_ref, bits_ref, seeds_ref, out_ref):
     x, y = place_ref[0], place_ref[1]
-    row = lax.broadcasted_iota(jnp.int32, (EXTRA, BLOCKS), 0)
-    passed = jnp.zeros((EXTRA, BLOCKS), jnp.float32)
+    out_ref[:FEAT, :] = folded_ref[...]
+    row = lax.broadcasted_iota(jnp.int32, (8, ROWS), 0)
+    ahead = jnp.zeros((8, ROWS), jnp.float32)
+    back = jnp.zeros((8, ROWS), jnp.float32)
     for k in range(4):
-        for at, line in ((k * 4 + y, k), (x * 4 + k, 4 + k)):
-            note = plane_ref[at, FEAT:, :].astype(jnp.float32)
-            note = jnp.concatenate([note[0:1], note[4:5]], axis=1)
-            passed = jnp.where(row == line, note, passed)
-    out_ref[:, :BLOCKS] = passed
-    out_ref[:, BLOCKS:] = jnp.broadcast_to(seeds_ref[...], (EXTRA, ROWS))
-
-
-def make_list(place_ref, notes_ref, list_v):
+        note = bits_ref[k * 4 + y].astype(jnp.float32)
+        ahead = jnp.where(row == 2 * k, note[0:1], jnp.where(row == 2 * k + 1, note[4:5], ahead))
+        note = bits_ref[x * 4 + k].astype(jnp.float32)
+        back = jnp.where(row == 2 * k, note[0:1], jnp.where(row == 2 * k + 1, note[4:5], back))
+    seeds = jnp.broadcast_to(seeds_ref[...].astype(jnp.float32), (8, ROWS))
+    out_ref[FEAT:, :] = jnp.concatenate([ahead, back, seeds], axis=0).astype(jnp.bfloat16)
+
+
+def make_list(place_ref, notes, list_v):
     x, y, zlo, core, zhi = (place_ref[k] for k in range(5))
     shape = (BLOCKS, BLOCKS)
     row = lax.broadcasted_iota(jnp.int32, shape, 0)
@@ -80,11 +78,16 @@
     b_zlo, b_x, b_core = (lane >> 3) & 1, (lane >> 1) & 3, lane & 1
     forward = (a_zhi == zhi) & (b_x == x) & (a_y == v_y) & (b_zlo == v_zlo) & (b_core == v_core)
     mirror = (a_zhi == u_zhi) & (a_y == y) & (b_zlo == zlo) & (b_x == u_x) & (b_core == core)
-    ahead = []
-    for u in range(GROUP):
-        note = notes_ref[zlo * 8 + core * 4 + u // 4, u % 4 : u % 4 + 1, :BLOCKS]
-        ahead.append(jnp.broadcast_to(note, (GROUP, BLOCKS)))
-    back = [notes_ref[at * 4 + zhi, 4:8, :BLOCKS] for at in range(4)]
+    ahead, back = [], []
+    for part in range(4):
+        note = notes[part].astype(jnp.float32)
+        for k in range(4):
+            full = jnp.concatenate([note[2 * k : 2 * k + 1], note[2 * k + 1 : 2 * k + 2]], axis=1)
+            ahead.append(jnp.broadcast_to(full, (GROUP, BLOCKS)))
+        note = notes[(part ^ (place_ref[5] >> 2)) * 4 + zhi].astype(jnp.float32)
+        for k in range(4, 8):
+            full = jnp.concatenate([note[2 * k : 2 * k + 1], note[2 * k + 1 : 2 * k + 2]], axis=1)
+            back.append(full)
     ahead = jnp.concatenate(ahead, axis=0)
     back = jnp.concatenate(back * GROUP, axis=0)
     hits = jnp.where(forward, ahead, 0.0) + jnp.where(mirror, back, 0.0)
@@ -97,34 +100,47 @@
         preferred_element_type=jnp.float32,
     )
     spot = jnp.where(lane.astype(jnp.float32) == upto - 1.0, live, 0.0)
-    slot_lane = lax.broadcasted_iota(jnp.int32, (EXTRA, BLOCKS), 1)
+    slot_lane = lax.broadcasted_iota(jnp.int32, (8, BLOCKS), 1)
     code = (
         (((slot_lane >> 4) & 3) * 4 + (slot_lane & 3)) * GROUP
         + ((slot_lane >> 3) & 1) * 8 + ((slot_lane >> 2) & 1) * 4 + (slot_lane >> 6)
     ).astype(jnp.float32).astype(jnp.bfloat16)
-    ones = jnp.ones((EXTRA, BLOCKS), jnp.bfloat16)
+    ones = jnp.ones((8, BLOCKS), jnp.bfloat16)
     codes = jnp.dot(code, spot.astype(jnp.bfloat16), preferred_element_type=jnp.float32)
     weights = jnp.dot(ones, (spot * counts).astype(jnp.bfloat16), preferred_element_type=jnp.float32)
     found = jnp.dot(ones, live.astype(jnp.bfloat16), preferred_element_type=jnp.float32)
-    line = lax.broadcasted_iota(jnp.int32, (EXTRA, BLOCKS), 0)
+    line = lax.broadcasted_iota(jnp.int32, (8, BLOCKS), 0)
     table = jnp.where(line == 0, codes, jnp.where(line == 1, weights, found))
     list_v[...] = (table + 0.5).astype(jnp.int32)
 
 
-def build_kernel(place_ref, notes_ref, plane_ref, own_ref, mate_ref, far_ref, far_mate_ref,
-                 tiles_ref, list_ref, deg_ref, seeds_ref, line_v, sums, list_v, list_sem, line_sem):
+def unfold(blocks, at):
+    return jnp.concatenate([blocks[at, f * ROWS : (f + 1) * ROWS, :] for f in range(FOLDS)], axis=1)
+
+
+def build_kernel(place_ref, plane_ref, own_ref, mate_ref, far_ref, far_mate_ref,
+                 tiles_ref, list_ref, deg_ref, seeds_ref, line_v, notes, sums, list_v, list_sem, line_sem, notes_sem):
     planes = place_ref[5] & 12
+    arrays = tuple(enumerate((own_ref, mate_ref, far_ref, far_mate_ref)))
+    extras = [
+        pltpu.make_async_copy(
+            part.at[:, pl.ds(FEAT, EXTRA)], notes.at[pl.ds(at * 4, 4)], notes_sem
+        )
+        for at, part in arrays
+    ]
     parts = [
-        pltpu.make_async_copy(part, line_v.at[pl.ds(at * 4, 4)], line_sem)
-        for at, part in enumerate((own_ref, mate_ref, far_ref, far_mate_ref))
+        pltpu.make_async_copy(part.at[:, pl.ds(0, FEAT)], line_v.at[pl.ds(at * 4, 4)], line_sem)
+        for at, part in arrays
     ]
-    for part in parts:
-        part.start()
-    make_list(place_ref, notes_ref, list_v)
+    for copy in extras + parts:
+        copy.start()
+    for copy in extras:
+        copy.wait()
+    make_list(place_ref, notes, list_v)
     list_copy = pltpu.make_async_copy(list_v, list_ref, list_sem)
     list_copy.start()
     for b in range(GROUP):
-        seeds_ref[b : b + 1, :] = notes_ref[b, 0:1, BLOCKS:].astype(jnp.int32)
+        seeds_ref[b : b + 1, :] = notes[b ^ planes, GROUP:, :].astype(jnp.float32)[0:1].astype(jnp.int32)
     sums[...] = jnp.zeros_like(sums)
     sharpness = FEAT**0.5
     diag_slot = place_ref[6]
@@ -143,11 +159,8 @@
             a, b = slot >> 4, slot & 15
             weight = list_ref[1, at].astype(jnp.float32)
             off = jnp.where(slot == diag_slot, weight, 0.0)
-            left = jnp.concatenate(
-                [plane_ref[a, f * ROWS : (f + 1) * ROWS, :] for f in range(FOLDS)], axis=1
-            )
             scores = lax.dot_general(
-                line_v[b ^ planes], left, (((1,), (1,)), ((), ())),
+                unfold(line_v, b ^ planes), unfold(plane_ref, a), (((1,), (1,)), ((), ())),
                 preferred_element_type=jnp.float32,
             )
             tile = jnp.exp(sharpness * (scores - 1.0)) * (weight - on_diag * off)
@@ -231,56 +244,56 @@
     x, y, zlo, core, zhi = (lax.axis_index(name) for name in ("x", "y", "zlo", "core", "zhi"))
     mine = zlo * 8 + core * 4 + zhi
     place = jnp.stack([x, y, zlo, core, zhi, mine, (x * 4 + y) * GROUP + mine]).astype(jnp.int32)
-    block, folded, own_seeds = call(
+    folded, bits = call(
         prep_kernel,
-        (
-            array(ROWS, FEAT, dtype=jnp.bfloat16),
-            array(FEAT + EXTRA, ROWS, dtype=jnp.bfloat16),
-            array(1, ROWS),
-        ),
-        [ANY] * 3,
-        (VMEM,) * 3,
+        (array(FEAT, ROWS, dtype=jnp.bfloat16), array(8, ROWS, dtype=jnp.bfloat16)),
+        [ANY] * 2,
+        (VMEM,) * 2,
         (
             pltpu.VMEM((ROWS, FEAT), jnp.bfloat16),
             pltpu.VMEM((2, 32), jnp.int32),
-            pltpu.VMEM((1, ROWS), jnp.int32),
-        )
-        + (pltpu.SemaphoreType.DMA,) * 3,
+            pltpu.SemaphoreType.DMA,
+            pltpu.SemaphoreType.DMA,
+        ),
         limit=60,
-    )(embeddings, tile_list.reshape(-1, 2).T, seeds[None, :])
-
+    )(embeddings, tile_list.reshape(-1, 2).T)
+    bits = gather(bits, PLANE)
+    folded, bits = lax.optimization_barrier((folded, bits))
+
+    block = call(
+        relay_kernel,
+        array(FEAT + EXTRA, ROWS, dtype=jnp.bfloat16),
+        [SMEM] + [VMEM] * 3,
+        VMEM,
+        limit=60,
+    )(place, folded, bits, seeds[None, :])
     plane = gather(folded, PLANE)
-    own = lax.all_gather(block, "zhi")
+    own = pltpu.with_memory_space_constraint(lax.all_gather(block, "zhi"), pltpu.HBM)
     mate = lax.ppermute(own, "core", pairs(2, 1))
     far = lax.ppermute(own, "zlo", pairs(2, 1))
     far_mate = lax.ppermute(far, "core", pairs(2, 1))
-    plane, own_seeds, place, mate, far_mate = lax.optimization_barrier(
-        (plane, own_seeds, place, mate, far_mate)
-    )
-    note = call(
-        relay_kernel, array(EXTRA, BLOCKS + ROWS), [SMEM, VMEM, VMEM], VMEM, limit=4
-    )(place, plane, own_seeds)
-    notes = gather(note, LINE)
 
     tiles, listing, partial_degree, line_seeds = call(
         build_kernel,
         (
             array(BLOCKS, ROWS, ROWS, dtype=jnp.bfloat16),
-            array(EXTRA, BLOCKS, dtype=jnp.int32),
+            array(8, BLOCKS, dtype=jnp.int32),
             array(GROUP, ROWS),
             array(GROUP, ROWS, dtype=jnp.int32),
         ),
-        [SMEM] + [VMEM] * 2 + [ANY] * 4,
+        [SMEM, VMEM] + [ANY] * 4,
         (VMEM, SMEM, VMEM, VMEM),
         (
-            pltpu.VMEM((GROUP, ROWS, FEAT), jnp.bfloat16),
+            pltpu.VMEM((GROUP, FEAT, ROWS), jnp.bfloat16),
+            pltpu.VMEM((GROUP, EXTRA, ROWS), jnp.bfloat16),
             pltpu.VMEM((GROUP, ROWS, ROWS), jnp.float32),
-            pltpu.VMEM((EXTRA, BLOCKS), jnp.int32),
+            pltpu.VMEM((8, BLOCKS), jnp.int32),
+            pltpu.SemaphoreType.DMA,
             pltpu.SemaphoreType.DMA,
             pltpu.SemaphoreType.DMA,
         ),
         limit=14,
-    )(place, notes, plane, own, mate, far, far_mate)
+    )(place, plane, own, mate, far, far_mate)
 
     scratch = (
         pltpu.VMEM((GROUP, CLASSES, ROWS), jnp.float32),

time: 174 us -> 171 us (0.983)
  local copies, waits for them, and re-layouts: 3.2 us -> 7.13 us
  waiting for transfers between devices: 18.6 us -> 15.4 us
  starting transfers between devices: 8.27 us -> 5.95 us
  blocking collectives: 124 us -> 122 us
    all_to_all x1, starting transfers between devices: 7.17 us -> 3.74 us  [exchange(): return lax.all_to_all(blocks, axes, 0, 0)]
    unnamed x6 -> x10, local copies, waits for them, and re-layouts: 0.01 us -> 2.5 us
    ppermute x1, waiting for transfers between devices: 2.54 us -> 0.61 us  [local(): far_mate = lax.ppermute(far, 'core', pairs(2, 1))]
  transfers between devices with their start and end apart: 4 -> 4, of which waited for: 3 -> 2; matrix products, arithmetic and copies ran while one was open for 0% -> 0% of each run, Pallas kernels for 0% -> 1%
where the time goes in v7:
time: 171 us; the launch traced here: 169 us
  blocking collectives  122 us (71%)
  Pallas kernels  17.4 us (10%)
  waiting for transfers between devices  15.4 us (9%)
  local copies, waits for them, and re-layouts  7.13 us (4%)
  starting transfers between devices  5.95 us (3%)
    all_to_all x7, blocking collectives, exchange(): return lax.all_to_all(blocks, axes, 0, 0)  101 us
    all_gather x1, blocking collectives, local(): lax.all_gather(block, 'zhi')  21.7 us
    ppermute x1, waiting for transfers between devices, local(): far = lax.ppermute(own, 'zlo', pairs(2, 1))  14.8 us
    pallas_call x1, Pallas kernels, local(): call(build_kernel, (array(BLOCKS, ROWS, ROWS, dtype=jnp.bfloat16), array(...  7.8 us
    pallas_call x2, Pallas kernels, local(): call(next_kernel, sums_out, [SMEM] + [VMEM] * 4, VMEM, scratch, limit=6)  4.14 us
    broadcast_in_dim x5, local copies, waits for them, and re-layouts, gather(): return exchange(jnp.broadcast_to(block[None], (GROUP,) + block.shape), axes)  3.96 us
    all_to_all x1, starting transfers between devices, exchange(): return lax.all_to_all(blocks, axes, 0, 0)  3.74 us
  transfers between devices with their start and end apart: 4, of which 2 were waited for; matrix products, arithmetic and copies ran while one was open for 0% of the time, Pallas kernels for 1%

profile of v7, /device:TPU:32, one launch (start us, length us, event | category | flops | bytes accessed | tf_op | source)
XLA Modules:
  0.0 169.1 jit_solution(434388457255264354)
XLA Ops:
  0.0 1.8 %shard_map.37 = (bf16[768,128]{1,0:T(8,128)(2,1)}, bf16[8,128]{1,0:T(8,128)(2,1)}) custom-call(bf16[128,768]{1,0:T(8,128)(2,1)} %emb_hbm.1, s32[2,32]{1,0:T(2,128)} %bitcast.26), custom_call_target="tpu_custom_call" | custom-call | tf_op jit(solution)/shard_map/pallas_call | solution.py:247
  1.8 0.7 broadcast_in_dim.12
  2.5 14.6 %all_to_all.40.bits_ref = bf16[16,8,128]{2,1,0:T(8,128)(2,1)} all-to-all(bf16[16,8,128]{2,1,0:T(8,128)(2,1)S(1)} %broadcast_in_dim.12), channel_id=1, replica_groups=mesh['zlo'=2,'x'=4,'core'=2,'zhi'=4,'y'=4] {'x','y'}, dimensions={0} | all-to-all | bytes 65536 | tf_op jit(solution)/shard_map/all_to_all | solution.py:232
  17.0 3.2 %broadcast_in_dim.13 = bf16[16,768,128]{2,1,0:T(8,128)(2,1)} broadcast(bf16[768,128]{1,0:T(8,128)(2,1)} %get-tuple-element.27.folded_ref), dimensions={1,2} | broadcast | bytes 3342336 | tf_op jit(solution)/shard_map/broadcast_in_dim | solution.py:236
  20.2 3.7 %all-to-all-start.1 = ((bf16[16,768,128]{2,1,0:T(8,128)(2,1)}), bf16[16,768,128]{2,1,0:T(8,128)(2,1)S(1)}, u32[]{:S(2)}, u32[]{:S(2)}) async-start(bf16[16,768,128]{2,1,0:T(8,128)(2,1)} %broadcast_in_dim.13), calls=%async_computation.1 | async-start | bytes 6291456 | tf_op jit(solution)/shard_map/all_to_all | solution.py:232
  24.0 0.7 stack.31.place_ref
  24.6 1.7 shard_map.38
  26.3 21.7 %all-gather = bf16[3168,128]{1,0:T(8,128)(2,1)S(1)} all-gather(bf16[792,128]{1,0:T(8,128)(2,1)} %shard_map.38), channel_id=2, replica_groups=mesh['zlo'=2,'x'=4,'core'=2,'zhi'=4,'y'=4] {'zhi'}, dimensions={0}, use_global_device_ids=true | all-gather | bytes 1013760 | tf_op jit(solution)/shard_map/all_gather | solution.py:271
  48.0 0.0 copy-start.1
  48.0 2.2 %collective-permute-start.1 = (bf16[4,792,128]{2,1,0:T(8,128)(2,1)S(1)}, bf16[4,792,128]{2,1,0:T(8,128)(2,1)S(1)}, u32[]{:S(2)}, u32[]{:S(2)}) collective-permute-start(bf16[4,792,128]{2,1,0:T(8,128)(2,1)S(1)} %bitcast.22), channel_id=1, source_target_pairs={{0,128},{128,0},{1,129},{129,1},{2,130},{130,2},{3,131},{131,3},{4... | collective-permute-start | bytes 2433032 | tf_op jit(solution)/shard_map/ppermute | solution.py:273
  50.2 0.0 collective-permute-start
  50.2 14.8 %collective-permute-done.1.far_ref = bf16[4,792,128]{2,1,0:T(8,128)(2,1)S(1)} collective-permute-done((bf16[4,792,128]{2,1,0:T(8,128)(2,1)S(1)}, bf16[4,792,128]{2,1,0:T(8,128)(2,1)S(1)}, u32[]{:S(2)}, u32[]{:S(2)}) %collective-permute-start.1) | collective-permute-done | bytes 811040 | tf_op jit(solution)/shard_map/ppermute | solution.py:273
  65.0 0.0 copy-start.2
  65.0 0.0 collective-permute-start.2
  65.0 0.0 collective-permute-done.mate_ref
  65.0 0.0 copy-done.1
  65.0 0.9 copy-done.2
  65.9 0.0 copy-start.3
  65.9 0.9 copy-done.3
  66.9 0.6 collective-permute-done.2.far_mate_ref
  67.5 0.0 all-to-all-done.1.plane_ref
  67.5 0.0 copy-start
  67.5 0.7 copy-done
  68.1 7.8 %shard_map.39 = (bf16[256,128,128]{2,1,0:T(8,128)(2,1)S(1)}, s32[8,256]{1,0:T(8,128)S(1)}, f32[16,128]{1,0:T(8,128)S(1)}, s32[16,128]{1,0:T(8,128)S(1)}) custom-call(s32[7]{0:T(128)S(1)} %copy-done, bf16[16,768,128]{2,1,0:T(8,128)(2,1)S(1)} %all-to-all-done.1.plane_ref, bf16[4,792,128]{2,1,0:T(8,128)(2,1)} %bitcast.24, bf16[4,792,128]{2,1,0:T(8,128)(2,1)} %copy-done.3, ...), custom_call_target="tpu_custom_call" | custom-call | tf_op jit(solution)/shard_map/pallas_call | solution.py:276
  76.0 14.7 %all_to_all.41.parts_ref = f32[16,16,128]{2,1,0:T(8,128)S(1)} all-to-all(f32[16,16,128]{2,1,0:T(8,128)S(1)} %broadcast_in_dim.15), channel_id=1, replica_groups=mesh['zlo'=2,'x'=4,'core'=2,'zhi'=4,'y'=4] {'zlo','core','zhi'}, dimensions={0} | all-to-all | bytes 262144 | tf_op jit(solution)/shard_map/all_to_all | solution.py:232
  90.7 2.0 %shard_map.40 = (bf16[16,64,128]{2,1,0:T(8,128)(2,1)S(1)}, f32[16,128]{1,0:T(8,128)S(1)}, f32[1,128]{1,0:T(1,128)S(1)}) custom-call(s32[7]{0:T(128)S(1)} %copy-done, s32[8,256]{1,0:T(8,128)S(1)} %get-tuple-element.29.list_ref, bf16[256,128,128]{2,1,0:T(8,128)(2,1)S(1)} %get-tuple-element.30.tiles_ref, s32[16,128]{1,0:T(8,128)S(1)} %get-tuple-element.31.seeds_ref, ...), custom_call_target="tpu_custom_call" | custom-call | tf_op jit(solution)/shard_map/pallas_call | solution.py:303
  92.8 18.1 %all_to_all.42 = bf16[16,64,128]{2,1,0:T(8,128)(2,1)S(1)} all-to-all(bf16[16,64,128]{2,1,0:T(8,128)(2,1)S(1)} %get-tuple-element.34), channel_id=1, replica_groups=mesh['zlo'=2,'x'=4,'core'=2,'zhi'=4,'y'=4] {'x','y'}, dimensions={0} | all-to-all | bytes 524288 | tf_op jit(solution)/shard_map/all_to_all | solution.py:232
  111.0 12.6 %all_to_all.43.smooth_ref = bf16[16,64,128]{2,1,0:T(8,128)(2,1)S(1)} all-to-all(bf16[16,64,128]{2,1,0:T(8,128)(2,1)S(1)} %broadcast_in_dim.16), channel_id=1, replica_groups=mesh['zlo'=2,'x'=4,'core'=2,'zhi'=4,'y'=4] {'zlo','core','zhi'}, dimensions={0} | all-to-all | bytes 524288 | tf_op jit(solution)/shard_map/all_to_all | solution.py:232
  123.5 2.1 %shard_map.41 = bf16[16,64,128]{2,1,0:T(8,128)(2,1)S(1)} custom-call(s32[8,256]{1,0:T(8,128)S(1)} %get-tuple-element.29.list_ref, bf16[256,128,128]{2,1,0:T(8,128)(2,1)S(1)} %get-tuple-element.30.tiles_ref, s32[16,128]{1,0:T(8,128)S(1)} %get-tuple-element.31.seeds_ref, f32[16,128]{1,0:T(8,128)S(1)} %get-tuple-element.33.scale_ref, ...), custom_call_target="tpu_custom_call" | custom-call | tf_op jit(solution)/shard_map/pallas_call | solution.py:314
  125.6 13.2 %all_to_all.44 = bf16[16,64,128]{2,1,0:T(8,128)(2,1)S(1)} all-to-all(bf16[16,64,128]{2,1,0:T(8,128)(2,1)S(1)} %shard_map.41), channel_id=1, replica_groups=mesh['zlo'=2,'x'=4,'core'=2,'zhi'=4,'y'=4] {'x','y'}, dimensions={0} | all-to-all | bytes 524288 | tf_op jit(solution)/shard_map/all_to_all | solution.py:232
  139.0 14.1 %all_to_all.45.smooth_ref = bf16[16,64,128]{2,1,0:T(8,128)(2,1)S(1)} all-to-all(bf16[16,64,128]{2,1,0:T(8,128)(2,1)S(1)} %broadcast_in_dim.17), channel_id=1, replica_groups=mesh['zlo'=2,'x'=4,'core'=2,'zhi'=4,'y'=4] {'zlo','core','zhi'}, dimensions={0} | all-to-all | bytes 524288 | tf_op jit(solution)/shard_map/all_to_all | solution.py:232
  153.1 0.0 copy-start.4
  153.1 2.1 %shard_map.42 = bf16[16,64,128]{2,1,0:T(8,128)(2,1)S(1)} custom-call(s32[8,256]{1,0:T(8,128)S(1)} %get-tuple-element.29.list_ref, bf16[256,128,128]{2,1,0:T(8,128)(2,1)S(1)} %get-tuple-element.30.tiles_ref, s32[16,128]{1,0:T(8,128)S(1)} %get-tuple-element.31.seeds_ref, f32[16,128]{1,0:T(8,128)S(1)} %get-tuple-element.33.scale_ref, ...), custom_call_target="tpu_custom_call" | custom-call | tf_op jit(solution)/shard_map/pallas_call | solution.py:314
  155.2 13.2 %all_to_all.46 = bf16[16,64,128]{2,1,0:T(8,128)(2,1)S(1)} all-to-all(bf16[16,64,128]{2,1,0:T(8,128)(2,1)S(1)} %shard_map.42), channel_id=1, replica_groups=mesh['zlo'=2,'x'=4,'core'=2,'zhi'=4,'y'=4] {'x','y'}, dimensions={0} | all-to-all | bytes 524288 | tf_op jit(solution)/shard_map/all_to_all | solution.py:232
  168.5 0.0 copy-done.4
  168.5 0.6 fusion
  (11 shorter events, 0.2 us)
Async XLA Ops:
  20.2 47.3 %all-to-all-start.1 = ((bf16[16,768,128]{2,1,0:T(8,128)(2,1)}), bf16[16,768,128]{2,1,0:T(8,128)(2,1)S(1)}, u32[]{:S(2)}, u32[]{:S(2)}) async-start(bf16[16,768,128]{2,1,0:T(8,128)(2,1)} %broadcast_in_dim.13), calls=%async_computation.1 | async-start | bytes 6291456 | tf_op jit(solution)/shard_map/all_to_all | solution.py:232
  48.0 17.0 %copy-start.1 = (bf16[3168,128]{1,0:T(8,128)(2,1)}, bf16[3168,128]{1,0:T(8,128)(2,1)S(1)}, u32[]{:S(2)}) copy-start(bf16[3168,128]{1,0:T(8,128)(2,1)S(1)} %all-gather) | copy-start | bytes 2433028
  48.0 17.0 %collective-permute-start.1 = (bf16[4,792,128]{2,1,0:T(8,128)(2,1)S(1)}, bf16[4,792,128]{2,1,0:T(8,128)(2,1)S(1)}, u32[]{:S(2)}, u32[]{:S(2)}) collective-permute-start(bf16[4,792,128]{2,1,0:T(8,128)(2,1)S(1)} %bitcast.22), channel_id=1, source_target_pairs={{0,128},{128,0},{1,129},{129,1},{2,130},{130,2},{3,131},{131,3},{4... | collective-permute-start | bytes 2433032 | tf_op jit(solution)/shard_map/ppermute | solution.py:273
  50.2 14.8 %collective-permute-start = (bf16[4,792,128]{2,1,0:T(8,128)(2,1)S(1)}, bf16[4,792,128]{2,1,0:T(8,128)(2,1)S(1)}, u32[]{:S(2)}, u32[]{:S(2)}) collective-permute-start(bf16[4,792,128]{2,1,0:T(8,128)(2,1)S(1)} %bitcast.23), channel_id=1, source_target_pairs={{0,16},{16,0},{1,17},{17,1},{2,18},{18,2},{3,19},{19,3},{4,20},{20... | collective-permute-start | bytes 2433032 | tf_op jit(solution)/shard_map/ppermute | solution.py:272
  65.0 0.9 copy-start.2
  65.0 2.5 %collective-permute-start.2 = (bf16[4,792,128]{2,1,0:T(8,128)(2,1)S(1)}, bf16[4,792,128]{2,1,0:T(8,128)(2,1)}, u32[]{:S(2)}, u32[]{:S(2)}) collective-permute-start(bf16[4,792,128]{2,1,0:T(8,128)(2,1)S(1)} %collective-permute-done.1.far_ref), channel_id=1, source_target_pairs={{0,16},{16,0},{1,17},{17,1},{2,18},{18,2},{3,19},{19,3},{4,20},{20... | collective-permute-start | bytes 2433032 | tf_op jit(solution)/shard_map/ppermute | solution.py:274
  65.9 0.9 copy-start.3
  67.5 0.7 copy-start
  153.1 15.4 %copy-start.4 = (s32[128]{0:T(128)S(1)}, s32[128]{0:T(128)}, u32[]{:S(2)}) copy-start(s32[128]{0:T(128)} %param.5) | copy-start | bytes 1540

commit v8 on v7

--- a/solution.py
+++ b/solution.py
@@ -27,7 +27,13 @@
 ANY = pl.BlockSpec(memory_space=pl.ANY)
 
 
-def prep_kernel(emb_hbm, slots_hbm, folded_ref, bits_ref, emb_ref, slots_ref, emb_sem, slots_sem):
+def position():
+    x, y, zlo, core, zhi = (lax.axis_index(name) for name in ("x", "y", "zlo", "core", "zhi"))
+    return x, y, zlo, core, zhi, zlo * 8 + core * 4 + zhi
+
+
+def prep_kernel(emb_hbm, slots_hbm, folded_ref, copies_ref, bits_ref,
+                emb_ref, slots_ref, emb_sem, slots_sem, out_sem):
     copies = [
         pltpu.make_async_copy(emb_hbm, emb_ref, emb_sem),
         pltpu.make_async_copy(slots_hbm, slots_ref, slots_sem),
@@ -41,6 +47,9 @@
     normed = (features * norm).astype(jnp.bfloat16)
     for k in range(FOLDS):
         folded_ref[k * ROWS : (k + 1) * ROWS, :] = normed[:, k * ROWS : (k + 1) * ROWS]
+    sends = [pltpu.make_async_copy(folded_ref, copies_ref.at[k], out_sem) for k in range(GROUP)]
+    for send in sends:
+        send.start()
     first, second = slots_ref[0:1, :], slots_ref[1:2, :]
     ids = jnp.where(first >= 0, first * GROUP + second, -1)
     hits = (lax.broadcasted_iota(jnp.int32, (BLOCKS, 32), 0) == ids).astype(jnp.float32)
@@ -49,11 +58,14 @@
         preferred_element_type=jnp.float32,
     )
     row = lax.broadcasted_iota(jnp.int32, (8, ROWS), 0)
-    bits_ref[...] = jnp.where(row < 4, bits[:, :ROWS], bits[:, ROWS:]).astype(jnp.bfloat16)
-
-
-def relay_kernel(place_ref, folded_ref, bits_ref, seeds_ref, out_ref):
-    x, y = place_ref[0], place_ref[1]
+    halves = jnp.where(row < 4, bits[:, :ROWS], bits[:, ROWS:]).astype(jnp.bfloat16)
+    bits_ref[...] = jnp.broadcast_to(halves[None], (GROUP, 8, ROWS))
+    for send in sends:
+        send.wait()
+
+
+def relay_kernel(folded_ref, bits_ref, seeds_ref, out_ref):
+    x, y, *_ = position()
     out_ref[:FEAT, :] = folded_ref[...]
     row = lax.broadcasted_iota(jnp.int32, (8, ROWS), 0)
     ahead = jnp.zeros((8, ROWS), jnp.float32)
@@ -67,8 +79,8 @@
     out_ref[FEAT:, :] = jnp.concatenate([ahead, back, seeds], axis=0).astype(jnp.bfloat16)
 
 
-def make_list(place_ref, notes, list_v):
-    x, y, zlo, core, zhi = (place_ref[k] for k in range(5))
+def make_list(notes, list_v):
+    x, y, zlo, core, zhi, mine = position()
     shape = (BLOCKS, BLOCKS)
     row = lax.broadcasted_iota(jnp.int32, shape, 0)
     lane = lax.broadcasted_iota(jnp.int32, shape, 1)
@@ -84,7 +96,7 @@
         for k in range(4):
             full = jnp.concatenate([note[2 * k : 2 * k + 1], note[2 * k + 1 : 2 * k + 2]], axis=1)
             ahead.append(jnp.broadcast_to(full, (GROUP, BLOCKS)))
-        note = notes[(part ^ (place_ref[5] >> 2)) * 4 + zhi].astype(jnp.float32)
+        note = notes[(part ^ (mine >> 2)) * 4 + zhi].astype(jnp.float32)
         for k in range(4, 8):
             full = jnp.concatenate([note[2 * k : 2 * k + 1], note[2 * k + 1 : 2 * k + 2]], axis=1)
             back.append(full)
@@ -118,9 +130,10 @@
     return jnp.concatenate([blocks[at, f * ROWS : (f + 1) * ROWS, :] for f in range(FOLDS)], axis=1)
 
 
-def build_kernel(place_ref, plane_ref, own_ref, mate_ref, far_ref, far_mate_ref,
+def build_kernel(plane_ref, own_ref, mate_ref, far_ref, far_mate_ref,
                  tiles_ref, list_ref, deg_ref, seeds_ref, line_v, notes, sums, list_v, list_sem, line_sem, notes_sem):
-    planes = place_ref[5] & 12
+    x, y, *_, mine = position()
+    planes = mine & 12
     arrays = tuple(enumerate((own_ref, mate_ref, far_ref, far_mate_ref)))
     extras = [
         pltpu.make_async_copy(
@@ -136,14 +149,14 @@
         copy.start()
     for copy in extras:
         copy.wait()
-    make_list(place_ref, notes, list_v)
+    make_list(notes, list_v)
     list_copy = pltpu.make_async_copy(list_v, list_ref, list_sem)
     list_copy.start()
     for b in range(GROUP):
         seeds_ref[b : b + 1, :] = notes[b ^ planes, GROUP:, :].astype(jnp.float32)[0:1].astype(jnp.int32)
     sums[...] = jnp.zeros_like(sums)
     sharpness = FEAT**0.5
-    diag_slot = place_ref[6]
+    diag_slot = (x * 4 + y) * GROUP + mine
     on_diag = (
         lax.broadcasted_iota(jnp.int32, (ROWS, ROWS), 0)
         == lax.broadcasted_iota(jnp.int32, (ROWS, ROWS), 1)
@@ -194,22 +207,26 @@
     return classes == seeds_ref[b : b + 1, :]
 
 
-def first_kernel(place_ref, list_ref, tiles_ref, seeds_ref, parts_ref,
+def first_kernel(list_ref, tiles_ref, seeds_ref, parts_ref,
                  out_ref, scale_ref, own_ref, total, spread):
     scale_ref[...] = lax.rsqrt(jnp.sum(parts_ref[...], axis=0))
-    own_ref[...] = scale_ref[pl.ds(place_ref[5], 1), :]
+    own_ref[...] = scale_ref[pl.ds(position()[5], 1), :]
     for b in range(GROUP):
         seeded = jnp.where(seeded_block(seeds_ref, b), scale_ref[b : b + 1, :], 0.0)
         spread[b] = seeded.astype(jnp.bfloat16)
     run_apply(list_ref, tiles_ref, out_ref, total, spread)
 
 
-def next_kernel(list_ref, tiles_ref, seeds_ref, scale_ref, smooth_ref, out_ref, total, spread):
-    for b in range(GROUP):
-        seed_part = jnp.where(
-            seeded_block(seeds_ref, b), (1.0 - BLEND) * scale_ref[b : b + 1, :], 0.0
-        )
-        spread[b] = (smooth_ref[b].astype(jnp.float32) + seed_part).astype(jnp.bfloat16)
+def next_kernel(list_ref, tiles_ref, seeds_ref, scale_ref, own_ref, mate_ref,
+                out_ref, total, spread):
+    core = lax.axis_index("core")
+    classes = lax.broadcasted_iota(jnp.int32, (CLASSES, ROWS), 0)
+    for k in range(GROUP // 2):
+        for smooth_ref, side in ((own_ref, core), (mate_ref, 1 - core)):
+            b = (k // 4) * 8 + side * 4 + k % 4
+            seeded = classes == seeds_ref[pl.ds(b, 1), :]
+            seed_part = jnp.where(seeded, (1.0 - BLEND) * scale_ref[pl.ds(b, 1), :], 0.0)
+            spread[b] = (smooth_ref[k].astype(jnp.float32) + seed_part).astype(jnp.bfloat16)
     run_apply(list_ref, tiles_ref, out_ref, total, spread)
 
 
@@ -232,8 +249,8 @@
     return lax.all_to_all(blocks, axes, 0, 0)
 
 
-def gather(block, axes):
-    return exchange(jnp.broadcast_to(block[None], (GROUP,) + block.shape), axes)
+def gather(block, axes, count=GROUP):
+    return exchange(jnp.broadcast_to(block[None], (count,) + block.shape), axes)
 
 
 def pairs(count, step):
@@ -241,33 +258,35 @@
 
 
 def local(embeddings, tile_list, seeds):
-    x, y, zlo, core, zhi = (lax.axis_index(name) for name in ("x", "y", "zlo", "core", "zhi"))
-    mine = zlo * 8 + core * 4 + zhi
-    place = jnp.stack([x, y, zlo, core, zhi, mine, (x * 4 + y) * GROUP + mine]).astype(jnp.int32)
-    folded, bits = call(
+    folded, copies, bits = call(
         prep_kernel,
-        (array(FEAT, ROWS, dtype=jnp.bfloat16), array(8, ROWS, dtype=jnp.bfloat16)),
+        (
+            array(FEAT, ROWS, dtype=jnp.bfloat16),
+            array(GROUP, FEAT, ROWS, dtype=jnp.bfloat16),
+            array(GROUP, 8, ROWS, dtype=jnp.bfloat16),
+        ),
         [ANY] * 2,
-        (VMEM,) * 2,
+        (VMEM, ANY, VMEM),
         (
             pltpu.VMEM((ROWS, FEAT), jnp.bfloat16),
             pltpu.VMEM((2, 32), jnp.int32),
             pltpu.SemaphoreType.DMA,
             pltpu.SemaphoreType.DMA,
+            pltpu.SemaphoreType.DMA,
         ),
         limit=60,
     )(embeddings, tile_list.reshape(-1, 2).T)
-    bits = gather(bits, PLANE)
-    folded, bits = lax.optimization_barrier((folded, bits))
+    bits = exchange(bits, PLANE)
+    copies, bits = lax.optimization_barrier((copies, bits))
 
     block = call(
         relay_kernel,
         array(FEAT + EXTRA, ROWS, dtype=jnp.bfloat16),
-        [SMEM] + [VMEM] * 3,
+        [VMEM] * 3,
         VMEM,
-        limit=60,
-    )(place, folded, bits, seeds[None, :])
-    plane = gather(folded, PLANE)
+        limit=4,
+    )(folded, bits, seeds[None, :])
+    plane = exchange(copies, PLANE)
     own = pltpu.with_memory_space_constraint(lax.all_gather(block, "zhi"), pltpu.HBM)
     mate = lax.ppermute(own, "core", pairs(2, 1))
     far = lax.ppermute(own, "zlo", pairs(2, 1))
@@ -281,7 +300,7 @@
             array(GROUP, ROWS),
             array(GROUP, ROWS, dtype=jnp.int32),
         ),
-        [SMEM, VMEM] + [ANY] * 4,
+        [VMEM] + [ANY] * 4,
         (VMEM, SMEM, VMEM, VMEM),
         (
             pltpu.VMEM((GROUP, FEAT, ROWS), jnp.bfloat16),
@@ -293,7 +312,7 @@
             pltpu.SemaphoreType.DMA,
         ),
         limit=14,
-    )(place, plane, own, mate, far, far_mate)
+    )(plane, own, mate, far, far_mate)
 
     scratch = (
         pltpu.VMEM((GROUP, CLASSES, ROWS), jnp.float32),
@@ -303,17 +322,18 @@
     partial, scale, own_scale = call(
         first_kernel,
         (sums_out, array(GROUP, ROWS), array(1, ROWS)),
-        [SMEM, SMEM, VMEM, VMEM, VMEM],
+        [SMEM, VMEM, VMEM, VMEM],
         (VMEM,) * 3,
         scratch,
         limit=6,
-    )(place, listing, tiles, line_seeds, gather(partial_degree, LINE))
+    )(listing, tiles, line_seeds, gather(partial_degree, LINE))
     for sweep in range(3):
         if sweep:
-            smooth = gather((BLEND * own_scale * own_scale * summed).astype(jnp.bfloat16), LINE)
+            smooth = (BLEND * own_scale * own_scale * summed).astype(jnp.bfloat16)
+            smooth = gather(smooth, ("zlo", "zhi"), GROUP // 2)
             partial = call(
-                next_kernel, sums_out, [SMEM] + [VMEM] * 4, VMEM, scratch, limit=6
-            )(listing, tiles, line_seeds, scale, smooth)
+                next_kernel, sums_out, [SMEM] + [VMEM] * 5, VMEM, scratch, limit=6
+            )(listing, tiles, line_seeds, scale, smooth, lax.ppermute(smooth, "core", pairs(2, 1)))
         summed, own_scale, seeds = lax.optimization_barrier((exchange(partial, PLANE), own_scale, seeds))
         summed = jnp.sum(summed.astype(jnp.float32), axis=0)
     seeded = seeds[None, :] == jnp.arange(CLASSES, dtype=jnp.int32)[:, None]

time: 171 us -> 162 us (0.947)
  blocking collectives: 122 us -> 114 us
  local copies, waits for them, and re-layouts: 7.13 us -> 1.89 us
  waiting for transfers between devices: 15.4 us -> 18.5 us
  Pallas kernels: 17.4 us -> 19.4 us
    all_to_all x7, blocking collectives: 101 us -> 93 us  [exchange(): return lax.all_to_all(blocks, axes, 0, 0)]
    broadcast_in_dim x5 -> x3, local copies, waits for them, and re-layouts: 3.96 us -> 0.05 us  [gather(): return exchange(jnp.broadcast_to(block[None], (count,) + block.shape), axes)]
    ppermute x0 -> x2, waiting for transfers between devices: none -> 2.69 us  [local(): lax.ppermute(smooth, 'core', pairs(2, 1))]
  transfers between devices with their start and end apart: 4 -> 6, of which waited for: 2 -> 5; matrix products, arithmetic and copies ran while one was open for 0% -> 0% of each run, Pallas kernels for 1% -> 0%
where the time goes in v8:
time: 162 us; the launch traced here: 161 us
  blocking collectives  114 us (70%)
  Pallas kernels  19.4 us (12%)
  waiting for transfers between devices  18.5 us (11%)
  starting transfers between devices  6.12 us (4%)
  local copies, waits for them, and re-layouts  1.89 us (1%)
    all_to_all x7, blocking collectives, exchange(): return lax.all_to_all(blocks, axes, 0, 0)  93 us
    all_gather x1, blocking collectives, local(): lax.all_gather(block, 'zhi')  21.5 us
    ppermute x1, waiting for transfers between devices, local(): far = lax.ppermute(own, 'zlo', pairs(2, 1))  14.8 us
    pallas_call x1, Pallas kernels, local(): call(build_kernel, (array(BLOCKS, ROWS, ROWS, dtype=jnp.bfloat16), array(...  8.47 us
    pallas_call x2, Pallas kernels, local(): call(next_kernel, sums_out, [SMEM] + [VMEM] * 5, VMEM, scratch, limit=6)  5 us
    all_to_all x1, starting transfers between devices, exchange(): return lax.all_to_all(blocks, axes, 0, 0)  3.87 us
    pallas_call x1, Pallas kernels, local(): call(prep_kernel, (array(FEAT, ROWS, dtype=jnp.bfloat16), array(GROUP, FE...  3.42 us
  transfers between devices with their start and end apart: 6, of which 5 were waited for; matrix products, arithmetic and copies ran while one was open for 0% of the time, Pallas kernels for 0%

profile of v8, /device:TPU:32, one launch (start us, length us, event | category | flops | bytes accessed | tf_op | source)
XLA Modules:
  0.0 161.3 jit_solution(12058187299961384532)
XLA Ops:
  0.0 3.4 %shard_map.37 = (bf16[768,128]{1,0:T(8,128)(2,1)}, bf16[16,768,128]{2,1,0:T(8,128)(2,1)}, bf16[16,8,128]{2,1,0:T(8,128)(2,1)}) custom-call(bf16[128,768]{1,0:T(8,128)(2,1)} %emb_hbm.1, s32[2,32]{1,0:T(2,128)} %bitcast.19), custom_call_target="tpu_custom_call" | custom-call | tf_op jit(solution)/shard_map/pallas_call | solution.py:261
  3.4 14.7 %all_to_all.40.bits_ref = bf16[16,8,128]{2,1,0:T(8,128)(2,1)S(1)} all-to-all(bf16[16,8,128]{2,1,0:T(8,128)(2,1)} %get-tuple-element.27), channel_id=1, replica_groups=mesh['zlo'=2,'x'=4,'core'=2,'zhi'=4,'y'=4] {'x','y'}, dimensions={0} | all-to-all | bytes 65536 | tf_op jit(solution)/shard_map/all_to_all | solution.py:249
  18.1 0.0 copy-start
  18.1 0.0 copy-start.1
  18.1 3.9 %all-to-all-start.1 = ((bf16[16,768,128]{2,1,0:T(8,128)(2,1)}), bf16[16,768,128]{2,1,0:T(8,128)(2,1)S(1)}, u32[]{:S(2)}, u32[]{:S(2)}) async-start(bf16[16,768,128]{2,1,0:T(8,128)(2,1)} %get-tuple-element.28), calls=%async_computation.1 | async-start | bytes 6291456 | tf_op jit(solution)/shard_map/all_to_all | solution.py:249
  22.0 0.0 copy-done
  22.0 0.0 copy-done.1
  22.0 21.5 %all-gather = bf16[3168,128]{1,0:T(8,128)(2,1)S(1)} all-gather(bf16[792,128]{1,0:T(8,128)(2,1)S(1)} %shard_map.38), channel_id=2, replica_groups=mesh['zlo'=2,'x'=4,'core'=2,'zhi'=4,'y'=4] {'zhi'}, dimensions={0}, use_global_device_ids=true | all-gather | bytes 1013760 | tf_op jit(solution)/shard_map/all_gather | solution.py:290
  43.5 0.0 copy-start.2
  43.5 2.2 %collective-permute-start.1 = (bf16[4,792,128]{2,1,0:T(8,128)(2,1)S(1)}, bf16[4,792,128]{2,1,0:T(8,128)(2,1)S(1)}, u32[]{:S(2)}, u32[]{:S(2)}) collective-permute-start(bf16[4,792,128]{2,1,0:T(8,128)(2,1)S(1)} %bitcast.16), channel_id=1, source_target_pairs={{0,128},{128,0},{1,129},{129,1},{2,130},{130,2},{3,131},{131,3},{4... | collective-permute-start | bytes 2433032 | tf_op jit(solution)/shard_map/ppermute | solution.py:292
  45.8 0.0 collective-permute-start
  45.8 14.8 %collective-permute-done.1.far_ref = bf16[4,792,128]{2,1,0:T(8,128)(2,1)S(1)} collective-permute-done((bf16[4,792,128]{2,1,0:T(8,128)(2,1)S(1)}, bf16[4,792,128]{2,1,0:T(8,128)(2,1)S(1)}, u32[]{:S(2)}, u32[]{:S(2)}) %collective-permute-start.1) | collective-permute-done | bytes 811040 | tf_op jit(solution)/shard_map/ppermute | solution.py:292
  60.6 0.0 copy-start.3
  60.6 0.0 collective-permute-start.2
  60.6 0.0 collective-permute-done.mate_ref
  60.6 0.0 copy-done.2
  60.6 0.9 copy-done.3
  61.5 0.0 copy-start.4
  61.5 0.9 copy-done.4
  62.4 0.6 collective-permute-done.2.far_mate_ref
  63.0 0.4 all-to-all-done.1.plane_ref
  63.5 8.5 %shard_map.39 = (bf16[256,128,128]{2,1,0:T(8,128)(2,1)S(1)}, s32[8,256]{1,0:T(8,128)S(1)}, f32[16,128]{1,0:T(8,128)S(1)}, s32[16,128]{1,0:T(8,128)S(1)}) custom-call(bf16[16,768,128]{2,1,0:T(8,128)(2,1)S(1)} %all-to-all-done.1.plane_ref, bf16[4,792,128]{2,1,0:T(8,128)(2,1)} %bitcast.18, bf16[4,792,128]{2,1,0:T(8,128)(2,1)} %copy-done.4, ...), custom_call_target="tpu_custom_call" | custom-call | tf_op jit(solution)/shard_map/pallas_call | solution.py:295
  71.9 15.0 %all_to_all.41.parts_ref = f32[16,16,128]{2,1,0:T(8,128)S(1)} all-to-all(f32[16,16,128]{2,1,0:T(8,128)S(1)} %broadcast_in_dim.9), channel_id=1, replica_groups=mesh['zlo'=2,'x'=4,'core'=2,'zhi'=4,'y'=4] {'zlo','core','zhi'}, dimensions={0} | all-to-all | bytes 262144 | tf_op jit(solution)/shard_map/all_to_all | solution.py:249
  86.9 2.5 %shard_map.40 = (bf16[16,64,128]{2,1,0:T(8,128)(2,1)S(1)}, f32[16,128]{1,0:T(8,128)S(1)}, f32[1,128]{1,0:T(1,128)S(1)}) custom-call(s32[8,256]{1,0:T(8,128)S(1)} %get-tuple-element.31.list_ref, bf16[256,128,128]{2,1,0:T(8,128)(2,1)S(1)} %get-tuple-element.32.tiles_ref, s32[16,128]{1,0:T(8,128)S(1)} %get-tuple-element.33.seeds_ref, ...), custom_call_target="tpu_custom_call" | custom-call | tf_op jit(solution)/shard_map/pallas_call | solution.py:322
  89.4 16.1 %all_to_all.42 = bf16[16,64,128]{2,1,0:T(8,128)(2,1)S(1)} all-to-all(bf16[16,64,128]{2,1,0:T(8,128)(2,1)S(1)} %get-tuple-element.36), channel_id=1, replica_groups=mesh['zlo'=2,'x'=4,'core'=2,'zhi'=4,'y'=4] {'x','y'}, dimensions={0} | all-to-all | bytes 524288 | tf_op jit(solution)/shard_map/all_to_all | solution.py:249
  105.6 10.8 %all_to_all.43.own_ref = bf16[8,64,128]{2,1,0:T(8,128)(2,1)S(1)} all-to-all(bf16[8,64,128]{2,1,0:T(8,128)(2,1)S(1)} %broadcast_in_dim.10), channel_id=1, replica_groups=mesh['zlo'=2,'x'=4,'core'=2,'zhi'=4,'y'=4] {'zlo','zhi'}, dimensions={0} | all-to-all | bytes 262144 | tf_op jit(solution)/shard_map/all_to_all | solution.py:249
  116.4 0.0 collective-permute-start.3
  116.4 1.3 collective-permute-done.3.mate_ref
  117.7 2.5 %shard_map.41 = bf16[16,64,128]{2,1,0:T(8,128)(2,1)S(1)} custom-call(s32[8,256]{1,0:T(8,128)S(1)} %get-tuple-element.31.list_ref, bf16[256,128,128]{2,1,0:T(8,128)(2,1)S(1)} %get-tuple-element.32.tiles_ref, s32[16,128]{1,0:T(8,128)S(1)} %get-tuple-element.33.seeds_ref, f32[16,128]{1,0:T(8,128)S(1)} %get-tuple-element.35.scale_ref, ...), custom_call_target="tpu_custom_call" | custom-call | tf_op jit(solution)/shard_map/pallas_call | solution.py:334
  120.2 12.9 %all_to_all.44 = bf16[16,64,128]{2,1,0:T(8,128)(2,1)S(1)} all-to-all(bf16[16,64,128]{2,1,0:T(8,128)(2,1)S(1)} %shard_map.41), channel_id=1, replica_groups=mesh['zlo'=2,'x'=4,'core'=2,'zhi'=4,'y'=4] {'x','y'}, dimensions={0} | all-to-all | bytes 524288 | tf_op jit(solution)/shard_map/all_to_all | solution.py:249
  133.2 10.7 %all_to_all.45.own_ref = bf16[8,64,128]{2,1,0:T(8,128)(2,1)S(1)} all-to-all(bf16[8,64,128]{2,1,0:T(8,128)(2,1)S(1)} %broadcast_in_dim.11), channel_id=1, replica_groups=mesh['zlo'=2,'x'=4,'core'=2,'zhi'=4,'y'=4] {'zlo','zhi'}, dimensions={0} | all-to-all | bytes 262144 | tf_op jit(solution)/shard_map/all_to_all | solution.py:249
  143.9 0.0 collective-permute-start.4
  143.9 1.3 collective-permute-done.4.mate_ref
  145.2 2.5 %shard_map.42 = bf16[16,64,128]{2,1,0:T(8,128)(2,1)S(1)} custom-call(s32[8,256]{1,0:T(8,128)S(1)} %get-tuple-element.31.list_ref, bf16[256,128,128]{2,1,0:T(8,128)(2,1)S(1)} %get-tuple-element.32.tiles_ref, s32[16,128]{1,0:T(8,128)S(1)} %get-tuple-element.33.seeds_ref, f32[16,128]{1,0:T(8,128)S(1)} %get-tuple-element.35.scale_ref, ...), custom_call_target="tpu_custom_call" | custom-call | tf_op jit(solution)/shard_map/pallas_call | solution.py:334
  147.8 12.9 %all_to_all.46 = bf16[16,64,128]{2,1,0:T(8,128)(2,1)S(1)} all-to-all(bf16[16,64,128]{2,1,0:T(8,128)(2,1)S(1)} %shard_map.42), channel_id=1, replica_groups=mesh['zlo'=2,'x'=4,'core'=2,'zhi'=4,'y'=4] {'x','y'}, dimensions={0} | all-to-all | bytes 524288 | tf_op jit(solution)/shard_map/all_to_all | solution.py:249
  160.7 0.6 fusion
  (12 shorter events, 0.2 us)
Async XLA Ops:
  18.1 3.9 %copy-start = (bf16[768,128]{1,0:T(8,128)(2,1)S(1)}, bf16[768,128]{1,0:T(8,128)(2,1)}, u32[]{:S(2)}) copy-start(bf16[768,128]{1,0:T(8,128)(2,1)} %get-tuple-element.29.folded_ref) | copy-start | bytes 589828
  18.1 3.9 %copy-start.1 = (s32[128]{0:T(128)S(1)}, s32[128]{0:T(128)}, u32[]{:S(2)}) copy-start(s32[128]{0:T(128)} %param.5) | copy-start | bytes 1540
  18.1 45.3 %all-to-all-start.1 = ((bf16[16,768,128]{2,1,0:T(8,128)(2,1)}), bf16[16,768,128]{2,1,0:T(8,128)(2,1)S(1)}, u32[]{:S(2)}, u32[]{:S(2)}) async-start(bf16[16,768,128]{2,1,0:T(8,128)(2,1)} %get-tuple-element.28), calls=%async_computation.1 | async-start | bytes 6291456 | tf_op jit(solution)/shard_map/all_to_all | solution.py:249
  43.5 17.0 %copy-start.2 = (bf16[3168,128]{1,0:T(8,128)(2,1)}, bf16[3168,128]{1,0:T(8,128)(2,1)S(1)}, u32[]{:S(2)}) copy-start(bf16[3168,128]{1,0:T(8,128)(2,1)S(1)} %all-gather) | copy-start | bytes 2433028
  43.5 17.0 %collective-permute-start.1 = (bf16[4,792,128]{2,1,0:T(8,128)(2,1)S(1)}, bf16[4,792,128]{2,1,0:T(8,128)(2,1)S(1)}, u32[]{:S(2)}, u32[]{:S(2)}) collective-permute-start(bf16[4,792,128]{2,1,0:T(8,128)(2,1)S(1)} %bitcast.16), channel_id=1, source_target_pairs={{0,128},{128,0},{1,129},{129,1},{2,130},{130,2},{3,131},{131,3},{4... | collective-permute-start | bytes 2433032 | tf_op jit(solution)/shard_map/ppermute | solution.py:292
  45.8 14.8 %collective-permute-start = (bf16[4,792,128]{2,1,0:T(8,128)(2,1)S(1)}, bf16[4,792,128]{2,1,0:T(8,128)(2,1)S(1)}, u32[]{:S(2)}, u32[]{:S(2)}) collective-permute-start(bf16[4,792,128]{2,1,0:T(8,128)(2,1)S(1)} %bitcast.17), channel_id=1, source_target_pairs={{0,16},{16,0},{1,17},{17,1},{2,18},{18,2},{3,19},{19,3},{4,20},{20... | collective-permute-start | bytes 2433032 | tf_op jit(solution)/shard_map/ppermute | solution.py:291
  60.6 0.9 copy-start.3
  60.6 2.5 %collective-permute-start.2 = (bf16[4,792,128]{2,1,0:T(8,128)(2,1)S(1)}, bf16[4,792,128]{2,1,0:T(8,128)(2,1)}, u32[]{:S(2)}, u32[]{:S(2)}) collective-permute-start(bf16[4,792,128]{2,1,0:T(8,128)(2,1)S(1)} %collective-permute-done.1.far_ref), channel_id=1, source_target_pairs={{0,16},{16,0},{1,17},{17,1},{2,18},{18,2},{3,19},{19,3},{4,20},{20... | collective-permute-start | bytes 2433032 | tf_op jit(solution)/shard_map/ppermute | solution.py:293
  61.5 0.9 copy-start.4
  116.4 1.3 collective-permute-start.3
  143.9 1.3 collective-permute-start.4

commit v9 on v8

--- a/solution.py
+++ b/solution.py
@@ -5,6 +5,7 @@
 from jax.experimental.pallas import tpu as pltpu
 from jax.sharding import Mesh
 from jax.sharding import PartitionSpec as P
+
 
 CLASSES = 64
 BLEND = 0.8
@@ -59,24 +60,26 @@
     )
     row = lax.broadcasted_iota(jnp.int32, (8, ROWS), 0)
     halves = jnp.where(row < 4, bits[:, :ROWS], bits[:, ROWS:]).astype(jnp.bfloat16)
-    bits_ref[...] = jnp.broadcast_to(halves[None], (GROUP, 8, ROWS))
+    bits_ref[...] = halves
     for send in sends:
         send.wait()
 
 
-def relay_kernel(folded_ref, bits_ref, seeds_ref, out_ref):
+def relay_kernel(folded_ref, seeds_ref, bits_ref, *refs):
     x, y, *_ = position()
+    out_ref = refs[6]
     out_ref[:FEAT, :] = folded_ref[...]
     row = lax.broadcasted_iota(jnp.int32, (8, ROWS), 0)
-    ahead = jnp.zeros((8, ROWS), jnp.float32)
-    back = jnp.zeros((8, ROWS), jnp.float32)
-    for k in range(4):
-        note = bits_ref[k * 4 + y].astype(jnp.float32)
-        ahead = jnp.where(row == 2 * k, note[0:1], jnp.where(row == 2 * k + 1, note[4:5], ahead))
-        note = bits_ref[x * 4 + k].astype(jnp.float32)
-        back = jnp.where(row == 2 * k, note[0:1], jnp.where(row == 2 * k + 1, note[4:5], back))
-    seeds = jnp.broadcast_to(seeds_ref[...].astype(jnp.float32), (8, ROWS))
-    out_ref[FEAT:, :] = jnp.concatenate([ahead, back, seeds], axis=0).astype(jnp.bfloat16)
+    groups = []
+    for own, others in ((x, refs[:3]), (y, refs[3:6])):
+        rows = jnp.zeros((8, ROWS), jnp.float32)
+        for step, ref in enumerate((bits_ref, *others)):
+            at = 2 * (own ^ step)
+            note = ref[...].astype(jnp.float32)
+            rows = jnp.where(row == at, note[0:1], jnp.where(row == at + 1, note[4:5], rows))
+        groups.append(rows)
+    groups.append(jnp.broadcast_to(seeds_ref[...].astype(jnp.float32), (8, ROWS)))
+    out_ref[FEAT:, :] = jnp.concatenate(groups, axis=0).astype(jnp.bfloat16)
 
 
 def make_list(notes, list_v):
@@ -263,7 +266,7 @@
         (
             array(FEAT, ROWS, dtype=jnp.bfloat16),
             array(GROUP, FEAT, ROWS, dtype=jnp.bfloat16),
-            array(GROUP, 8, ROWS, dtype=jnp.bfloat16),
+            array(8, ROWS, dtype=jnp.bfloat16),
         ),
         [ANY] * 2,
         (VMEM, ANY, VMEM),
@@ -276,17 +279,18 @@
         ),
         limit=60,
     )(embeddings, tile_list.reshape(-1, 2).T)
-    bits = exchange(bits, PLANE)
-    copies, bits = lax.optimization_barrier((copies, bits))
-
+    others = []
+    for axis in PLANE:
+        for step in (1, 2, 3):
+            others.append(lax.ppermute(bits, axis, pairs(4, step)))
+    plane = exchange(copies, PLANE)
     block = call(
         relay_kernel,
         array(FEAT + EXTRA, ROWS, dtype=jnp.bfloat16),
-        [VMEM] * 3,
+        [VMEM] * 9,
         VMEM,
         limit=4,
-    )(folded, bits, seeds[None, :])
-    plane = exchange(copies, PLANE)
+    )(folded, seeds[None, :], bits, *others)
     own = pltpu.with_memory_space_constraint(lax.all_gather(block, "zhi"), pltpu.HBM)
     mate = lax.ppermute(own, "core", pairs(2, 1))
     far = lax.ppermute(own, "zlo", pairs(2, 1))

time: 162 us -> 191 us (1.18)
  waiting for transfers between devices: 18.5 us -> 44.8 us
  starting transfers between devices: 6.12 us -> 25 us
  blocking collectives: 114 us -> 102 us
  Pallas kernels: 19.4 us -> 15.7 us
    ppermute x0 -> x6, waiting for transfers between devices: none -> 26.1 us  [local(): others.append(lax.ppermute(bits, axis, pairs(4, step)))]
    ppermute x0 -> x6, starting transfers between devices: none -> 15.6 us  [local(): others.append(lax.ppermute(bits, axis, pairs(4, step)))]
    all_to_all x7 -> x6, blocking collectives: 93 us -> 81.2 us  [exchange(): return lax.all_to_all(blocks, axes, 0, 0)]
    all_to_all x1, starting transfers between devices: 3.87 us -> 7.18 us  [exchange(): return lax.all_to_all(blocks, axes, 0, 0)]
  transfers between devices with their start and end apart: 6 -> 12, of which waited for: 5 -> 7; matrix products, arithmetic and copies ran while one was open for 0% -> 0% of each run, Pallas kernels for 0% -> 0%
where the time goes in v9:
time: 191 us
  blocking collectives  102 us (53%)
  waiting for transfers between devices  44.8 us (23%)
  starting transfers between devices  25 us (13%)
  Pallas kernels  15.7 us (8%)
    all_to_all x6, blocking collectives, exchange(): return lax.all_to_all(blocks, axes, 0, 0)  81.2 us
    ppermute x6, waiting for transfers between devices, local(): others.append(lax.ppermute(bits, axis, pairs(4, step)))  26.1 us
    all_gather x1, blocking collectives, local(): lax.all_gather(block, 'zhi')  21.3 us
    ppermute x6, starting transfers between devices, local(): others.append(lax.ppermute(bits, axis, pairs(4, step)))  15.6 us
    ppermute x1, waiting for transfers between devices, local(): far = lax.ppermute(own, 'zlo', pairs(2, 1))  15.4 us
    all_to_all x1, starting transfers between devices, exchange(): return lax.all_to_all(blocks, axes, 0, 0)  7.18 us
    pallas_call x1, Pallas kernels, local(): call(build_kernel, (array(BLOCKS, ROWS, ROWS, dtype=jnp.bfloat16), array(...  6.72 us
  transfers between devices with their start and end apart: 12, of which 7 were waited for; matrix products, arithmetic and copies ran while one was open for 0% of the time, Pallas kernels for 0%

profile of v9, /device:TPU:32, one launch (start us, length us, event | category | flops | bytes accessed | tf_op | source)
XLA Modules:
  0.0 190.8 jit_solution(12424107943353164304)
XLA Ops:
  0.0 3.4 %shard_map.37 = (bf16[768,128]{1,0:T(8,128)(2,1)}, bf16[16,768,128]{2,1,0:T(8,128)(2,1)}, bf16[8,128]{1,0:T(8,128)(2,1)}) custom-call(bf16[128,768]{1,0:T(8,128)(2,1)} %emb_hbm.1, s32[2,32]{1,0:T(2,128)} %bitcast.19), custom_call_target="tpu_custom_call" | custom-call | tf_op jit(solution)/shard_map/pallas_call | solution.py:264
  3.4 0.0 copy-start.1
  3.4 0.0 copy-start
  3.4 0.0 copy-start.2
  3.5 7.2 %all-to-all-start = ((bf16[16,768,128]{2,1,0:T(8,128)(2,1)}), bf16[16,768,128]{2,1,0:T(8,128)(2,1)S(1)}, u32[]{:S(2)}, u32[]{:S(2)}) async-start(bf16[16,768,128]{2,1,0:T(8,128)(2,1)} %get-tuple-element.24), calls=%async_computation | async-start | bytes 6291456 | tf_op jit(solution)/shard_map/all_to_all | solution.py:252
  10.6 0.0 copy-done.1
  10.7 3.2 %collective-permute-start.5 = (bf16[8,128]{1,0:T(8,128)(2,1)S(1)}, bf16[8,128]{1,0:T(8,128)(2,1)S(1)}, u32[]{:S(2)}, u32[]{:S(2)}) collective-permute-start(bf16[8,128]{1,0:T(8,128)(2,1)S(1)} %copy-done.1), channel_id=1, source_target_pairs={{0,3},{1,2},{2,1},{3,0},{4,7},{5,6},{6,5},{7,4},{8,11},{9,10},{10,... | collective-permute-start | bytes 6152 | tf_op jit(solution)/shard_map/ppermute | solution.py:285
  13.9 0.9 collective-permute-start.4
  14.7 0.1 collective-permute-start.3
  14.8 3.1 %collective-permute-start.2 = (bf16[8,128]{1,0:T(8,128)(2,1)S(1)}, bf16[8,128]{1,0:T(8,128)(2,1)S(1)}, u32[]{:S(2)}, u32[]{:S(2)}) collective-permute-start(bf16[8,128]{1,0:T(8,128)(2,1)S(1)} %copy-done.1), channel_id=1, source_target_pairs={{0,96},{32,64},{64,32},{96,0},{1,97},{33,65},{65,33},{97,1},{2,98}... | collective-permute-start | bytes 6152 | tf_op jit(solution)/shard_map/ppermute | solution.py:285
  18.0 0.9 collective-permute-start.1
  18.8 16.4 %collective-permute-done.5.refs_5_ = bf16[8,128]{1,0:T(8,128)(2,1)S(1)} collective-permute-done((bf16[8,128]{1,0:T(8,128)(2,1)S(1)}, bf16[8,128]{1,0:T(8,128)(2,1)S(1)}, u32[]{:S(2)}, u32[]{:S(2)}) %collective-permute-start.5) | collective-permute-done | bytes 2080 | tf_op jit(solution)/shard_map/ppermute | solution.py:285
  35.3 7.4 %collective-permute-start = (bf16[8,128]{1,0:T(8,128)(2,1)S(1)}, bf16[8,128]{1,0:T(8,128)(2,1)S(1)}, u32[]{:S(2)}, u32[]{:S(2)}) collective-permute-start(bf16[8,128]{1,0:T(8,128)(2,1)S(1)} %copy-done.1), channel_id=1, source_target_pairs={{0,32},{32,0},{64,96},{96,64},{1,33},{33,1},{65,97},{97,65},{2,34}... | collective-permute-start | bytes 6152 | tf_op jit(solution)/shard_map/ppermute | solution.py:285
  42.7 0.0 collective-permute-done.4.refs_4_
  42.7 0.0 collective-permute-done.3.refs_3_
  42.7 4.4 %collective-permute-done.2.refs_2_ = bf16[8,128]{1,0:T(8,128)(2,1)S(1)} collective-permute-done((bf16[8,128]{1,0:T(8,128)(2,1)S(1)}, bf16[8,128]{1,0:T(8,128)(2,1)S(1)}, u32[]{:S(2)}, u32[]{:S(2)}) %collective-permute-start.2) | collective-permute-done | bytes 2080 | tf_op jit(solution)/shard_map/ppermute | solution.py:285
  47.1 5.3 %collective-permute-done.1.refs_1_ = bf16[8,128]{1,0:T(8,128)(2,1)S(1)} collective-permute-done((bf16[8,128]{1,0:T(8,128)(2,1)S(1)}, bf16[8,128]{1,0:T(8,128)(2,1)S(1)}, u32[]{:S(2)}, u32[]{:S(2)}) %collective-permute-start.1) | collective-permute-done | bytes 2080 | tf_op jit(solution)/shard_map/ppermute | solution.py:285
  52.4 0.0 collective-permute-done.refs_0_
  52.4 0.0 copy-done
  52.4 0.0 copy-done.2
  52.4 21.3 %all-gather = bf16[3168,128]{1,0:T(8,128)(2,1)S(1)} all-gather(bf16[792,128]{1,0:T(8,128)(2,1)S(1)} %shard_map.38), channel_id=2, replica_groups=mesh['zlo'=2,'x'=4,'core'=2,'zhi'=4,'y'=4] {'zhi'}, dimensions={0}, use_global_device_ids=true | all-gather | bytes 1013760 | tf_op jit(solution)/shard_map/all_gather | solution.py:294
  73.7 0.0 copy-start.3
  73.7 2.2 %collective-permute-start.7 = (bf16[4,792,128]{2,1,0:T(8,128)(2,1)S(1)}, bf16[4,792,128]{2,1,0:T(8,128)(2,1)S(1)}, u32[]{:S(2)}, u32[]{:S(2)}) collective-permute-start(bf16[4,792,128]{2,1,0:T(8,128)(2,1)S(1)} %bitcast.16), channel_id=1, source_target_pairs={{0,128},{128,0},{1,129},{129,1},{2,130},{130,2},{3,131},{131,3},{4... | collective-permute-start | bytes 2433032 | tf_op jit(solution)/shard_map/ppermute | solution.py:296
  75.9 0.0 collective-permute-start.6
  75.9 15.4 %collective-permute-done.7.far_ref = bf16[4,792,128]{2,1,0:T(8,128)(2,1)S(1)} collective-permute-done((bf16[4,792,128]{2,1,0:T(8,128)(2,1)S(1)}, bf16[4,792,128]{2,1,0:T(8,128)(2,1)S(1)}, u32[]{:S(2)}, u32[]{:S(2)}) %collective-permute-start.7) | collective-permute-done | bytes 811040 | tf_op jit(solution)/shard_map/ppermute | solution.py:296
  91.2 0.0 copy-start.4
  91.2 0.0 collective-permute-start.8
  91.2 0.0 collective-permute-done.6.mate_ref
  91.3 0.0 copy-done.3
  91.3 0.9 copy-done.4
  92.2 0.9 copy-done.5
  93.1 0.6 collective-permute-done.8.far_mate_ref
  93.7 0.0 all-to-all-done.plane_ref
  93.7 6.7 %shard_map.39 = (bf16[256,128,128]{2,1,0:T(8,128)(2,1)S(1)}, s32[8,256]{1,0:T(8,128)S(1)}, f32[16,128]{1,0:T(8,128)S(1)}, s32[16,128]{1,0:T(8,128)S(1)}) custom-call(bf16[16,768,128]{2,1,0:T(8,128)(2,1)S(1)} %all-to-all-done.plane_ref, bf16[4,792,128]{2,1,0:T(8,128)(2,1)} %bitcast.18, bf16[4,792,128]{2,1,0:T(8,128)(2,1)} %copy-done.5, ...), custom_call_target="tpu_custom_call" | custom-call | tf_op jit(solution)/shard_map/pallas_call | solution.py:299
  100.4 14.5 %all_to_all.35.parts_ref = f32[16,16,128]{2,1,0:T(8,128)S(1)} all-to-all(f32[16,16,128]{2,1,0:T(8,128)S(1)} %broadcast_in_dim.9), channel_id=1, replica_groups=mesh['zlo'=2,'x'=4,'core'=2,'zhi'=4,'y'=4] {'zlo','core','zhi'}, dimensions={0} | all-to-all | bytes 262144 | tf_op jit(solution)/shard_map/all_to_all | solution.py:252
  114.9 1.8 shard_map.40
  116.7 17.8 %all_to_all.36 = bf16[16,64,128]{2,1,0:T(8,128)(2,1)S(1)} all-to-all(bf16[16,64,128]{2,1,0:T(8,128)(2,1)S(1)} %get-tuple-element.32), channel_id=1, replica_groups=mesh['zlo'=2,'x'=4,'core'=2,'zhi'=4,'y'=4] {'x','y'}, dimensions={0} | all-to-all | bytes 524288 | tf_op jit(solution)/shard_map/all_to_all | solution.py:252
  134.7 11.2 %all_to_all.37.own_ref = bf16[8,64,128]{2,1,0:T(8,128)(2,1)S(1)} all-to-all(bf16[8,64,128]{2,1,0:T(8,128)(2,1)S(1)} %broadcast_in_dim.10), channel_id=1, replica_groups=mesh['zlo'=2,'x'=4,'core'=2,'zhi'=4,'y'=4] {'zlo','zhi'}, dimensions={0} | all-to-all | bytes 262144 | tf_op jit(solution)/shard_map/all_to_all | solution.py:252
  145.8 0.0 collective-permute-start.9
  145.8 1.3 collective-permute-done.9.mate_ref
  147.2 1.9 shard_map.41
  149.1 13.3 %all_to_all.38 = bf16[16,64,128]{2,1,0:T(8,128)(2,1)S(1)} all-to-all(bf16[16,64,128]{2,1,0:T(8,128)(2,1)S(1)} %shard_map.41), channel_id=1, replica_groups=mesh['zlo'=2,'x'=4,'core'=2,'zhi'=4,'y'=4] {'x','y'}, dimensions={0} | all-to-all | bytes 524288 | tf_op jit(solution)/shard_map/all_to_all | solution.py:252
  162.4 11.1 %all_to_all.39.own_ref = bf16[8,64,128]{2,1,0:T(8,128)(2,1)S(1)} all-to-all(bf16[8,64,128]{2,1,0:T(8,128)(2,1)S(1)} %broadcast_in_dim.11), channel_id=1, replica_groups=mesh['zlo'=2,'x'=4,'core'=2,'zhi'=4,'y'=4] {'zlo','zhi'}, dimensions={0} | all-to-all | bytes 262144 | tf_op jit(solution)/shard_map/all_to_all | solution.py:252
  173.5 0.0 collective-permute-start.10
  173.6 1.3 collective-permute-done.10.mate_ref
  174.9 1.9 shard_map.42
  176.8 13.3 %all_to_all.40 = bf16[16,64,128]{2,1,0:T(8,128)(2,1)S(1)} all-to-all(bf16[16,64,128]{2,1,0:T(8,128)(2,1)S(1)} %shard_map.42), channel_id=1, replica_groups=mesh['zlo'=2,'x'=4,'core'=2,'zhi'=4,'y'=4] {'x','y'}, dimensions={0} | all-to-all | bytes 524288 | tf_op jit(solution)/shard_map/all_to_all | solution.py:252
  190.1 0.6 fusion
  (13 shorter events, 0.2 us)
Async XLA Ops:
  3.4 7.2 %copy-start.1 = (bf16[8,128]{1,0:T(8,128)(2,1)S(1)}, bf16[8,128]{1,0:T(8,128)(2,1)}, u32[]{:S(2)}) copy-start(bf16[8,128]{1,0:T(8,128)(2,1)} %get-tuple-element.26.bits_ref) | copy-start | bytes 6148
  3.4 49.0 %copy-start = (bf16[768,128]{1,0:T(8,128)(2,1)S(1)}, bf16[768,128]{1,0:T(8,128)(2,1)}, u32[]{:S(2)}) copy-start(bf16[768,128]{1,0:T(8,128)(2,1)} %get-tuple-element.25.folded_ref) | copy-start | bytes 589828
  3.4 48.9 %copy-start.2 = (s32[128]{0:T(128)S(1)}, s32[128]{0:T(128)}, u32[]{:S(2)}) copy-start(s32[128]{0:T(128)} %param.5) | copy-start | bytes 1540
  3.5 90.2 %all-to-all-start = ((bf16[16,768,128]{2,1,0:T(8,128)(2,1)}), bf16[16,768,128]{2,1,0:T(8,128)(2,1)S(1)}, u32[]{:S(2)}, u32[]{:S(2)}) async-start(bf16[16,768,128]{2,1,0:T(8,128)(2,1)} %get-tuple-element.24), calls=%async_computation | async-start | bytes 6291456 | tf_op jit(solution)/shard_map/all_to_all | solution.py:252
  10.7 24.6 %collective-permute-start.5 = (bf16[8,128]{1,0:T(8,128)(2,1)S(1)}, bf16[8,128]{1,0:T(8,128)(2,1)S(1)}, u32[]{:S(2)}, u32[]{:S(2)}) collective-permute-start(bf16[8,128]{1,0:T(8,128)(2,1)S(1)} %copy-done.1), channel_id=1, source_target_pairs={{0,3},{1,2},{2,1},{3,0},{4,7},{5,6},{6,5},{7,4},{8,11},{9,10},{10,... | collective-permute-start | bytes 6152 | tf_op jit(solution)/shard_map/ppermute | solution.py:285
  13.9 28.8 %collective-permute-start.4 = (bf16[8,128]{1,0:T(8,128)(2,1)S(1)}, bf16[8,128]{1,0:T(8,128)(2,1)S(1)}, u32[]{:S(2)}, u32[]{:S(2)}) collective-permute-start(bf16[8,128]{1,0:T(8,128)(2,1)S(1)} %copy-done.1), channel_id=1, source_target_pairs={{0,2},{1,3},{2,0},{3,1},{4,6},{5,7},{6,4},{7,5},{8,10},{9,11},{10,... | collective-permute-start | bytes 6152 | tf_op jit(solution)/shard_map/ppermute | solution.py:285
  14.7 28.0 %collective-permute-start.3 = (bf16[8,128]{1,0:T(8,128)(2,1)S(1)}, bf16[8,128]{1,0:T(8,128)(2,1)S(1)}, u32[]{:S(2)}, u32[]{:S(2)}) collective-permute-start(bf16[8,128]{1,0:T(8,128)(2,1)S(1)} %copy-done.1), channel_id=1, source_target_pairs={{0,1},{1,0},{2,3},{3,2},{4,5},{5,4},{6,7},{7,6},{8,9},{9,8},{10,11... | collective-permute-start | bytes 6152 | tf_op jit(solution)/shard_map/ppermute | solution.py:285
  14.8 32.2 %collective-permute-start.2 = (bf16[8,128]{1,0:T(8,128)(2,1)S(1)}, bf16[8,128]{1,0:T(8,128)(2,1)S(1)}, u32[]{:S(2)}, u32[]{:S(2)}) collective-permute-start(bf16[8,128]{1,0:T(8,128)(2,1)S(1)} %copy-done.1), channel_id=1, source_target_pairs={{0,96},{32,64},{64,32},{96,0},{1,97},{33,65},{65,33},{97,1},{2,98}... | collective-permute-start | bytes 6152 | tf_op jit(solution)/shard_map/ppermute | solution.py:285
  18.0 34.4 %collective-permute-start.1 = (bf16[8,128]{1,0:T(8,128)(2,1)S(1)}, bf16[8,128]{1,0:T(8,128)(2,1)S(1)}, u32[]{:S(2)}, u32[]{:S(2)}) collective-permute-start(bf16[8,128]{1,0:T(8,128)(2,1)S(1)} %copy-done.1), channel_id=1, source_target_pairs={{0,64},{32,96},{64,0},{96,32},{1,65},{33,97},{65,1},{97,33},{2,66}... | collective-permute-start | bytes 6152 | tf_op jit(solution)/shard_map/ppermute | solution.py:285
  35.3 17.1 %collective-permute-start = (bf16[8,128]{1,0:T(8,128)(2,1)S(1)}, bf16[8,128]{1,0:T(8,128)(2,1)S(1)}, u32[]{:S(2)}, u32[]{:S(2)}) collective-permute-start(bf16[8,128]{1,0:T(8,128)(2,1)S(1)} %copy-done.1), channel_id=1, source_target_pairs={{0,32},{32,0},{64,96},{96,64},{1,33},{33,1},{65,97},{97,65},{2,34}... | collective-permute-start | bytes 6152 | tf_op jit(solution)/shard_map/ppermute | solution.py:285
  73.7 17.6 %copy-start.3 = (bf16[3168,128]{1,0:T(8,128)(2,1)}, bf16[3168,128]{1,0:T(8,128)(2,1)S(1)}, u32[]{:S(2)}) copy-start(bf16[3168,128]{1,0:T(8,128)(2,1)S(1)} %all-gather) | copy-start | bytes 2433028
  73.7 17.5 %collective-permute-start.7 = (bf16[4,792,128]{2,1,0:T(8,128)(2,1)S(1)}, bf16[4,792,128]{2,1,0:T(8,128)(2,1)S(1)}, u32[]{:S(2)}, u32[]{:S(2)}) collective-permute-start(bf16[4,792,128]{2,1,0:T(8,128)(2,1)S(1)} %bitcast.16), channel_id=1, source_target_pairs={{0,128},{128,0},{1,129},{129,1},{2,130},{130,2},{3,131},{131,3},{4... | collective-permute-start | bytes 2433032 | tf_op jit(solution)/shard_map/ppermute | solution.py:296
  75.9 15.4 %collective-permute-start.6 = (bf16[4,792,128]{2,1,0:T(8,128)(2,1)S(1)}, bf16[4,792,128]{2,1,0:T(8,128)(2,1)S(1)}, u32[]{:S(2)}, u32[]{:S(2)}) collective-permute-start(bf16[4,792,128]{2,1,0:T(8,128)(2,1)S(1)} %bitcast.17), channel_id=1, source_target_pairs={{0,16},{16,0},{1,17},{17,1},{2,18},{18,2},{3,19},{19,3},{4,20},{20... | collective-permute-start | bytes 2433032 | tf_op jit(solution)/shard_map/ppermute | solution.py:295
  91.2 0.9 copy-start.4
  91.2 2.5 %collective-permute-start.8 = (bf16[4,792,128]{2,1,0:T(8,128)(2,1)S(1)}, bf16[4,792,128]{2,1,0:T(8,128)(2,1)}, u32[]{:S(2)}, u32[]{:S(2)}) collective-permute-start(bf16[4,792,128]{2,1,0:T(8,128)(2,1)S(1)} %collective-permute-done.7.far_ref), channel_id=1, source_target_pairs={{0,16},{16,0},{1,17},{17,1},{2,18},{18,2},{3,19},{19,3},{4,20},{20... | collective-permute-start | bytes 2433032 | tf_op jit(solution)/shard_map/ppermute | solution.py:297
  92.2 0.9 copy-start.5
  145.8 1.3 collective-permute-start.9
  173.5 1.3 collective-permute-start.10

commit v10 on v9

--- a/solution.py
+++ b/solution.py
@@ -34,7 +34,7 @@
 
 
 def prep_kernel(emb_hbm, slots_hbm, folded_ref, copies_ref, bits_ref,
-                emb_ref, slots_ref, emb_sem, slots_sem, out_sem):
+                emb_ref, slots_ref, turned_ref, emb_sem, slots_sem, out_sem):
     copies = [
         pltpu.make_async_copy(emb_hbm, emb_ref, emb_sem),
         pltpu.make_async_copy(slots_hbm, slots_ref, slots_sem),
@@ -45,10 +45,12 @@
         copy.wait()
     features = emb_ref[...].astype(jnp.float32)
     norm = lax.rsqrt(jnp.sum(features * features, axis=1, keepdims=True) + EPSILON)
-    normed = (features * norm).astype(jnp.bfloat16)
+    normed = features * norm
     for k in range(FOLDS):
-        folded_ref[k * ROWS : (k + 1) * ROWS, :] = normed[:, k * ROWS : (k + 1) * ROWS]
-    sends = [pltpu.make_async_copy(folded_ref, copies_ref.at[k], out_sem) for k in range(GROUP)]
+        part = normed[:, k * ROWS : (k + 1) * ROWS]
+        folded_ref[k * ROWS : (k + 1) * ROWS, :] = part.astype(jnp.bfloat16)
+        turned_ref[k * ROWS : (k + 1) * ROWS, :] = part.T.astype(jnp.bfloat16)
+    sends = [pltpu.make_async_copy(turned_ref, copies_ref.at[k], out_sem) for k in range(GROUP)]
     for send in sends:
         send.start()
     first, second = slots_ref[0:1, :], slots_ref[1:2, :]
@@ -175,9 +177,8 @@
             a, b = slot >> 4, slot & 15
             weight = list_ref[1, at].astype(jnp.float32)
             off = jnp.where(slot == diag_slot, weight, 0.0)
-            scores = lax.dot_general(
-                unfold(line_v, b ^ planes), unfold(plane_ref, a), (((1,), (1,)), ((), ())),
-                preferred_element_type=jnp.float32,
+            scores = jnp.dot(
+                unfold(line_v, b ^ planes), plane_ref[a], preferred_element_type=jnp.float32
             )
             tile = jnp.exp(sharpness * (scores - 1.0)) * (weight - on_diag * off)
             tiles_ref[at] = tile.astype(jnp.bfloat16)
@@ -273,6 +274,7 @@
         (
             pltpu.VMEM((ROWS, FEAT), jnp.bfloat16),
             pltpu.VMEM((2, 32), jnp.int32),
+            pltpu.VMEM((FEAT, ROWS), jnp.bfloat16),
             pltpu.SemaphoreType.DMA,
             pltpu.SemaphoreType.DMA,
             pltpu.SemaphoreType.DMA,
@@ -294,6 +296,7 @@
     own = pltpu.with_memory_space_constraint(lax.all_gather(block, "zhi"), pltpu.HBM)
     mate = lax.ppermute(own, "core", pairs(2, 1))
     far = lax.ppermute(own, "zlo", pairs(2, 1))
+    far, mate = lax.optimization_barrier((far, mate))
     far_mate = lax.ppermute(far, "core", pairs(2, 1))
 
     tiles, listing, partial_degree, line_seeds = call(

time: 191 us -> 195 us (1.021)
  waiting for transfers between devices: 44.8 us -> 49.1 us
    ppermute x1, waiting for transfers between devices: 15.4 us -> 18.3 us  [local(): far = lax.ppermute(own, 'zlo', pairs(2, 1))]
  transfers between devices with their start and end apart: 12 -> 12, of which waited for: 7 -> 8; matrix products, arithmetic and copies ran while one was open for 0% -> 0% of each run, Pallas kernels for 0% -> 0%
where the time goes in v10:
time: 195 us; the launch traced here: 194 us
  blocking collectives  103 us (53%)
  waiting for transfers between devices  49.1 us (25%)
  starting transfers between devices  24.6 us (13%)
  Pallas kernels  15.8 us (8%)
    all_to_all x6, blocking collectives, exchange(): return lax.all_to_all(blocks, axes, 0, 0)  81.6 us
    ppermute x6, waiting for transfers between devices, local(): others.append(lax.ppermute(bits, axis, pairs(4, step)))  26.1 us
    all_gather x1, blocking collectives, local(): lax.all_gather(block, 'zhi')  21.3 us
    ppermute x1, waiting for transfers between devices, local(): far = lax.ppermute(own, 'zlo', pairs(2, 1))  18.3 us
    ppermute x6, starting transfers between devices, local(): others.append(lax.ppermute(bits, axis, pairs(4, step)))  15.6 us
    all_to_all x1, starting transfers between devices, exchange(): return lax.all_to_all(blocks, axes, 0, 0)  7.18 us
    pallas_call x1, Pallas kernels, local(): call(build_kernel, (array(BLOCKS, ROWS, ROWS, dtype=jnp.bfloat16), array(...  6.68 us
  transfers between devices with their start and end apart: 12, of which 8 were waited for; matrix products, arithmetic and copies ran while one was open for 0% of the time, Pallas kernels for 0%

profile of v10, /device:TPU:32, one launch (start us, length us, event | category | flops | bytes accessed | tf_op | source)
XLA Modules:
  0.0 194.3 jit_solution(18008593020245538467)
XLA Ops:
  0.0 3.5 %shard_map.37 = (bf16[768,128]{1,0:T(8,128)(2,1)}, bf16[16,768,128]{2,1,0:T(8,128)(2,1)}, bf16[8,128]{1,0:T(8,128)(2,1)}) custom-call(bf16[128,768]{1,0:T(8,128)(2,1)} %emb_hbm.1, s32[2,32]{1,0:T(2,128)} %bitcast.19), custom_call_target="tpu_custom_call" | custom-call | tf_op jit(solution)/shard_map/pallas_call | solution.py:265
  3.5 0.0 copy-start.1
  3.5 0.0 copy-start
  3.5 0.0 copy-start.2
  3.5 7.2 %all-to-all-start = ((bf16[16,768,128]{2,1,0:T(8,128)(2,1)}), bf16[16,768,128]{2,1,0:T(8,128)(2,1)S(1)}, u32[]{:S(2)}, u32[]{:S(2)}) async-start(bf16[16,768,128]{2,1,0:T(8,128)(2,1)} %get-tuple-element.26), calls=%async_computation | async-start | bytes 6291456 | tf_op jit(solution)/shard_map/all_to_all | solution.py:253
  10.7 0.0 copy-done.1
  10.7 3.2 %collective-permute-start.5 = (bf16[8,128]{1,0:T(8,128)(2,1)S(1)}, bf16[8,128]{1,0:T(8,128)(2,1)S(1)}, u32[]{:S(2)}, u32[]{:S(2)}) collective-permute-start(bf16[8,128]{1,0:T(8,128)(2,1)S(1)} %copy-done.1), channel_id=1, source_target_pairs={{0,3},{1,2},{2,1},{3,0},{4,7},{5,6},{6,5},{7,4},{8,11},{9,10},{10,... | collective-permute-start | bytes 6152 | tf_op jit(solution)/shard_map/ppermute | solution.py:287
  14.0 0.9 collective-permute-start.4
  14.8 0.1 collective-permute-start.3
  14.9 3.1 %collective-permute-start.2 = (bf16[8,128]{1,0:T(8,128)(2,1)S(1)}, bf16[8,128]{1,0:T(8,128)(2,1)S(1)}, u32[]{:S(2)}, u32[]{:S(2)}) collective-permute-start(bf16[8,128]{1,0:T(8,128)(2,1)S(1)} %copy-done.1), channel_id=1, source_target_pairs={{0,96},{32,64},{64,32},{96,0},{1,97},{33,65},{65,33},{97,1},{2,98}... | collective-permute-start | bytes 6152 | tf_op jit(solution)/shard_map/ppermute | solution.py:287
  18.1 0.9 collective-permute-start.1
  18.9 16.4 %collective-permute-done.5.refs_5_ = bf16[8,128]{1,0:T(8,128)(2,1)S(1)} collective-permute-done((bf16[8,128]{1,0:T(8,128)(2,1)S(1)}, bf16[8,128]{1,0:T(8,128)(2,1)S(1)}, u32[]{:S(2)}, u32[]{:S(2)}) %collective-permute-start.5) | collective-permute-done | bytes 2080 | tf_op jit(solution)/shard_map/ppermute | solution.py:287
  35.4 7.4 %collective-permute-start = (bf16[8,128]{1,0:T(8,128)(2,1)S(1)}, bf16[8,128]{1,0:T(8,128)(2,1)S(1)}, u32[]{:S(2)}, u32[]{:S(2)}) collective-permute-start(bf16[8,128]{1,0:T(8,128)(2,1)S(1)} %copy-done.1), channel_id=1, source_target_pairs={{0,32},{32,0},{64,96},{96,64},{1,33},{33,1},{65,97},{97,65},{2,34}... | collective-permute-start | bytes 6152 | tf_op jit(solution)/shard_map/ppermute | solution.py:287
  42.8 0.0 collective-permute-done.4.refs_4_
  42.8 0.0 collective-permute-done.3.refs_3_
  42.8 4.4 %collective-permute-done.2.refs_2_ = bf16[8,128]{1,0:T(8,128)(2,1)S(1)} collective-permute-done((bf16[8,128]{1,0:T(8,128)(2,1)S(1)}, bf16[8,128]{1,0:T(8,128)(2,1)S(1)}, u32[]{:S(2)}, u32[]{:S(2)}) %collective-permute-start.2) | collective-permute-done | bytes 2080 | tf_op jit(solution)/shard_map/ppermute | solution.py:287
  47.2 5.3 %collective-permute-done.1.refs_1_ = bf16[8,128]{1,0:T(8,128)(2,1)S(1)} collective-permute-done((bf16[8,128]{1,0:T(8,128)(2,1)S(1)}, bf16[8,128]{1,0:T(8,128)(2,1)S(1)}, u32[]{:S(2)}, u32[]{:S(2)}) %collective-permute-start.1) | collective-permute-done | bytes 2080 | tf_op jit(solution)/shard_map/ppermute | solution.py:287
  52.5 0.0 collective-permute-done.refs_0_
  52.5 0.0 copy-done
  52.5 0.0 copy-done.2
  52.5 21.3 %all-gather = bf16[3168,128]{1,0:T(8,128)(2,1)S(1)} all-gather(bf16[792,128]{1,0:T(8,128)(2,1)S(1)} %shard_map.38), channel_id=2, replica_groups=mesh['zlo'=2,'x'=4,'core'=2,'zhi'=4,'y'=4] {'zhi'}, dimensions={0}, use_global_device_ids=true | all-gather | bytes 1013760 | tf_op jit(solution)/shard_map/all_gather | solution.py:296
  73.8 0.0 copy-start.3
  73.8 0.0 collective-permute-start.7
  73.8 1.9 collective-permute-start.6
  75.7 0.5 collective-permute-done.7.mate_ref
  76.1 0.0 copy-start.4
  76.1 18.3 %collective-permute-done.6.far_ref = bf16[4,792,128]{2,1,0:T(8,128)(2,1)S(1)} collective-permute-done((bf16[4,792,128]{2,1,0:T(8,128)(2,1)S(1)}, bf16[4,792,128]{2,1,0:T(8,128)(2,1)S(1)}, u32[]{:S(2)}, u32[]{:S(2)}) %collective-permute-start.6) | collective-permute-done | bytes 811040 | tf_op jit(solution)/shard_map/ppermute | solution.py:298
  94.4 0.0 collective-permute-start.8
  94.4 0.0 copy-done.3
  94.4 0.0 copy-done.4
  94.4 0.9 copy-done.5
  95.3 1.5 collective-permute-done.8.far_mate_ref
  96.8 0.0 all-to-all-done.plane_ref
  96.8 6.7 %shard_map.39 = (bf16[256,128,128]{2,1,0:T(8,128)(2,1)S(1)}, s32[8,256]{1,0:T(8,128)S(1)}, f32[16,128]{1,0:T(8,128)S(1)}, s32[16,128]{1,0:T(8,128)S(1)}) custom-call(bf16[16,768,128]{2,1,0:T(8,128)(2,1)S(1)} %all-to-all-done.plane_ref, bf16[4,792,128]{2,1,0:T(8,128)(2,1)} %bitcast.18, bf16[4,792,128]{2,1,0:T(8,128)(2,1)} %copy-done.4, ...), custom_call_target="tpu_custom_call" | custom-call | tf_op jit(solution)/shard_map/pallas_call | solution.py:302
  103.6 14.5 %all_to_all.35.parts_ref = f32[16,16,128]{2,1,0:T(8,128)S(1)} all-to-all(f32[16,16,128]{2,1,0:T(8,128)S(1)} %broadcast_in_dim.9), channel_id=1, replica_groups=mesh['zlo'=2,'x'=4,'core'=2,'zhi'=4,'y'=4] {'zlo','core','zhi'}, dimensions={0} | all-to-all | bytes 262144 | tf_op jit(solution)/shard_map/all_to_all | solution.py:253
  118.0 1.8 shard_map.40
  119.9 18.2 %all_to_all.36 = bf16[16,64,128]{2,1,0:T(8,128)(2,1)S(1)} all-to-all(bf16[16,64,128]{2,1,0:T(8,128)(2,1)S(1)} %get-tuple-element.36), channel_id=1, replica_groups=mesh['zlo'=2,'x'=4,'core'=2,'zhi'=4,'y'=4] {'x','y'}, dimensions={0} | all-to-all | bytes 524288 | tf_op jit(solution)/shard_map/all_to_all | solution.py:253
  138.2 11.2 %all_to_all.37.own_ref = bf16[8,64,128]{2,1,0:T(8,128)(2,1)S(1)} all-to-all(bf16[8,64,128]{2,1,0:T(8,128)(2,1)S(1)} %broadcast_in_dim.10), channel_id=1, replica_groups=mesh['zlo'=2,'x'=4,'core'=2,'zhi'=4,'y'=4] {'zlo','zhi'}, dimensions={0} | all-to-all | bytes 262144 | tf_op jit(solution)/shard_map/all_to_all | solution.py:253
  149.4 0.0 collective-permute-start.9
  149.4 1.3 collective-permute-done.9.mate_ref
  150.7 1.9 shard_map.41
  152.6 13.3 %all_to_all.38 = bf16[16,64,128]{2,1,0:T(8,128)(2,1)S(1)} all-to-all(bf16[16,64,128]{2,1,0:T(8,128)(2,1)S(1)} %shard_map.41), channel_id=1, replica_groups=mesh['zlo'=2,'x'=4,'core'=2,'zhi'=4,'y'=4] {'x','y'}, dimensions={0} | all-to-all | bytes 524288 | tf_op jit(solution)/shard_map/all_to_all | solution.py:253
  166.0 11.1 %all_to_all.39.own_ref = bf16[8,64,128]{2,1,0:T(8,128)(2,1)S(1)} all-to-all(bf16[8,64,128]{2,1,0:T(8,128)(2,1)S(1)} %broadcast_in_dim.11), channel_id=1, replica_groups=mesh['zlo'=2,'x'=4,'core'=2,'zhi'=4,'y'=4] {'zlo','zhi'}, dimensions={0} | all-to-all | bytes 262144 | tf_op jit(solution)/shard_map/all_to_all | solution.py:253
  177.1 0.0 collective-permute-start.10
  177.1 1.3 collective-permute-done.10.mate_ref
  178.4 1.9 shard_map.42
  180.3 13.3 %all_to_all.40 = bf16[16,64,128]{2,1,0:T(8,128)(2,1)S(1)} all-to-all(bf16[16,64,128]{2,1,0:T(8,128)(2,1)S(1)} %shard_map.42), channel_id=1, replica_groups=mesh['zlo'=2,'x'=4,'core'=2,'zhi'=4,'y'=4] {'x','y'}, dimensions={0} | all-to-all | bytes 524288 | tf_op jit(solution)/shard_map/all_to_all | solution.py:253
  193.7 0.6 fusion
  (13 shorter events, 0.2 us)
Async XLA Ops:
  3.5 7.2 %copy-start.1 = (bf16[8,128]{1,0:T(8,128)(2,1)S(1)}, bf16[8,128]{1,0:T(8,128)(2,1)}, u32[]{:S(2)}) copy-start(bf16[8,128]{1,0:T(8,128)(2,1)} %get-tuple-element.28.bits_ref) | copy-start | bytes 6148
  3.5 49.0 %copy-start = (bf16[768,128]{1,0:T(8,128)(2,1)S(1)}, bf16[768,128]{1,0:T(8,128)(2,1)}, u32[]{:S(2)}) copy-start(bf16[768,128]{1,0:T(8,128)(2,1)} %get-tuple-element.27.folded_ref) | copy-start | bytes 589828
  3.5 48.9 %copy-start.2 = (s32[128]{0:T(128)S(1)}, s32[128]{0:T(128)}, u32[]{:S(2)}) copy-start(s32[128]{0:T(128)} %param.5) | copy-start | bytes 1540
  3.5 93.3 %all-to-all-start = ((bf16[16,768,128]{2,1,0:T(8,128)(2,1)}), bf16[16,768,128]{2,1,0:T(8,128)(2,1)S(1)}, u32[]{:S(2)}, u32[]{:S(2)}) async-start(bf16[16,768,128]{2,1,0:T(8,128)(2,1)} %get-tuple-element.26), calls=%async_computation | async-start | bytes 6291456 | tf_op jit(solution)/shard_map/all_to_all | solution.py:253
  10.7 24.6 %collective-permute-start.5 = (bf16[8,128]{1,0:T(8,128)(2,1)S(1)}, bf16[8,128]{1,0:T(8,128)(2,1)S(1)}, u32[]{:S(2)}, u32[]{:S(2)}) collective-permute-start(bf16[8,128]{1,0:T(8,128)(2,1)S(1)} %copy-done.1), channel_id=1, source_target_pairs={{0,3},{1,2},{2,1},{3,0},{4,7},{5,6},{6,5},{7,4},{8,11},{9,10},{10,... | collective-permute-start | bytes 6152 | tf_op jit(solution)/shard_map/ppermute | solution.py:287
  14.0 28.8 %collective-permute-start.4 = (bf16[8,128]{1,0:T(8,128)(2,1)S(1)}, bf16[8,128]{1,0:T(8,128)(2,1)S(1)}, u32[]{:S(2)}, u32[]{:S(2)}) collective-permute-start(bf16[8,128]{1,0:T(8,128)(2,1)S(1)} %copy-done.1), channel_id=1, source_target_pairs={{0,2},{1,3},{2,0},{3,1},{4,6},{5,7},{6,4},{7,5},{8,10},{9,11},{10,... | collective-permute-start | bytes 6152 | tf_op jit(solution)/shard_map/ppermute | solution.py:287
  14.8 28.0 %collective-permute-start.3 = (bf16[8,128]{1,0:T(8,128)(2,1)S(1)}, bf16[8,128]{1,0:T(8,128)(2,1)S(1)}, u32[]{:S(2)}, u32[]{:S(2)}) collective-permute-start(bf16[8,128]{1,0:T(8,128)(2,1)S(1)} %copy-done.1), channel_id=1, source_target_pairs={{0,1},{1,0},{2,3},{3,2},{4,5},{5,4},{6,7},{7,6},{8,9},{9,8},{10,11... | collective-permute-start | bytes 6152 | tf_op jit(solution)/shard_map/ppermute | solution.py:287
  14.9 32.2 %collective-permute-start.2 = (bf16[8,128]{1,0:T(8,128)(2,1)S(1)}, bf16[8,128]{1,0:T(8,128)(2,1)S(1)}, u32[]{:S(2)}, u32[]{:S(2)}) collective-permute-start(bf16[8,128]{1,0:T(8,128)(2,1)S(1)} %copy-done.1), channel_id=1, source_target_pairs={{0,96},{32,64},{64,32},{96,0},{1,97},{33,65},{65,33},{97,1},{2,98}... | collective-permute-start | bytes 6152 | tf_op jit(solution)/shard_map/ppermute | solution.py:287
  18.1 34.4 %collective-permute-start.1 = (bf16[8,128]{1,0:T(8,128)(2,1)S(1)}, bf16[8,128]{1,0:T(8,128)(2,1)S(1)}, u32[]{:S(2)}, u32[]{:S(2)}) collective-permute-start(bf16[8,128]{1,0:T(8,128)(2,1)S(1)} %copy-done.1), channel_id=1, source_target_pairs={{0,64},{32,96},{64,0},{96,32},{1,65},{33,97},{65,1},{97,33},{2,66}... | collective-permute-start | bytes 6152 | tf_op jit(solution)/shard_map/ppermute | solution.py:287
  35.4 17.1 %collective-permute-start = (bf16[8,128]{1,0:T(8,128)(2,1)S(1)}, bf16[8,128]{1,0:T(8,128)(2,1)S(1)}, u32[]{:S(2)}, u32[]{:S(2)}) collective-permute-start(bf16[8,128]{1,0:T(8,128)(2,1)S(1)} %copy-done.1), channel_id=1, source_target_pairs={{0,32},{32,0},{64,96},{96,64},{1,33},{33,1},{65,97},{97,65},{2,34}... | collective-permute-start | bytes 6152 | tf_op jit(solution)/shard_map/ppermute | solution.py:287
  73.8 20.6 %copy-start.3 = (bf16[3168,128]{1,0:T(8,128)(2,1)}, bf16[3168,128]{1,0:T(8,128)(2,1)S(1)}, u32[]{:S(2)}) copy-start(bf16[3168,128]{1,0:T(8,128)(2,1)S(1)} %all-gather) | copy-start | bytes 2433028
  73.8 2.3 %collective-permute-start.7 = (bf16[4,792,128]{2,1,0:T(8,128)(2,1)S(1)}, bf16[4,792,128]{2,1,0:T(8,128)(2,1)S(1)}, u32[]{:S(2)}, u32[]{:S(2)}) collective-permute-start(bf16[4,792,128]{2,1,0:T(8,128)(2,1)S(1)} %bitcast.16), channel_id=1, source_target_pairs={{0,16},{16,0},{1,17},{17,1},{2,18},{18,2},{3,19},{19,3},{4,20},{20... | collective-permute-start | bytes 2433032 | tf_op jit(solution)/shard_map/ppermute | solution.py:297
  73.8 20.6 %collective-permute-start.6 = (bf16[4,792,128]{2,1,0:T(8,128)(2,1)S(1)}, bf16[4,792,128]{2,1,0:T(8,128)(2,1)S(1)}, u32[]{:S(2)}, u32[]{:S(2)}) collective-permute-start(bf16[4,792,128]{2,1,0:T(8,128)(2,1)S(1)} %bitcast.17), channel_id=1, source_target_pairs={{0,128},{128,0},{1,129},{129,1},{2,130},{130,2},{3,131},{131,3},{4... | collective-permute-start | bytes 2433032 | tf_op jit(solution)/shard_map/ppermute | solution.py:298
  76.1 18.3 %copy-start.4 = (bf16[4,792,128]{2,1,0:T(8,128)(2,1)}, bf16[4,792,128]{2,1,0:T(8,128)(2,1)S(1)}, u32[]{:S(2)}) copy-start(bf16[4,792,128]{2,1,0:T(8,128)(2,1)S(1)} %collective-permute-done.7.mate_ref) | copy-start | bytes 2433028
  94.4 0.9 copy-start.5
  94.4 2.5 %collective-permute-start.8 = (bf16[4,792,128]{2,1,0:T(8,128)(2,1)S(1)}, bf16[4,792,128]{2,1,0:T(8,128)(2,1)}, u32[]{:S(2)}, u32[]{:S(2)}) collective-permute-start(bf16[4,792,128]{2,1,0:T(8,128)(2,1)S(1)} %collective-permute-done.6.far_ref), channel_id=1, source_target_pairs={{0,16},{16,0},{1,17},{17,1},{2,18},{18,2},{3,19},{19,3},{4,20},{20... | collective-permute-start | bytes 2433032 | tf_op jit(solution)/shard_map/ppermute | solution.py:300
  149.4 1.3 collective-permute-start.9
  177.1 1.3 collective-permute-start.10
